TPU v7x, 512 devices: a whole 4x4x16 slice. The times are simulated.
512 devices in a mesh: group: 32 (over x, y, core), tp: 16 (over z).
Axes of the slice: x: 4, y: 4, z: 16, core: 2. Of those that a mesh axis runs over, the one named last changes fastest.
Arguments:
- tokens: bfloat16 [24576, 8192], P('group', 'tp'), may hold values from -6 to 6
- w_query: bfloat16 [8192, 4096], P(None, 'tp'), may hold values from -0.0625 to 0.0625
- adapter_down: bfloat16 [384, 16, 8192], P('group', None, 'tp'), may hold values from -0.0625 to 0.0625
- adapter_up: bfloat16 [384, 16, 4096], P('group', None, 'tp'), may hold values from -1.5 to 1.5
- adapter_id: int32 [24576], P('group'), may hold values from 0 to 383, as said below
Outputs:
- query: bfloat16 [24576, 4096], P('group', 'tp')
Inputs may be any that keep to these rules, and one draw needn't show every extreme that they name: `adapter_id`: adapter a is owned by group a // 12. Among the 768 requests of one group (an aligned block), at most 48 use adapters of any one owner; in every draw one owner receives exactly 48 from every group.
All inputs are finite; a program needn't handle non-finite values.
Results may differ from a plain program's by a relative error of at most 0.014.
Values may be sent and summed in bfloat16 or wider, within the bound.
No kernel may reach another device: no remote copies, remote signals or barrier semaphores. Data moves between devices by JAX's collectives and lax.ppermute only.
A program may use at most 128 MiB of HBM per device.

v0:
```python
import jax
import jax.numpy as jnp
from jax import lax
from jax.sharding import PartitionSpec as P

adapter_scale_factor = 2.0


def on_device(tokens, w_query, adapter_down, adapter_up, adapter_id):
    pool_down, pool_up = (
        lax.all_gather(adapter_down, "group", axis=0, tiled=True),
        lax.all_gather(adapter_up, "group", axis=0, tiled=True),
    )
    picked_down = jnp.take(pool_down, adapter_id, axis=0)
    partial_value = jnp.einsum(
        "nd,nrd->nr", tokens, picked_down, preferred_element_type=jnp.float32
    )
    total_output = lax.psum(partial_value, "tp")
    scaled_delta = (adapter_scale_factor * total_output).astype(jnp.bfloat16)
    picked_up = jnp.take(pool_up, adapter_id, axis=0)
    delta_rows = jnp.einsum(
        "nr,nrh->nh", scaled_delta, picked_up, preferred_element_type=jnp.float32
    ).astype(jnp.bfloat16)
    base = jnp.dot(
        lax.all_gather(tokens, "tp", axis=1, tiled=True),
        w_query,
        preferred_element_type=jnp.float32,
    )
    return (base + delta_rows.astype(jnp.float32)).astype(jnp.bfloat16)


def solution(mesh):
    placed = (
        P("group", "tp"),
        P(None, "tp"),
        P("group", None, "tp"),
        P("group", None, "tp"),
        P("group"),
    )
    return jax.shard_map(
        on_device, mesh=mesh, in_specs=placed, out_specs=P("group", "tp"), check_vma=False
    )
```

profile of v0, /device:TPU:1, one launch (start us, length us, event | category | flops | bytes accessed | tf_op | source)
XLA Modules:
  0.0 317.1 jit_solution(11295828361454792933)
XLA Ops:
  6.5 0.0 all-gather.8.cloned.1.call-start
  6.5 0.7 all-gather.8.cloned.1.call-update
  7.3 0.0 all-gather.6.cloned.1.call-start
  7.3 0.7 all-gather.6.cloned.1.call-update
  8.0 0.0 all-gather.4.cloned.1.call-start
  8.1 0.7 all-gather.4.cloned.1.call-update
  8.7 0.7 compare_select_fusion
  9.4 0.7 compare_and_fusion
  10.1 66.6 %all-gather.8.cloned.1.call-done = bf16[384,16,256]{2,1,0:T(8,128)(2,1)} async-done(((bf16[12,16,256]{2,1,0:T(8,128)(2,1)}), bf16[384,16,256]{2,1,0:T(8,128)(2,1)}) %all-gather.8.cloned.1.call-update) | async-done | bytes 3145744 | tf_op jit(solution)/shard_map/all_gather | solution.py:12
  76.7 7.0 %gather_fusion.1 = bf16[768,16,256]{2,1,0:T(8,128)(2,1)} fusion(bf16[384,16,256]{2,1,0:T(8,128)(2,1)} %all-gather.8.cloned.1.call-done, s32[1024]{0:T(1024)S(1)} %pad_clamp_fusion), kind=kCustom, calls=%fused_computation.1 | custom fusion | bytes 12585984 | tf_op jit(solution)/shard_map/jit(_take)/gather | solution.py:20
  83.6 0.0 copy-start
  83.6 60.0 %all-gather.6.cloned.1.call-done = bf16[384,16,512]{2,1,0:T(8,128)(2,1)} async-done(((bf16[12,16,512]{2,1,0:T(8,128)(2,1)}), bf16[384,16,512]{2,1,0:T(8,128)(2,1)}) %all-gather.6.cloned.1.call-update) | async-done | bytes 6291472 | tf_op jit(solution)/shard_map/all_gather | solution.py:11
  143.7 22.4 %gather_fusion = bf16[768,16,512]{2,1,0:T(8,128)(2,1)} fusion(bf16[384,16,512]{2,1,0:T(8,128)(2,1)} %all-gather.6.cloned.1.call-done, s32[1024]{0:T(1024)S(1)} %pad_clamp_fusion), kind=kCustom, calls=%fused_computation | custom fusion | bytes 25168896 | tf_op jit(solution)/shard_map/jit(_take)/gather | solution.py:14
  166.1 0.0 copy-done
  166.1 9.9 %fusion = f32[768,1,16]{2,1,0:T(1,128)S(1)} fusion(bf16[768,16,512]{2,1,0:T(8,128)(2,1)} %gather_fusion, pred[768]{0:T(1024)(128)(4,1)S(1)} %compare_and_fusion, bf16[768,512,1]{1,0,2:T(8,128)(2,1)S(1)} %bitcast.11), kind=kOutput, calls=%fused_computation.2 | convolution fusion | flops 18874368 | bytes 13419264 | tf_op jit(solution)/shard_map/nd,nrd->nr/dot_general | solution.py:15
  176.1 61.4 %psum.7 = f32[768,16]{1,0:T(8,128)S(1)} all-reduce(f32[768,16]{1,0:T(8,128)S(1)} %bitcast.12), channel_id=1, replica_groups=mesh['group'=32,'tp'=16] {'tp'}, use_global_device_ids=true, to_apply=%region_0.1 | all-reduce | flops 12288 | bytes 98304 | tf_op jit(solution)/shard_map/psum | solution.py:18
  237.5 8.5 %fusion.3 = bf16[768,1,256]{2,1,0:T(2,128)(2,1)S(1)} fusion(bf16[768,16,256]{2,1,0:T(8,128)(2,1)} %gather_fusion.1, pred[768]{0:T(1024)(128)(4,1)S(1)} %compare_and_fusion, bf16[768,16,1]{1,0,2:T(8,128)(2,1)S(1)} %fusion.11), kind=kOutput, calls=%fused_computation.5 | convolution fusion | flops 9437184 | bytes 6710016 | tf_op jit(solution)/shard_map/nr,nrh->nh/dot_general | solution.py:21
  246.0 54.7 %all-gather.4.cloned.1.call-done = bf16[768,8192]{1,0:T(8,128)(2,1)} async-done(((bf16[768,512]{1,0:T(8,128)(2,1)}), bf16[768,8192]{1,0:T(8,128)(2,1)}) %all-gather.4.cloned.1.call-update) | async-done | bytes 12582928 | tf_op jit(solution)/shard_map/all_gather | solution.py:25
  300.7 9.9 %fusion.9 = bf16[768,256]{1,0:T(8,128)(2,1)} fusion(bf16[768,8192]{1,0:T(8,128)(2,1)} %all-gather.4.cloned.1.call-done, bf16[8192,256]{1,0:T(8,128)(2,1)} %param.6, bf16[768,1,256]{2,1,0:T(2,128)(2,1)S(1)} %fusion.3), kind=kOutput, calls=%fused_computation.12 | convolution fusion | flops 3221815296 | bytes 17563648 | tf_op jit(solution)/shard_map/dot_general | solution.py:24
  (2 shorter events, 0.0 us)
Async XLA Ops:
  6.5 70.2 %all-gather.8.cloned.1.call-start = ((), (), s32[]{:S(2)}) async-start(), calls=%async_computation.2 | async-start | bytes 3244032 | tf_op jit(solution)/shard_map/all_gather | solution.py:12
  7.3 136.4 %all-gather.6.cloned.1.call-start = ((), (), s32[]{:S(2)}) async-start(), calls=%async_computation.1 | async-start | bytes 6488064 | tf_op jit(solution)/shard_map/all_gather | solution.py:11
  8.0 292.7 %all-gather.4.cloned.1.call-start = ((), (), s32[]{:S(2)}) async-start(), calls=%async_computation | async-start | bytes 13369344 | tf_op jit(solution)/shard_map/all_gather | solution.py:25
  83.6 82.5 %copy-start = (bf16[768,512]{1,0:T(8,128)(2,1)S(1)}, bf16[768,512]{1,0:T(8,128)(2,1)}, u32[]{:S(2)}) copy-start(bf16[768,512]{1,0:T(8,128)(2,1)} %param.5) | copy-start | bytes 2359300
Sparse Core Ops, SparseCore 0:
  10.5 66.1 all-gather.7
  79.8 63.8 all-gather.5
  145.8 154.8 all-gather.3
where the time goes:
time: 317 us
  waiting for transfers between devices  183 us (58%)
  blocking collectives  61.4 us (19%)
  local copies, waits for them, and re-layouts  29.4 us (9%)
  matrix products  28.3 us (9%)
  between operations  13.2 us (4%)
    all_gather x1, waiting for transfers between devices, on_device(): lax.all_gather(adapter_up, 'group', axis=0, tiled=True)  66.6 us
    psum x1, blocking collectives, on_device(): total_output = lax.psum(partial_value, 'tp')  61.4 us
    all_gather x1, waiting for transfers between devices, on_device(): lax.all_gather(adapter_down, 'group', axis=0, tiled=True)  60 us
    all_gather x1, waiting for transfers between devices, on_device(): lax.all_gather(tokens, 'tp', axis=1, tiled=True)  54.7 us
    gather x1, local copies, waits for them, and re-layouts, on_device(): picked_down = jnp.take(pool_down, adapter_id, axis=0)  22.4 us
    dot_general x1, matrix products, on_device(): jnp.dot(lax.all_gather(tokens, 'tp', axis=1, tiled=True), w_query, prefer...  9.92 us
    dot_general x1, matrix products, on_device(): jnp.einsum('nd,nrd->nr', tokens, picked_down, preferred_element_type=jnp....  9.91 us
    dot_general x1, matrix products, on_device(): jnp.einsum('nr,nrh->nh', scaled_delta, picked_up, preferred_element_type=...  8.51 us
  transfers between devices with their start and end apart: 3, of which 3 were waited for; matrix products, arithmetic and copies ran while one was open for 16% of the time, Pallas kernels for 0%

commit v1 on v0

v1 whole, which is shorter than its diff:
```python
import jax
import jax.numpy as jnp
from jax import lax
from jax.sharding import PartitionSpec as P

adapter_scale_factor = 2.0
owner_slots = 48
F32, BF16 = jnp.float32, jnp.bfloat16


def slot_of_request(adapter_id, groups, per_group):
    n = adapter_id.shape[0]
    owner = adapter_id // per_group
    to_owner = owner[:, None] == lax.broadcasted_iota(jnp.int32, (n, groups), 1)
    before = lax.broadcasted_iota(jnp.int32, (n, n), 0) > lax.broadcasted_iota(jnp.int32, (n, n), 1)
    count = jnp.dot(before.astype(BF16), to_owner.astype(BF16), preferred_element_type=F32)
    rank = jnp.sum(jnp.where(to_owner, count, 0.0), axis=1).astype(jnp.int32)
    return owner * owner_slots + rank


def lora(tokens, adapter_down, adapter_up, adapter_id, groups, tp):
    n, d = tokens.shape
    per_group, rank, _ = adapter_down.shape
    ho = adapter_up.shape[2]
    slots = groups * owner_slots
    slot = slot_of_request(adapter_id, groups, per_group)
    place = (lax.broadcasted_iota(jnp.int32, (slots, n), 0) == slot[None, :]).astype(BF16)
    out_rows = jnp.dot(place, tokens, preferred_element_type=F32).astype(BF16)
    local = (adapter_id % per_group).astype(BF16)
    out_ids = jnp.dot(place, local[:, None], preferred_element_type=F32).astype(BF16)
    out_ids = out_ids.reshape(groups, 1, owner_slots)
    out_ids = jnp.pad(out_ids, ((0, 0), (0, 7), (0, d - owner_slots)))
    sent = jnp.concatenate([out_rows.reshape(groups, owner_slots, d), out_ids], axis=1)
    here = lax.all_to_all(sent, "group", 0, 0, tiled=True)
    rows = here[:, :owner_slots].reshape(slots, d)
    ids = here[:, owner_slots, :owner_slots].astype(jnp.int32).reshape(1, 1, slots)
    mine = lax.broadcasted_iota(jnp.int32, (per_group, 1, slots), 0) == ids
    part = lax.dot_general(
        adapter_down.reshape(per_group * rank, d), rows, (((1,), (1,)), ((), ())), preferred_element_type=F32
    ).reshape(per_group, rank, slots)
    part = jnp.sum(jnp.where(mine, part, 0.0), axis=0)
    share = rank // tp
    part = lax.all_to_all(part.reshape(tp, share, slots), "tp", 0, 0, tiled=True)
    scaled = (adapter_scale_factor * jnp.sum(part, axis=0)).astype(BF16)
    scaled = lax.all_to_all(
        jnp.broadcast_to(scaled[None], (tp, share, slots)), "tp", 0, 0, tiled=True
    ).reshape(1, rank, slots)
    spread = jnp.where(mine, scaled, jnp.zeros((), BF16)).reshape(per_group * rank, slots)
    delta = lax.dot_general(
        spread, adapter_up.reshape(per_group * rank, ho), (((0,), (0,)), ((), ())), preferred_element_type=F32
    ).astype(BF16)
    delta = lax.all_to_all(delta.reshape(groups, owner_slots, ho), "group", 0, 0, tiled=True)
    return lax.dot_general(
        place, delta.reshape(slots, ho), (((0,), (0,)), ((), ())), preferred_element_type=F32
    ).astype(BF16)


def solution(mesh):
    groups, tp = mesh.shape["group"], mesh.shape["tp"]

    def on_device(tokens, w_query, adapter_down, adapter_up, adapter_id):
        gathered = lax.all_gather(tokens, "tp", axis=1, tiled=True)
        delta = lora(tokens, adapter_down, adapter_up, adapter_id, groups, tp)
        base = jnp.dot(gathered, w_query, preferred_element_type=F32)
        return (base + delta.astype(F32)).astype(BF16)

    placed = (
        P("group", "tp"),
        P(None, "tp"),
        P("group", None, "tp"),
        P("group", None, "tp"),
        P("group"),
    )
    return jax.shard_map(
        on_device, mesh=mesh, in_specs=placed, out_specs=P("group", "tp"), check_vma=False
    )
```

time: 317 us -> 186 us (0.59)
  waiting for transfers between devices: 183 us -> 69.6 us
  local copies, waits for them, and re-layouts: 29.4 us -> 1.06 us
  blocking collectives: 61.4 us -> 78.7 us
  matrix products: 28.3 us -> 14.5 us
  starting transfers between devices: 0.08 us -> 5.74 us
    all_gather x3 -> x1, waiting for transfers between devices: 181 us -> 68.9 us  [on_device(): gathered = lax.all_gather(tokens, 'tp', axis=1, tiled=True)]
    all_to_all x0 -> x3, blocking collectives: none -> 78.7 us  [the longest x1 35.1 us: lora(): here = lax.all_to_all(sent, 'group', 0, 0, tiled=True)]
    psum x1 -> x0, blocking collectives: 61.4 us -> none  [on_device(): total_output = lax.psum(partial_value, 'tp')]
    gather x2 -> x0, local copies, waits for them, and re-layouts: 29.4 us -> none  [the longest x1 22.4 us: on_device(): picked_down = jnp.take(pool_down, adapter_id, axis=0)]
    dot_general x3 -> x7, matrix products: 28.3 us -> 14.5 us  [the longest x1 7.62 us: on_device(): base = jnp.dot(gathered, w_query, preferred_element_type=F32)]
    all_to_all x0 -> x1, starting transfers between devices: none -> 5.74 us  [lora(): lax.all_to_all(delta.reshape(groups, owner_slots, ho), 'group', 0, 0, til...]
  transfers between devices with their start and end apart: 3 -> 2, of which waited for: 3 -> 1; matrix products, arithmetic and copies ran while one was open for 16% -> 9% of each run, Pallas kernels for 0% -> 0%
where the time goes in v1:
time: 186 us
  blocking collectives  78.7 us (42%)
  waiting for transfers between devices  69.6 us (37%)
  matrix products  14.5 us (8%)
  between operations  13.5 us (7%)
  starting transfers between devices  5.74 us (3%)
  other arithmetic  2.74 us (1%)
    all_gather x1, waiting for transfers between devices, on_device(): gathered = lax.all_gather(tokens, 'tp', axis=1, tiled=True)  68.9 us
    all_to_all x1, blocking collectives, lora(): here = lax.all_to_all(sent, 'group', 0, 0, tiled=True)  35.1 us
    all_to_all x1, blocking collectives, lora(): lax.all_to_all(part.reshape(tp, share, slots), 'tp', 0, 0, tiled=True)  26 us
    all_to_all x1, blocking collectives, lora(): lax.all_to_all(jnp.broadcast_to(scaled[None], (tp, share, slots)), 'tp',...  17.6 us
    dot_general x1, matrix products, on_device(): base = jnp.dot(gathered, w_query, preferred_element_type=F32)  7.62 us
    all_to_all x1, starting transfers between devices, lora(): lax.all_to_all(delta.reshape(groups, owner_slots, ho), 'group', 0, 0, til...  5.74 us
  transfers between devices with their start and end apart: 2, of which 1 were waited for; matrix products, arithmetic and copies ran while one was open for 9% of the time, Pallas kernels for 0%

profile of v1, /device:TPU:1, one launch (start us, length us, event | category | flops | bytes accessed | tf_op | source)
XLA Modules:
  0.0 185.8 jit_solution(9114596857953348343)
XLA Ops:
  6.5 0.0 copy-start
  6.5 0.0 copy-start.1
  6.5 0.0 all-gather.2.cloned.1.call-start
  6.5 0.7 all-gather.2.cloned.1.call-update
  7.3 0.7 add_select_fusion.1
  8.0 0.4 fusion.16
  8.3 0.7 convert_add_fusion
  9.0 0.9 fusion.17
  9.9 0.1 reshape.86
  10.0 0.0 copy-done.1
  10.0 1.4 fusion.4
  11.4 0.1 fusion.10
  11.6 35.1 %all_to_all.20 = bf16[32,56,512]{2,1,0:T(8,128)(2,1)S(1)} all-to-all(bf16[32,56,512]{2,1,0:T(8,128)(2,1)S(1)} %fusion.10), channel_id=1, replica_groups=mesh['group'=32,'tp'=16] {'group'}, dimensions={0} | all-to-all | bytes 3670016 | tf_op jit(solution)/shard_map/all_to_all | solution.py:34
  46.7 0.1 fusion.23
  46.8 0.1 reshape.81
  46.8 0.2 slice.9
  47.0 0.0 copy-done
  47.0 0.7 fusion.28
  47.7 0.0 copy-start.2
  47.7 0.1 select_reduce_fusion
  47.9 0.1 reshape.78
  47.9 26.0 %all_to_all.21 = f32[16,1,1536]{2,1,0:T(1,128)S(1)} all-to-all(f32[16,1,1536]{2,1,0:T(1,128)S(1)} %reshape.78), channel_id=1, replica_groups=mesh['group'=32,'tp'=16] {'tp'}, dimensions={0} | all-to-all | bytes 196608 | tf_op jit(solution)/shard_map/all_to_all | solution.py:43
  74.0 0.1 reduce_sum.29
  74.0 0.1 broadcast_in_dim.48
  74.1 0.5 broadcast.31
  74.6 0.9 reduce.7
  75.6 17.6 %all_to_all.22 = bf16[16,2,768]{2,1,0:T(2,128)(2,1)S(1)} all-to-all(bf16[16,2,768]{2,1,0:T(2,128)(2,1)S(1)} %reshape.94), channel_id=1, replica_groups=mesh['group'=32,'tp'=16] {'tp'}, dimensions={0} | all-to-all | bytes 98304 | tf_op jit(solution)/shard_map/all_to_all | solution.py:45
  93.2 0.0 copy-done.2
  93.2 1.4 fusion.5
  94.5 5.7 %all-to-all-start.3 = ((bf16[32,48,256]{2,1,0:T(8,128)(2,1)}), bf16[32,48,256]{2,1,0:T(8,128)(2,1)S(1)}, u32[]{:S(2)}, u32[]{:S(2)}) async-start(bf16[32,48,256]{2,1,0:T(8,128)(2,1)} %bitcast.6), calls=%async_computation.3 | async-start | bytes 1572864 | tf_op jit(solution)/shard_map/all_to_all | solution.py:52
  100.3 68.9 %all-gather.2.cloned.1.call-done = bf16[768,8192]{1,0:T(8,128)(2,1)} async-done(((bf16[768,512]{1,0:T(8,128)(2,1)}), bf16[768,8192]{1,0:T(8,128)(2,1)}) %all-gather.2.cloned.1.call-update) | async-done | bytes 12582928 | tf_op jit(solution)/shard_map/all_gather | solution.py:62
  169.1 7.6 %fusion.27 = f32[768,256]{1,0:T(8,128)S(1)} fusion(bf16[768,8192]{1,0:T(8,128)(2,1)} %all-gather.2.cloned.1.call-done, bf16[8192,256]{1,0:T(8,128)(2,1)} %param.6), kind=kOutput, calls=%fused_computation.42 | convolution fusion | flops 3221225472 | bytes 17563648 | tf_op jit(solution)/shard_map/dot_general | solution.py:64
  176.8 0.0 all-to-all-done.3
  176.8 2.2 %fusion.14 = bf16[768,256]{1,0:T(8,128)(2,1)} fusion(f32[768,256]{1,0:T(8,128)S(1)} %fusion.27, bf16[1536,256]{1,0:T(8,128)(2,1)S(1)} %bitcast.27, s32[768]{0:T(1024)S(1)} %get-tuple-element.5), kind=kOutput, calls=%fused_computation.18 | convolution fusion | flops 605945856 | bytes 1969152 | tf_op jit(solution)/shard_map/dot_general | solution.py:53
  (6 shorter events, 0.1 us)
Async XLA Ops:
  6.5 40.5 %copy-start = (bf16[12,16,512]{2,1,0:T(8,128)(2,1)S(1)}, bf16[12,16,512]{2,1,0:T(8,128)(2,1)}, u32[]{:S(2)}) copy-start(bf16[12,16,512]{2,1,0:T(8,128)(2,1)} %param.7) | copy-start | bytes 589828
  6.5 3.5 %copy-start.1 = (bf16[768,512]{1,0:T(8,128)(2,1)S(1)}, bf16[768,512]{1,0:T(8,128)(2,1)}, u32[]{:S(2)}) copy-start(bf16[768,512]{1,0:T(8,128)(2,1)} %param.5) | copy-start | bytes 2359300
  6.5 162.6 %all-gather.2.cloned.1.call-start = ((), (), s32[]{:S(2)}) async-start(), calls=%async_computation.4 | async-start | bytes 13369344 | tf_op jit(solution)/shard_map/all_gather | solution.py:62
  47.7 45.5 %copy-start.2 = (bf16[12,16,256]{2,1,0:T(8,128)(2,1)S(1)}, bf16[12,16,256]{2,1,0:T(8,128)(2,1)}, u32[]{:S(2)}) copy-start(bf16[12,16,256]{2,1,0:T(8,128)(2,1)} %param.8) | copy-start | bytes 294916
  94.5 82.2 %all-to-all-start.3 = ((bf16[32,48,256]{2,1,0:T(8,128)(2,1)}), bf16[32,48,256]{2,1,0:T(8,128)(2,1)S(1)}, u32[]{:S(2)}, u32[]{:S(2)}) async-start(bf16[32,48,256]{2,1,0:T(8,128)(2,1)} %bitcast.6), calls=%async_computation.3 | async-start | bytes 1572864 | tf_op jit(solution)/shard_map/all_to_all | solution.py:52
Sparse Core Ops, SparseCore 0:
  9.4 159.6 all-gather.1

commit v2 on v1

--- a/solution.py
+++ b/solution.py
@@ -1,6 +1,8 @@
 import jax
 import jax.numpy as jnp
 from jax import lax
+from jax.experimental import pallas as pl
+from jax.experimental.pallas import tpu as pltpu
 from jax.sharding import PartitionSpec as P
 
 adapter_scale_factor = 2.0
@@ -18,20 +20,22 @@
     return owner * owner_slots + rank
 
 
-def lora(tokens, adapter_down, adapter_up, adapter_id, groups, tp):
+def outgoing(tokens, adapter_id, groups, per_group):
     n, d = tokens.shape
-    per_group, rank, _ = adapter_down.shape
-    ho = adapter_up.shape[2]
     slots = groups * owner_slots
     slot = slot_of_request(adapter_id, groups, per_group)
     place = (lax.broadcasted_iota(jnp.int32, (slots, n), 0) == slot[None, :]).astype(BF16)
-    out_rows = jnp.dot(place, tokens, preferred_element_type=F32).astype(BF16)
+    rows = jnp.dot(place, tokens, preferred_element_type=F32).astype(BF16)
     local = (adapter_id % per_group).astype(BF16)
-    out_ids = jnp.dot(place, local[:, None], preferred_element_type=F32).astype(BF16)
-    out_ids = out_ids.reshape(groups, 1, owner_slots)
-    out_ids = jnp.pad(out_ids, ((0, 0), (0, 7), (0, d - owner_slots)))
-    sent = jnp.concatenate([out_rows.reshape(groups, owner_slots, d), out_ids], axis=1)
-    here = lax.all_to_all(sent, "group", 0, 0, tiled=True)
+    ids = jnp.dot(place, local[:, None], preferred_element_type=F32).astype(BF16)
+    ids = jnp.pad(ids.reshape(groups, 1, owner_slots), ((0, 0), (0, 7), (0, d - owner_slots)))
+    return jnp.concatenate([rows.reshape(groups, owner_slots, d), ids], axis=1), place
+
+
+def lora(here, place, adapter_down, adapter_up, groups, tp):
+    per_group, rank, d = adapter_down.shape
+    ho = adapter_up.shape[2]
+    slots = groups * owner_slots
     rows = here[:, :owner_slots].reshape(slots, d)
     ids = here[:, owner_slots, :owner_slots].astype(jnp.int32).reshape(1, 1, slots)
     mine = lax.broadcasted_iota(jnp.int32, (per_group, 1, slots), 0) == ids
@@ -55,14 +59,60 @@
     ).astype(BF16)
 
 
+def partial_kernel(tok_a, tok_b, w_a, w_b, out):
+    depth = tok_a.shape[1]
+    cols = out.shape[2]
+    acc = jnp.dot(tok_a[...], w_a[...].reshape(depth, cols), preferred_element_type=F32)
+    acc += jnp.dot(tok_b[...], w_b[...].reshape(depth, cols), preferred_element_type=F32)
+    out[0] = acc.astype(out.dtype)
+
+
+def partials(tok_a, tok_b, w_a, w_b):
+    n, depth = tok_a.shape
+    chips, tp, r, cols = w_a.shape
+    tok_spec = pl.BlockSpec((n, depth), lambda q: (0, 0))
+    w_spec = pl.BlockSpec((chips, 1, r, cols), lambda q: (0, q, 0, 0))
+    return pl.pallas_call(
+        partial_kernel,
+        grid=(tp,),
+        in_specs=[tok_spec, tok_spec, w_spec, w_spec],
+        out_specs=pl.BlockSpec((1, n, cols), lambda q: (q, 0, 0)),
+        out_shape=jax.ShapeDtypeStruct((tp, n, cols), BF16),
+        compiler_params=pltpu.CompilerParams(dimension_semantics=("arbitrary",)),
+        name="partials",
+    )(tok_a, tok_b, w_a, w_b)
+
+
 def solution(mesh):
     groups, tp = mesh.shape["group"], mesh.shape["tp"]
+    chips = groups // 2
+    same_core = [[2 * chip + core for chip in range(chips)] for core in range(2)]
+    other_core = [(g, g ^ 1) for g in range(groups)]
 
     def on_device(tokens, w_query, adapter_down, adapter_up, adapter_id):
-        gathered = lax.all_gather(tokens, "tp", axis=1, tiled=True)
-        delta = lora(tokens, adapter_down, adapter_up, adapter_id, groups, tp)
-        base = jnp.dot(gathered, w_query, preferred_element_type=F32)
-        return (base + delta.astype(F32)).astype(BF16)
+        n, depth = tokens.shape
+        cols = w_query.shape[1]
+        r = depth // groups
+        me = lax.axis_index("group")
+        core, chip = me % 2, me // 2
+        w_mine = lax.dynamic_index_in_dim(
+            w_query.reshape(tp, groups, r, cols), core * chips + chip, 1, keepdims=False
+        )
+        w_mine = lax.all_to_all(w_mine, "tp", 0, 0, tiled=True)
+        w_half = lax.all_to_all(
+            jnp.broadcast_to(w_mine[None], (chips, tp, r, cols)), "group", 0, 0, axis_index_groups=same_core, tiled=True
+        )
+        sent, place = outgoing(tokens, adapter_id, groups, adapter_down.shape[0])
+        w_half, sent = lax.optimization_barrier((w_half, sent))
+        w_other = lax.ppermute(w_half, "group", other_core)
+        here = lax.all_to_all(sent, "group", 0, 0, tiled=True)
+        half = depth // 2
+        tok_half = lax.dynamic_slice_in_dim(tokens, core * half, half, 1)
+        tok_other = lax.dynamic_slice_in_dim(tokens, (1 - core) * half, half, 1)
+        part = partials(tok_half, tok_other, w_half, w_other)
+        base = lax.psum_scatter(part, "tp", scatter_dimension=0, tiled=False)
+        delta = lora(here, place, adapter_down, adapter_up, groups, tp)
+        return (base.astype(F32) + delta.astype(F32)).astype(BF16)
 
     placed = (
         P("group", "tp"),

time: 186 us -> 197 us (1.059)
  waiting for transfers between devices: 69.6 us -> 23.7 us
  blocking collectives: 78.7 us -> 113 us
  Pallas kernels: 0 us -> 13.6 us
  matrix products: 14.5 us -> 5.14 us
  starting transfers between devices: 5.74 us -> 14.9 us
  local copies, waits for them, and re-layouts: 1.06 us -> 8.41 us
    all_gather x1 -> x0, waiting for transfers between devices: 68.9 us -> none  [on_device(): gathered = lax.all_gather(tokens, 'tp', axis=1, tiled=True)]
    all_to_all x1 -> x3, blocking collectives: 35.1 us -> 77.4 us  [the longest x1 30.2 us: on_device(): here = lax.all_to_all(sent, 'group', 0, 0, tiled=True)]
    all_to_all x1, waiting for transfers between devices: 0.01 us -> 20.7 us  [on_device(): lax.all_to_all(jnp.broadcast_to(w_mine[None], (chips, tp, r, cols)), 'gro...]
    pallas_call x0 -> x1, Pallas kernels: none -> 13.6 us  [partials(): pl.pallas_call(partial_kernel, grid=(tp,), in_specs=[tok_spec, tok_spec,...]
    all_to_all x1, blocking collectives: 26 us -> 17.8 us  [lora(): lax.all_to_all(part.reshape(tp, share, slots), 'tp', 0, 0, tiled=True)]
    ppermute x0 -> x1, starting transfers between devices: none -> 7.93 us  [on_device(): w_other = lax.ppermute(w_half, 'group', other_core)]
    dot_general x3 -> x2, matrix products: 9.91 us -> 2.29 us  [the longest x1 1.39 us: outgoing(): rows = jnp.dot(place, tokens, preferred_element_type=F32).astype(BF16)]
    ppermute x0 -> x1, waiting for transfers between devices: none -> 2.94 us  [on_device(): w_other = lax.ppermute(w_half, 'group', other_core)]
  transfers between devices with their start and end apart: 2 -> 3, of which waited for: 1 -> 2; matrix products, arithmetic and copies ran while one was open for 9% -> 5% of each run, Pallas kernels for 0% -> 0%
where the time goes in v2:
time: 197 us; the launch traced here: 196 us
  blocking collectives  113 us (57%)
  waiting for transfers between devices  23.7 us (12%)
  starting transfers between devices  14.9 us (8%)
  Pallas kernels  13.6 us (7%)
  between operations  13.6 us (7%)
  local copies, waits for them, and re-layouts  8.41 us (4%)
  matrix products  5.14 us (3%)
  other arithmetic  4.42 us (2%)
    all_to_all x1, blocking collectives, on_device(): here = lax.all_to_all(sent, 'group', 0, 0, tiled=True)  30.2 us
    all_to_all x1, blocking collectives, on_device(): w_mine = lax.all_to_all(w_mine, 'tp', 0, 0, tiled=True)  27.5 us
    all_to_all x1, waiting for transfers between devices, on_device(): lax.all_to_all(jnp.broadcast_to(w_mine[None], (chips, tp, r, cols)), 'gro...  20.7 us
    all_to_all x1, blocking collectives, lora(): lax.all_to_all(delta.reshape(groups, owner_slots, ho), 'group', 0, 0, til...  19.6 us
    all_to_all x1, blocking collectives, lora(): lax.all_to_all(part.reshape(tp, share, slots), 'tp', 0, 0, tiled=True)  17.8 us
    all_to_all x1, blocking collectives, lora(): lax.all_to_all(jnp.broadcast_to(scaled[None], (tp, share, slots)), 'tp',...  17.4 us
    pallas_call x1, Pallas kernels, partials(): pl.pallas_call(partial_kernel, grid=(tp,), in_specs=[tok_spec, tok_spec,...  13.6 us
    ppermute x1, starting transfers between devices, on_device(): w_other = lax.ppermute(w_half, 'group', other_core)  7.93 us
  transfers between devices with their start and end apart: 3, of which 2 were waited for; matrix products, arithmetic and copies ran while one was open for 5% of the time, Pallas kernels for 0%

profile of v2, /device:TPU:1, one launch (start us, length us, event | category | flops | bytes accessed | tf_op | source)
XLA Modules:
  0.0 196.4 jit_solution(9812970617364653265)
XLA Ops:
  6.5 0.0 copy-start
  6.5 1.0 dynamic-slice_bitcast_fusion
  7.5 27.5 %all_to_all.30 = bf16[16,16,256]{2,1,0:T(8,128)(2,1)S(1)} all-to-all(bf16[16,16,256]{2,1,0:T(8,128)(2,1)S(1)} %dynamic-slice_bitcast_fusion), channel_id=1, replica_groups=mesh['group'=32,'tp'=16] {'tp'}, dimensions={0} | all-to-all | bytes 262144 | tf_op jit(solution)/shard_map/all_to_all | solution.py:101
  35.0 1.6 broadcast_in_dim.51
  36.6 0.0 copy-start.5
  36.6 6.9 %all-to-all-start.1 = ((bf16[16,16,16,256]{3,2,1,0:T(8,128)(2,1)}), bf16[16,16,16,256]{3,2,1,0:T(8,128)(2,1)S(1)}, u32[]{:S(2)}, u32[]{:S(2)}) async-start(bf16[16,16,16,256]{3,2,1,0:T(8,128)(2,1)} %broadcast_in_dim.51), calls=%async_computation.1 | async-start | bytes 4194304 | tf_op jit(solution)/shard_map/all_to_all | solution.py:102
  43.5 0.0 copy-start.4
  43.5 0.0 reduce-scatter.2.cloned.1.call-start
  43.6 0.0 copy-done.5
  43.6 0.3 fusion.14
  44.0 0.9 fusion.15
  44.9 0.1 reshape.94
  45.0 0.0 copy-done.4
  45.0 1.4 fusion.4
  46.4 1.4 fusion.10
  47.7 20.7 %all-to-all-done.1.w_a = bf16[16,16,16,256]{3,2,1,0:T(8,128)(2,1)S(1)} async-done(((bf16[16,16,16,256]{3,2,1,0:T(8,128)(2,1)}), bf16[16,16,16,256]{3,2,1,0:T(8,128)(2,1)S(1)}, u32[]{:S(2)}, u32[]{:S(2)}) %all-to-all-start.1) | async-done | bytes 2097184 | tf_op jit(solution)/shard_map/all_to_all | solution.py:102
  68.4 0.0 copy-start.1
  68.4 7.9 %collective-permute-start = (bf16[16,16,16,256]{3,2,1,0:T(8,128)(2,1)S(1)}, bf16[16,16,16,256]{3,2,1,0:T(8,128)(2,1)}, u32[]{:S(2)}, u32[]{:S(2)}) collective-permute-start(bf16[16,16,16,256]{3,2,1,0:T(8,128)(2,1)S(1)} %all-to-all-done.1.w_a), channel_id=1, source_target_pairs={{0,16},{16,0},{32,48},{48,32},{64,80},{80,64},{96,112},{112,96},{1... | collective-permute-start | bytes 6291464 | tf_op jit(solution)/shard_map/ppermute | solution.py:107
  76.4 0.9 constant_dynamic-slice_fusion
  77.3 2.9 %collective-permute-done.w_b = bf16[16,16,16,256]{3,2,1,0:T(8,128)(2,1)} collective-permute-done((bf16[16,16,16,256]{3,2,1,0:T(8,128)(2,1)S(1)}, bf16[16,16,16,256]{3,2,1,0:T(8,128)(2,1)}, u32[]{:S(2)}, u32[]{:S(2)}) %collective-permute-start) | collective-permute-done | bytes 2097184 | tf_op jit(solution)/shard_map/ppermute | solution.py:107
  80.3 0.0 copy-done.1
  80.3 13.6 %partials.1 = bf16[16,768,256]{2,1,0:T(8,128)(2,1)} custom-call(bf16[768,256]{1,0:T(8,128)(2,1)} %get-tuple-element.10.tok_a, bf16[768,256]{1,0:T(8,128)(2,1)} %get-tuple-element.9.tok_b, bf16[16,16,16,256]{3,2,1,0:T(8,128)(2,1)} %copy-done.1, bf16[16,16,16,256]{3,2,1,0:T(8,128)(2,1)} %collective-permute-done.w_b), custom_call_target="tpu_custom_call" | custom-call | tf_op jit(solution)/shard_map/partials/pallas_call | solution.py:75
  93.9 0.0 copy-start.2
  93.9 0.0 reduce-scatter.2.cloned.1.call-update
  93.9 1.5 copy-done.2
  95.4 30.2 %all_to_all.31 = bf16[32,56,512]{2,1,0:T(8,128)(2,1)S(1)} all-to-all(bf16[32,56,512]{2,1,0:T(8,128)(2,1)S(1)} %copy-done.2), channel_id=1, replica_groups=mesh['group'=32,'tp'=16] {'group'}, dimensions={0} | all-to-all | bytes 3670016 | tf_op jit(solution)/shard_map/all_to_all | solution.py:108
  125.6 0.0 copy-start.3
  125.6 1.2 copy-done.3
  126.9 0.1 fusion.22
  126.9 0.0 slice-start
  126.9 0.1 reshape.89
  127.0 0.0 copy-done
  127.0 1.3 slice-done
  128.4 0.7 fusion.26
  129.0 0.0 copy-start.6
  129.1 0.1 select_reduce_fusion
  129.2 0.1 reshape.85
  129.3 17.8 %all_to_all.32 = f32[16,1,1536]{2,1,0:T(1,128)S(1)} all-to-all(f32[16,1,1536]{2,1,0:T(1,128)S(1)} %reshape.85), channel_id=1, replica_groups=mesh['group'=32,'tp'=16] {'tp'}, dimensions={0} | all-to-all | bytes 196608 | tf_op jit(solution)/shard_map/all_to_all | solution.py:47
  147.1 0.1 reduce_sum.29
  147.2 0.1 broadcast_in_dim.55
  147.3 0.5 broadcast.40
  147.8 0.9 reduce.7
  148.7 17.4 %all_to_all.33 = bf16[16,2,768]{2,1,0:T(2,128)(2,1)S(1)} all-to-all(bf16[16,2,768]{2,1,0:T(2,128)(2,1)S(1)} %reshape.102), channel_id=1, replica_groups=mesh['group'=32,'tp'=16] {'tp'}, dimensions={0} | all-to-all | bytes 98304 | tf_op jit(solution)/shard_map/all_to_all | solution.py:49
  166.2 0.0 copy-done.6
  166.2 0.4 fusion.5
  166.7 19.6 %all_to_all.34 = bf16[32,48,256]{2,1,0:T(8,128)(2,1)S(1)} all-to-all(bf16[32,48,256]{2,1,0:T(8,128)(2,1)S(1)} %bitcast.31), channel_id=1, replica_groups=mesh['group'=32,'tp'=16] {'group'}, dimensions={0} | all-to-all | bytes 1572864 | tf_op jit(solution)/shard_map/all_to_all | solution.py:56
  186.3 1.4 fusion.12
  187.7 0.0 reduce-scatter.2.cloned.1.call-done
  187.8 1.8 fusion.16
  (8 shorter events, 0.1 us)
Async XLA Ops:
  6.5 120.5 %copy-start = (bf16[12,16,512]{2,1,0:T(8,128)(2,1)S(1)}, bf16[12,16,512]{2,1,0:T(8,128)(2,1)}, u32[]{:S(2)}) copy-start(bf16[12,16,512]{2,1,0:T(8,128)(2,1)} %param.7) | copy-start | bytes 589828
  36.6 7.0 %copy-start.5 = (s32[768]{0:T(1024)S(1)}, s32[768]{0:T(1024)}, u32[]{:S(2)}) copy-start(s32[768]{0:T(1024)} %param.9) | copy-start | bytes 9220
  36.6 31.8 %all-to-all-start.1 = ((bf16[16,16,16,256]{3,2,1,0:T(8,128)(2,1)}), bf16[16,16,16,256]{3,2,1,0:T(8,128)(2,1)S(1)}, u32[]{:S(2)}, u32[]{:S(2)}) async-start(bf16[16,16,16,256]{3,2,1,0:T(8,128)(2,1)} %broadcast_in_dim.51), calls=%async_computation.1 | async-start | bytes 4194304 | tf_op jit(solution)/shard_map/all_to_all | solution.py:102
  43.5 1.5 copy-start.4
  43.5 144.2 %reduce-scatter.2.cloned.1.call-start = ((), (), s32[]{:S(2)}) async-start(), calls=%async_computation.7 | async-start | bytes 6684672 | tf_op jit(solution)/shard_map/reduce_scatter | solution.py:113
  68.4 11.8 %copy-start.1 = (bf16[16,16,16,256]{3,2,1,0:T(8,128)(2,1)}, bf16[16,16,16,256]{3,2,1,0:T(8,128)(2,1)S(1)}, u32[]{:S(2)}) copy-start(bf16[16,16,16,256]{3,2,1,0:T(8,128)(2,1)S(1)} %all-to-all-done.1.w_a) | copy-start | bytes 6291460
  68.4 11.8 %collective-permute-start = (bf16[16,16,16,256]{3,2,1,0:T(8,128)(2,1)S(1)}, bf16[16,16,16,256]{3,2,1,0:T(8,128)(2,1)}, u32[]{:S(2)}, u32[]{:S(2)}) collective-permute-start(bf16[16,16,16,256]{3,2,1,0:T(8,128)(2,1)S(1)} %all-to-all-done.1.w_a), channel_id=1, source_target_pairs={{0,16},{16,0},{32,48},{48,32},{64,80},{80,64},{96,112},{112,96},{1... | collective-permute-start | bytes 6291464 | tf_op jit(solution)/shard_map/ppermute | solution.py:107
  93.9 1.5 copy-start.2
  125.6 1.2 copy-start.3
  126.9 1.4 slice-start
  129.0 37.2 %copy-start.6 = (bf16[12,16,256]{2,1,0:T(8,128)(2,1)S(1)}, bf16[12,16,256]{2,1,0:T(8,128)(2,1)}, u32[]{:S(2)}) copy-start(bf16[12,16,256]{2,1,0:T(8,128)(2,1)} %param.8) | copy-start | bytes 294916
Sparse Core Ops, SparseCore 0:
  94.0 80.3 reduce-scatter.1

commit v3 on v1

--- a/solution.py
+++ b/solution.py
@@ -18,20 +18,24 @@
     return owner * owner_slots + rank
 
 
-def lora(tokens, adapter_down, adapter_up, adapter_id, groups, tp):
+def outgoing(tokens, adapter_id, groups, per_group):
     n, d = tokens.shape
-    per_group, rank, _ = adapter_down.shape
-    ho = adapter_up.shape[2]
     slots = groups * owner_slots
     slot = slot_of_request(adapter_id, groups, per_group)
     place = (lax.broadcasted_iota(jnp.int32, (slots, n), 0) == slot[None, :]).astype(BF16)
-    out_rows = jnp.dot(place, tokens, preferred_element_type=F32).astype(BF16)
+    rows = jnp.dot(place, tokens, preferred_element_type=F32).astype(BF16)
     local = (adapter_id % per_group).astype(BF16)
-    out_ids = jnp.dot(place, local[:, None], preferred_element_type=F32).astype(BF16)
-    out_ids = out_ids.reshape(groups, 1, owner_slots)
-    out_ids = jnp.pad(out_ids, ((0, 0), (0, 7), (0, d - owner_slots)))
-    sent = jnp.concatenate([out_rows.reshape(groups, owner_slots, d), out_ids], axis=1)
-    here = lax.all_to_all(sent, "group", 0, 0, tiled=True)
+    ids = jnp.dot(place, local[:, None], preferred_element_type=F32).astype(BF16)
+    ids = jnp.pad(ids.reshape(groups, 1, owner_slots), ((0, 0), (0, 7), (0, d - owner_slots)))
+    return jnp.concatenate([rows.reshape(groups, owner_slots, d), ids], axis=1), place
+
+
+def lora(sent, place, at, adapter_down, adapter_up, groups, tp):
+    per_group, rank, d = adapter_down.shape
+    ho = adapter_up.shape[2]
+    slots = groups * owner_slots
+    here = lax.all_to_all(at(0, sent), "group", 0, 0, tiled=True)
+    here = at(2, here)
     rows = here[:, :owner_slots].reshape(slots, d)
     ids = here[:, owner_slots, :owner_slots].astype(jnp.int32).reshape(1, 1, slots)
     mine = lax.broadcasted_iota(jnp.int32, (per_group, 1, slots), 0) == ids
@@ -41,10 +45,12 @@
     part = jnp.sum(jnp.where(mine, part, 0.0), axis=0)
     share = rank // tp
     part = lax.all_to_all(part.reshape(tp, share, slots), "tp", 0, 0, tiled=True)
+    part = at(4, part)
     scaled = (adapter_scale_factor * jnp.sum(part, axis=0)).astype(BF16)
     scaled = lax.all_to_all(
         jnp.broadcast_to(scaled[None], (tp, share, slots)), "tp", 0, 0, tiled=True
-    ).reshape(1, rank, slots)
+    )
+    scaled = at(6, scaled).reshape(1, rank, slots)
     spread = jnp.where(mine, scaled, jnp.zeros((), BF16)).reshape(per_group * rank, slots)
     delta = lax.dot_general(
         spread, adapter_up.reshape(per_group * rank, ho), (((0,), (0,)), ((), ())), preferred_element_type=F32
@@ -57,11 +63,42 @@
 
 def solution(mesh):
     groups, tp = mesh.shape["group"], mesh.shape["tp"]
+    right = [(z, (z + 1) % tp) for z in range(tp)]
+    left = [(z, (z - 1) % tp) for z in range(tp)]
 
     def on_device(tokens, w_query, adapter_down, adapter_up, adapter_id):
-        gathered = lax.all_gather(tokens, "tp", axis=1, tiled=True)
-        delta = lora(tokens, adapter_down, adapter_up, adapter_id, groups, tp)
-        base = jnp.dot(gathered, w_query, preferred_element_type=F32)
+        n, depth = tokens.shape
+        cols = w_query.shape[1]
+        z = lax.axis_index("tp")
+        w = w_query.reshape(tp, depth, cols)
+
+        def times_w(rows, owner):
+            block = lax.dynamic_index_in_dim(w, owner % tp, 0, keepdims=False)
+            return jnp.dot(rows, block, preferred_element_type=F32)
+
+        from_left = [tokens]
+        from_right = [tokens]
+        for t in range(1, tp // 2):
+            from_left.append(lax.ppermute(from_left[-1], "tp", right))
+            from_right.append(lax.ppermute(from_right[-1], "tp", left))
+        far = jnp.concatenate(
+            [
+                lax.ppermute(from_left[-1][: n // 2], "tp", right),
+                lax.ppermute(from_right[-1][n // 2 :], "tp", left),
+            ],
+            axis=0,
+        )
+        base = times_w(tokens, z)
+        for t in range(1, tp // 2):
+            base += times_w(from_left[t], z + tp - t)
+            base += times_w(from_right[t], z + t)
+        base += times_w(far, z + tp // 2)
+
+        def at(t, x):
+            return lax.optimization_barrier((x, from_left[t]))[0]
+
+        sent, place = outgoing(tokens, adapter_id, groups, adapter_down.shape[0])
+        delta = lora(sent, place, at, adapter_down, adapter_up, groups, tp)
         return (base + delta.astype(F32)).astype(BF16)
 
     placed = (

time: 186 us -> 196 us (1.054); the launches traced: 186 us -> 192 us
  starting transfers between devices: 5.74 us -> 101 us
  blocking collectives: 78.7 us -> 0 us
  waiting for transfers between devices: 69.6 us -> 47.4 us
  matrix products: 14.5 us -> 33.5 us
  between operations: 13.5 us -> 0.77 us
  local copies, waits for them, and re-layouts: 1.06 us -> 5.84 us
    all_to_all x3 -> x0, blocking collectives: 78.7 us -> none  [the longest x1 35.1 us: lora(): here = lax.all_to_all(sent, 'group', 0, 0, tiled=True)]
    all_gather x1 -> x0, waiting for transfers between devices: 68.9 us -> none  [on_device(): gathered = lax.all_gather(tokens, 'tp', axis=1, tiled=True)]
    ppermute x0 -> x16, starting transfers between devices: none -> 62 us  [the longest x7 37.6 us: on_device(): from_right.append(lax.ppermute(from_right[-1], 'tp', left))]
    ppermute x0 -> x16, waiting for transfers between devices: none -> 45.4 us  [the longest x7 22.1 us: on_device(): from_left.append(lax.ppermute(from_left[-1], 'tp', right))]
    all_to_all x0 -> x3, starting transfers between devices: none -> 23.4 us  [the longest x1 8.04 us: lora(): here = lax.all_to_all(at(0, sent), 'group', 0, 0, tiled=True)]
    dot_general x3 -> x18, matrix products: 9.91 us -> 28.8 us  [the longest x16 25.4 us: times_w(): return jnp.dot(rows, block, preferred_element_type=F32)]
    all_to_all x1, starting transfers between devices: 5.74 us -> 15.5 us  [lora(): lax.all_to_all(delta.reshape(groups, owner_slots, ho), 'group', 0, 0, til...]
    unnamed x9 -> x16, local copies, waits for them, and re-layouts: 0.08 us -> 2.46 us
  transfers between devices with their start and end apart: 2 -> 20, of which waited for: 1 -> 9; matrix products, arithmetic and copies ran while one was open for 9% -> 20% of each run, Pallas kernels for 0% -> 0%
where the time goes in v3:
time: 196 us; the launch traced here: 192 us
  starting transfers between devices  101 us (52%)
  waiting for transfers between devices  47.4 us (24%)
  matrix products  33.5 us (17%)
  local copies, waits for them, and re-layouts  5.84 us (3%)
  other arithmetic  4.03 us (2%)
    ppermute x7, starting transfers between devices, on_device(): from_right.append(lax.ppermute(from_right[-1], 'tp', left))  37.6 us
    dot_general x16, matrix products, times_w(): return jnp.dot(rows, block, preferred_element_type=F32)  25.4 us
    ppermute x7, waiting for transfers between devices, on_device(): from_left.append(lax.ppermute(from_left[-1], 'tp', right))  22.1 us
    ppermute x7, waiting for transfers between devices, on_device(): from_right.append(lax.ppermute(from_right[-1], 'tp', left))  19.8 us
    ppermute x7, starting transfers between devices, on_device(): from_left.append(lax.ppermute(from_left[-1], 'tp', right))  17.6 us
    all_to_all x1, starting transfers between devices, lora(): lax.all_to_all(delta.reshape(groups, owner_slots, ho), 'group', 0, 0, til...  15.5 us
    all_to_all x1, starting transfers between devices, lora(): here = lax.all_to_all(at(0, sent), 'group', 0, 0, tiled=True)  8.04 us
    all_to_all x1, starting transfers between devices, lora(): lax.all_to_all(jnp.broadcast_to(scaled[None], (tp, share, slots)), 'tp',...  7.68 us
  transfers between devices with their start and end apart: 20, of which 9 were waited for; matrix products, arithmetic and copies ran while one was open for 20% of the time, Pallas kernels for 0%

profile of v3, /device:TPU:1, one launch (start us, length us, event | category | flops | bytes accessed | tf_op | source)
XLA Modules:
  0.0 192.4 jit_solution(5390462455739411403)
XLA Ops:
  0.0 4.5 %collective-permute-start = (bf16[768,512]{1,0:T(8,128)(2,1)}, bf16[768,512]{1,0:T(8,128)(2,1)}, u32[]{:S(2)}, u32[]{:S(2)}) collective-permute-start(bf16[768,512]{1,0:T(8,128)(2,1)} %param.5), channel_id=1, source_target_pairs={{0,1},{1,2},{2,3},{3,4},{4,5},{5,6},{6,7},{7,8},{8,9},{9,10},{10,1... | collective-permute-start | bytes 2359304 | tf_op jit(solution)/shard_map/ppermute | solution.py:82
  4.5 9.5 %collective-permute-start.1 = (bf16[768,512]{1,0:T(8,128)(2,1)}, bf16[768,512]{1,0:T(8,128)(2,1)}, u32[]{:S(2)}, u32[]{:S(2)}) collective-permute-start(bf16[768,512]{1,0:T(8,128)(2,1)} %param.5), channel_id=1, source_target_pairs={{0,15},{1,0},{2,1},{3,2},{4,3},{5,4},{6,5},{7,6},{8,7},{9,8},{10,9... | collective-permute-start | bytes 2359304 | tf_op jit(solution)/shard_map/ppermute | solution.py:83
  14.0 0.7 add_select_fusion.1
  14.7 0.4 fusion.24
  15.1 0.7 convert_add_fusion
  15.8 0.9 fusion.25
  16.8 2.5 %fusion.4 = bf16[1536,512]{1,0:T(8,128)(2,1)S(1)} fusion(bf16[768,512]{1,0:T(8,128)(2,1)} %param.5, s32[768]{0:T(1024)S(1)} %get-tuple-element.13), kind=kOutput, calls=%fused_computation.6 | convolution fusion | flops 1209925632 | bytes 2362368 | tf_op jit(solution)/shard_map/dot_general | solution.py:26
  19.3 1.4 fusion.10
  20.8 8.0 %all-to-all-start = ((bf16[32,56,512]{2,1,0:T(8,128)(2,1)}), bf16[32,56,512]{2,1,0:T(8,128)(2,1)S(1)}, u32[]{:S(2)}, u32[]{:S(2)}) async-start(bf16[32,56,512]{2,1,0:T(8,128)(2,1)} %fusion.10), calls=%async_computation | async-start | bytes 3670016 | tf_op jit(solution)/shard_map/all_to_all | solution.py:37
  28.8 1.7 collective-permute-done.1
  30.5 5.3 %collective-permute-start.3 = (bf16[768,512]{1,0:T(8,128)(2,1)}, bf16[768,512]{1,0:T(8,128)(2,1)}, u32[]{:S(2)}, u32[]{:S(2)}) collective-permute-start(bf16[768,512]{1,0:T(8,128)(2,1)} %collective-permute-done.1), channel_id=1, source_target_pairs={{0,15},{1,0},{2,1},{3,2},{4,3},{5,4},{6,5},{7,6},{8,7},{9,8},{10,9... | collective-permute-start | bytes 2359304 | tf_op jit(solution)/shard_map/ppermute | solution.py:83
  35.8 1.9 collective-permute-start.2
  38.0 1.4 fusion.55
  39.4 1.6 convolution_add_fusion.7
  41.0 10.4 %collective-permute-done.3 = bf16[768,512]{1,0:T(8,128)(2,1)} collective-permute-done((bf16[768,512]{1,0:T(8,128)(2,1)}, bf16[768,512]{1,0:T(8,128)(2,1)}, u32[]{:S(2)}, u32[]{:S(2)}) %collective-permute-start.3) | collective-permute-done | bytes 786464 | tf_op jit(solution)/shard_map/ppermute | solution.py:83
  51.4 5.3 %collective-permute-start.5 = (bf16[768,512]{1,0:T(8,128)(2,1)}, bf16[768,512]{1,0:T(8,128)(2,1)}, u32[]{:S(2)}, u32[]{:S(2)}) collective-permute-start(bf16[768,512]{1,0:T(8,128)(2,1)} %collective-permute-done.3), channel_id=1, source_target_pairs={{0,15},{1,0},{2,1},{3,2},{4,3},{5,4},{6,5},{7,6},{8,7},{9,8},{10,9... | collective-permute-start | bytes 2359304 | tf_op jit(solution)/shard_map/ppermute | solution.py:83
  56.7 1.9 collective-permute-start.4
  58.7 1.6 convolution_add_fusion.6
  60.3 1.6 fusion.50
  62.0 1.6 fusion.19
  63.8 7.6 %collective-permute-done.5 = bf16[768,512]{1,0:T(8,128)(2,1)} collective-permute-done((bf16[768,512]{1,0:T(8,128)(2,1)}, bf16[768,512]{1,0:T(8,128)(2,1)}, u32[]{:S(2)}, u32[]{:S(2)}) %collective-permute-start.5) | collective-permute-done | bytes 786464 | tf_op jit(solution)/shard_map/ppermute | solution.py:83
  71.4 5.3 %collective-permute-start.7 = (bf16[768,512]{1,0:T(8,128)(2,1)}, bf16[768,512]{1,0:T(8,128)(2,1)}, u32[]{:S(2)}, u32[]{:S(2)}) collective-permute-start(bf16[768,512]{1,0:T(8,128)(2,1)} %collective-permute-done.5), channel_id=1, source_target_pairs={{0,15},{1,0},{2,1},{3,2},{4,3},{5,4},{6,5},{7,6},{8,7},{9,8},{10,9... | collective-permute-start | bytes 2359304 | tf_op jit(solution)/shard_map/ppermute | solution.py:83
  76.7 1.9 collective-permute-start.6
  78.7 0.2 slice.15
  78.9 0.7 fusion.94
  79.5 0.1 select_reduce_fusion
  79.7 0.7 reshape.82
  80.4 7.7 %all-to-all-start.1 = ((f32[16,1,1536]{2,1,0:T(1,128)}), f32[16,1,1536]{2,1,0:T(1,128)S(1)}, u32[]{:S(2)}, u32[]{:S(2)}) async-start(f32[16,1,1536]{2,1,0:T(1,128)} %reshape.82), calls=%async_computation.1 | async-start | bytes 196608 | tf_op jit(solution)/shard_map/all_to_all | solution.py:47
  88.1 8.4 %collective-permute-done.6 = bf16[768,512]{1,0:T(8,128)(2,1)} collective-permute-done((bf16[768,512]{1,0:T(8,128)(2,1)}, bf16[768,512]{1,0:T(8,128)(2,1)}, u32[]{:S(2)}, u32[]{:S(2)}) %collective-permute-start.6) | collective-permute-done | bytes 786464 | tf_op jit(solution)/shard_map/ppermute | solution.py:82
  96.5 1.9 collective-permute-start.8
  98.4 1.6 fusion.47
  100.1 4.6 %collective-permute-start.9 = (bf16[768,512]{1,0:T(8,128)(2,1)}, bf16[768,512]{1,0:T(8,128)(2,1)}, u32[]{:S(2)}, u32[]{:S(2)}) collective-permute-start(bf16[768,512]{1,0:T(8,128)(2,1)} %collective-permute-done.7), channel_id=1, source_target_pairs={{0,15},{1,0},{2,1},{3,2},{4,3},{5,4},{6,5},{7,6},{8,7},{9,8},{10,9... | collective-permute-start | bytes 2359304 | tf_op jit(solution)/shard_map/ppermute | solution.py:83
  104.6 1.6 fusion.18
  106.5 0.5 broadcast.53
  107.0 0.9 reduce.7
  107.9 0.6 reshape.98
  108.5 7.7 %all-to-all-start.2 = ((bf16[16,2,768]{2,1,0:T(2,128)(2,1)}), bf16[16,2,768]{2,1,0:T(2,128)(2,1)S(1)}, u32[]{:S(2)}, u32[]{:S(2)}) async-start(bf16[16,2,768]{2,1,0:T(2,128)(2,1)} %reshape.98), calls=%async_computation.2 | async-start | bytes 98304 | tf_op jit(solution)/shard_map/all_to_all | solution.py:50
  116.2 3.3 %collective-permute-start.10 = (bf16[768,512]{1,0:T(8,128)(2,1)}, bf16[768,512]{1,0:T(8,128)(2,1)}, u32[]{:S(2)}, u32[]{:S(2)}) collective-permute-start(bf16[768,512]{1,0:T(8,128)(2,1)} %collective-permute-done.8), channel_id=1, source_target_pairs={{0,1},{1,2},{2,3},{3,4},{4,5},{5,6},{6,7},{7,8},{8,9},{9,10},{10,1... | collective-permute-start | bytes 2359304 | tf_op jit(solution)/shard_map/ppermute | solution.py:82
  119.5 1.6 fusion.44
  121.2 3.2 %collective-permute-start.11 = (bf16[768,512]{1,0:T(8,128)(2,1)}, bf16[768,512]{1,0:T(8,128)(2,1)}, u32[]{:S(2)}, u32[]{:S(2)}) collective-permute-start(bf16[768,512]{1,0:T(8,128)(2,1)} %collective-permute-done.9), channel_id=1, source_target_pairs={{0,15},{1,0},{2,1},{3,2},{4,3},{5,4},{6,5},{7,6},{8,7},{9,8},{10,9... | collective-permute-start | bytes 2359304 | tf_op jit(solution)/shard_map/ppermute | solution.py:83
  124.4 1.6 fusion.17
  126.0 2.1 %all-to-all-done.2 = bf16[16,2,768]{2,1,0:T(2,128)(2,1)S(1)} async-done(((bf16[16,2,768]{2,1,0:T(2,128)(2,1)}), bf16[16,2,768]{2,1,0:T(2,128)(2,1)S(1)}, u32[]{:S(2)}, u32[]{:S(2)}) %all-to-all-start.2) | async-done | bytes 49184 | tf_op jit(solution)/shard_map/all_to_all | solution.py:50
  128.2 1.6 fusion.41
  129.8 3.0 %collective-permute-done.10 = bf16[768,512]{1,0:T(8,128)(2,1)} collective-permute-done((bf16[768,512]{1,0:T(8,128)(2,1)}, bf16[768,512]{1,0:T(8,128)(2,1)}, u32[]{:S(2)}, u32[]{:S(2)}) %collective-permute-start.10) | collective-permute-done | bytes 786464 | tf_op jit(solution)/shard_map/ppermute | solution.py:82
  132.8 1.3 fusion.5
  134.1 15.5 %all-to-all-start.3 = ((bf16[32,48,256]{2,1,0:T(8,128)(2,1)}), bf16[32,48,256]{2,1,0:T(8,128)(2,1)}, u32[]{:S(2)}, u32[]{:S(2)}) async-start(bf16[32,48,256]{2,1,0:T(8,128)(2,1)} %bitcast.24), calls=%async_computation.3 | async-start | bytes 1572864 | tf_op jit(solution)/shard_map/all_to_all | solution.py:58
  149.6 2.1 %collective-permute-start.12 = (bf16[768,512]{1,0:T(8,128)(2,1)}, bf16[768,512]{1,0:T(8,128)(2,1)S(1)}, u32[]{:S(2)}, u32[]{:S(2)}) collective-permute-start(bf16[768,512]{1,0:T(8,128)(2,1)} %collective-permute-done.10), channel_id=1, source_target_pairs={{0,1},{1,2},{2,3},{3,4},{4,5},{5,6},{6,7},{7,8},{8,9},{9,10},{10,1... | collective-permute-start | bytes 2359304 | tf_op jit(solution)/shard_map/ppermute | solution.py:82
  151.7 4.3 %collective-permute-start.13 = (bf16[768,512]{1,0:T(8,128)(2,1)}, bf16[768,512]{1,0:T(8,128)(2,1)S(1)}, u32[]{:S(2)}, u32[]{:S(2)}) collective-permute-start(bf16[768,512]{1,0:T(8,128)(2,1)} %collective-permute-done.11), channel_id=1, source_target_pairs={{0,15},{1,0},{2,1},{3,2},{4,3},{5,4},{6,5},{7,6},{8,7},{9,8},{10,9... | collective-permute-start | bytes 2359304 | tf_op jit(solution)/shard_map/ppermute | solution.py:83
  156.1 1.6 fusion.16
  157.7 1.6 fusion.38
  159.4 1.6 fusion.15
  161.0 10.7 %collective-permute-done.12 = bf16[768,512]{1,0:T(8,128)(2,1)S(1)} collective-permute-done((bf16[768,512]{1,0:T(8,128)(2,1)}, bf16[768,512]{1,0:T(8,128)(2,1)S(1)}, u32[]{:S(2)}, u32[]{:S(2)}) %collective-permute-start.12) | collective-permute-done | bytes 786464 | tf_op jit(solution)/shard_map/ppermute | solution.py:82
  171.7 0.9 copy-done.1
  172.7 1.9 collective-permute-start.14
  174.6 0.9 copy-done.3
  175.5 0.8 slice.17
  176.3 4.9 %collective-permute-start.15 = (bf16[384,512]{1,0:T(8,128)(2,1)}, bf16[384,512]{1,0:T(8,128)(2,1)}, u32[]{:S(2)}, u32[]{:S(2)}) collective-permute-start(bf16[384,512]{1,0:T(8,128)(2,1)} %slice.17), channel_id=1, source_target_pairs={{0,15},{1,0},{2,1},{3,2},{4,3},{5,4},{6,5},{7,6},{8,7},{9,8},{10,9... | collective-permute-start | bytes 1179656 | tf_op jit(solution)/shard_map/ppermute | solution.py:87
  181.2 2.4 %fusion.22 = f32[768,256]{0,1:T(8,128)S(1)} fusion(bf16[1536,256]{1,0:T(8,128)(2,1)} %bitcast.25, s32[768]{0:T(1024)S(1)} %get-tuple-element.13), kind=kOutput, calls=%fused_computation.34 | convolution fusion | flops 605552640 | bytes 1575936 | tf_op jit(solution)/shard_map/dot_general | solution.py:59
  183.6 1.4 fusion.35
  184.9 0.4 collective-permute-done.14
  185.4 3.1 %collective-permute-done.15 = bf16[384,512]{1,0:T(8,128)(2,1)} collective-permute-done((bf16[384,512]{1,0:T(8,128)(2,1)}, bf16[384,512]{1,0:T(8,128)(2,1)}, u32[]{:S(2)}, u32[]{:S(2)}) %collective-permute-start.15) | collective-permute-done | bytes 393248 | tf_op jit(solution)/shard_map/ppermute | solution.py:87
  188.4 1.6 fusion.26
  190.1 1.4 fusion.20
  191.5 0.9 copy.20
  (34 shorter events, 0.5 us)
Async XLA Ops:
  0.0 78.9 %copy-start = (bf16[12,16,512]{2,1,0:T(8,128)(2,1)S(1)}, bf16[12,16,512]{2,1,0:T(8,128)(2,1)}, u32[]{:S(2)}) copy-start(bf16[12,16,512]{2,1,0:T(8,128)(2,1)} %param.7) | copy-start | bytes 589828
  0.0 35.8 %collective-permute-start = (bf16[768,512]{1,0:T(8,128)(2,1)}, bf16[768,512]{1,0:T(8,128)(2,1)}, u32[]{:S(2)}, u32[]{:S(2)}) collective-permute-start(bf16[768,512]{1,0:T(8,128)(2,1)} %param.5), channel_id=1, source_target_pairs={{0,1},{1,2},{2,3},{3,4},{4,5},{5,6},{6,7},{7,8},{8,9},{9,10},{10,1... | collective-permute-start | bytes 2359304 | tf_op jit(solution)/shard_map/ppermute | solution.py:82
  4.5 26.0 %collective-permute-start.1 = (bf16[768,512]{1,0:T(8,128)(2,1)}, bf16[768,512]{1,0:T(8,128)(2,1)}, u32[]{:S(2)}, u32[]{:S(2)}) collective-permute-start(bf16[768,512]{1,0:T(8,128)(2,1)} %param.5), channel_id=1, source_target_pairs={{0,15},{1,0},{2,1},{3,2},{4,3},{5,4},{6,5},{7,6},{8,7},{9,8},{10,9... | collective-permute-start | bytes 2359304 | tf_op jit(solution)/shard_map/ppermute | solution.py:83
  19.3 18.7 %copy-start.5 = (bf16[768,512]{1,0:T(8,128)(2,1)S(1)}, bf16[768,512]{1,0:T(8,128)(2,1)}, u32[]{:S(2)}) copy-start(bf16[768,512]{1,0:T(8,128)(2,1)} %param.5) | copy-start | bytes 2359300
  20.8 42.8 %all-to-all-start = ((bf16[32,56,512]{2,1,0:T(8,128)(2,1)}), bf16[32,56,512]{2,1,0:T(8,128)(2,1)S(1)}, u32[]{:S(2)}, u32[]{:S(2)}) async-start(bf16[32,56,512]{2,1,0:T(8,128)(2,1)} %fusion.10), calls=%async_computation | async-start | bytes 3670016 | tf_op jit(solution)/shard_map/all_to_all | solution.py:37
  30.5 20.9 %collective-permute-start.3 = (bf16[768,512]{1,0:T(8,128)(2,1)}, bf16[768,512]{1,0:T(8,128)(2,1)}, u32[]{:S(2)}, u32[]{:S(2)}) collective-permute-start(bf16[768,512]{1,0:T(8,128)(2,1)} %collective-permute-done.1), channel_id=1, source_target_pairs={{0,15},{1,0},{2,1},{3,2},{4,3},{5,4},{6,5},{7,6},{8,7},{9,8},{10,9... | collective-permute-start | bytes 2359304 | tf_op jit(solution)/shard_map/ppermute | solution.py:83
  35.8 20.9 %collective-permute-start.2 = (bf16[768,512]{1,0:T(8,128)(2,1)}, bf16[768,512]{1,0:T(8,128)(2,1)}, u32[]{:S(2)}, u32[]{:S(2)}) collective-permute-start(bf16[768,512]{1,0:T(8,128)(2,1)} %collective-permute-done), channel_id=1, source_target_pairs={{0,1},{1,2},{2,3},{3,4},{4,5},{5,6},{6,7},{7,8},{8,9},{9,10},{10,1... | collective-permute-start | bytes 2359304 | tf_op jit(solution)/shard_map/ppermute | solution.py:82
  51.4 20.0 %collective-permute-start.5 = (bf16[768,512]{1,0:T(8,128)(2,1)}, bf16[768,512]{1,0:T(8,128)(2,1)}, u32[]{:S(2)}, u32[]{:S(2)}) collective-permute-start(bf16[768,512]{1,0:T(8,128)(2,1)} %collective-permute-done.3), channel_id=1, source_target_pairs={{0,15},{1,0},{2,1},{3,2},{4,3},{5,4},{6,5},{7,6},{8,7},{9,8},{10,9... | collective-permute-start | bytes 2359304 | tf_op jit(solution)/shard_map/ppermute | solution.py:83
  56.7 20.0 %collective-permute-start.4 = (bf16[768,512]{1,0:T(8,128)(2,1)}, bf16[768,512]{1,0:T(8,128)(2,1)}, u32[]{:S(2)}, u32[]{:S(2)}) collective-permute-start(bf16[768,512]{1,0:T(8,128)(2,1)} %collective-permute-done.2), channel_id=1, source_target_pairs={{0,1},{1,2},{2,3},{3,4},{4,5},{5,6},{6,7},{7,8},{8,9},{9,10},{10,1... | collective-permute-start | bytes 2359304 | tf_op jit(solution)/shard_map/ppermute | solution.py:82
  71.4 28.7 %collective-permute-start.7 = (bf16[768,512]{1,0:T(8,128)(2,1)}, bf16[768,512]{1,0:T(8,128)(2,1)}, u32[]{:S(2)}, u32[]{:S(2)}) collective-permute-start(bf16[768,512]{1,0:T(8,128)(2,1)} %collective-permute-done.5), channel_id=1, source_target_pairs={{0,15},{1,0},{2,1},{3,2},{4,3},{5,4},{6,5},{7,6},{8,7},{9,8},{10,9... | collective-permute-start | bytes 2359304 | tf_op jit(solution)/shard_map/ppermute | solution.py:83
  76.7 19.8 %collective-permute-start.6 = (bf16[768,512]{1,0:T(8,128)(2,1)}, bf16[768,512]{1,0:T(8,128)(2,1)}, u32[]{:S(2)}, u32[]{:S(2)}) collective-permute-start(bf16[768,512]{1,0:T(8,128)(2,1)} %collective-permute-done.4), channel_id=1, source_target_pairs={{0,1},{1,2},{2,3},{3,4},{4,5},{5,6},{6,7},{7,8},{8,9},{9,10},{10,1... | collective-permute-start | bytes 2359304 | tf_op jit(solution)/shard_map/ppermute | solution.py:82
  80.4 25.9 %all-to-all-start.1 = ((f32[16,1,1536]{2,1,0:T(1,128)}), f32[16,1,1536]{2,1,0:T(1,128)S(1)}, u32[]{:S(2)}, u32[]{:S(2)}) async-start(f32[16,1,1536]{2,1,0:T(1,128)} %reshape.82), calls=%async_computation.1 | async-start | bytes 196608 | tf_op jit(solution)/shard_map/all_to_all | solution.py:47
  96.5 19.7 %collective-permute-start.8 = (bf16[768,512]{1,0:T(8,128)(2,1)}, bf16[768,512]{1,0:T(8,128)(2,1)}, u32[]{:S(2)}, u32[]{:S(2)}) collective-permute-start(bf16[768,512]{1,0:T(8,128)(2,1)} %collective-permute-done.6), channel_id=1, source_target_pairs={{0,1},{1,2},{2,3},{3,4},{4,5},{5,6},{6,7},{7,8},{8,9},{9,10},{10,1... | collective-permute-start | bytes 2359304 | tf_op jit(solution)/shard_map/ppermute | solution.py:82
  100.1 21.1 %collective-permute-start.9 = (bf16[768,512]{1,0:T(8,128)(2,1)}, bf16[768,512]{1,0:T(8,128)(2,1)}, u32[]{:S(2)}, u32[]{:S(2)}) collective-permute-start(bf16[768,512]{1,0:T(8,128)(2,1)} %collective-permute-done.7), channel_id=1, source_target_pairs={{0,15},{1,0},{2,1},{3,2},{4,3},{5,4},{6,5},{7,6},{8,7},{9,8},{10,9... | collective-permute-start | bytes 2359304 | tf_op jit(solution)/shard_map/ppermute | solution.py:83
  106.3 26.5 %copy-start.6 = (bf16[12,16,256]{2,1,0:T(8,128)(2,1)S(1)}, bf16[12,16,256]{2,1,0:T(8,128)(2,1)}, u32[]{:S(2)}) copy-start(bf16[12,16,256]{2,1,0:T(8,128)(2,1)} %param.8) | copy-start | bytes 294916
  108.5 19.6 %all-to-all-start.2 = ((bf16[16,2,768]{2,1,0:T(2,128)(2,1)}), bf16[16,2,768]{2,1,0:T(2,128)(2,1)S(1)}, u32[]{:S(2)}, u32[]{:S(2)}) async-start(bf16[16,2,768]{2,1,0:T(2,128)(2,1)} %reshape.98), calls=%async_computation.2 | async-start | bytes 98304 | tf_op jit(solution)/shard_map/all_to_all | solution.py:50
  116.2 16.5 %collective-permute-start.10 = (bf16[768,512]{1,0:T(8,128)(2,1)}, bf16[768,512]{1,0:T(8,128)(2,1)}, u32[]{:S(2)}, u32[]{:S(2)}) collective-permute-start(bf16[768,512]{1,0:T(8,128)(2,1)} %collective-permute-done.8), channel_id=1, source_target_pairs={{0,1},{1,2},{2,3},{3,4},{4,5},{5,6},{6,7},{7,8},{8,9},{9,10},{10,1... | collective-permute-start | bytes 2359304 | tf_op jit(solution)/shard_map/ppermute | solution.py:82
  121.2 30.6 %collective-permute-start.11 = (bf16[768,512]{1,0:T(8,128)(2,1)}, bf16[768,512]{1,0:T(8,128)(2,1)}, u32[]{:S(2)}, u32[]{:S(2)}) collective-permute-start(bf16[768,512]{1,0:T(8,128)(2,1)} %collective-permute-done.9), channel_id=1, source_target_pairs={{0,15},{1,0},{2,1},{3,2},{4,3},{5,4},{6,5},{7,6},{8,7},{9,8},{10,9... | collective-permute-start | bytes 2359304 | tf_op jit(solution)/shard_map/ppermute | solution.py:83
  134.1 47.0 %all-to-all-start.3 = ((bf16[32,48,256]{2,1,0:T(8,128)(2,1)}), bf16[32,48,256]{2,1,0:T(8,128)(2,1)}, u32[]{:S(2)}, u32[]{:S(2)}) async-start(bf16[32,48,256]{2,1,0:T(8,128)(2,1)} %bitcast.24), calls=%async_computation.3 | async-start | bytes 1572864 | tf_op jit(solution)/shard_map/all_to_all | solution.py:58
  149.6 22.2 %collective-permute-start.12 = (bf16[768,512]{1,0:T(8,128)(2,1)}, bf16[768,512]{1,0:T(8,128)(2,1)S(1)}, u32[]{:S(2)}, u32[]{:S(2)}) collective-permute-start(bf16[768,512]{1,0:T(8,128)(2,1)} %collective-permute-done.10), channel_id=1, source_target_pairs={{0,1},{1,2},{2,3},{3,4},{4,5},{5,6},{6,7},{7,8},{8,9},{9,10},{10,1... | collective-permute-start | bytes 2359304 | tf_op jit(solution)/shard_map/ppermute | solution.py:82
  151.7 22.9 %collective-permute-start.13 = (bf16[768,512]{1,0:T(8,128)(2,1)}, bf16[768,512]{1,0:T(8,128)(2,1)S(1)}, u32[]{:S(2)}, u32[]{:S(2)}) collective-permute-start(bf16[768,512]{1,0:T(8,128)(2,1)} %collective-permute-done.11), channel_id=1, source_target_pairs={{0,15},{1,0},{2,1},{3,2},{4,3},{5,4},{6,5},{7,6},{8,7},{9,8},{10,9... | collective-permute-start | bytes 2359304 | tf_op jit(solution)/shard_map/ppermute | solution.py:83
  171.7 0.9 copy-start.1
  172.7 12.7 %collective-permute-start.14 = (bf16[384,512]{1,0:T(8,128)(2,1)S(1)}, bf16[384,512]{1,0:T(8,128)(2,1)}, u32[]{:S(2)}, u32[]{:S(2)}) collective-permute-start(bf16[384,512]{1,0:T(8,128)(2,1)S(1)} %slice.16), channel_id=1, source_target_pairs={{0,1},{1,2},{2,3},{3,4},{4,5},{5,6},{6,7},{7,8},{8,9},{9,10},{10,1... | collective-permute-start | bytes 1179656 | tf_op jit(solution)/shard_map/ppermute | solution.py:86
  174.6 0.9 copy-start.3
  176.3 7.3 %copy-start.4 = (bf16[768,512]{1,0:T(8,128)(2,1)S(1)}, bf16[768,512]{1,0:T(8,128)(2,1)}, u32[]{:S(2)}) copy-start(bf16[768,512]{1,0:T(8,128)(2,1)} %copy-done.3) | copy-start | bytes 2359300
  176.3 12.2 %collective-permute-start.15 = (bf16[384,512]{1,0:T(8,128)(2,1)}, bf16[384,512]{1,0:T(8,128)(2,1)}, u32[]{:S(2)}, u32[]{:S(2)}) collective-permute-start(bf16[384,512]{1,0:T(8,128)(2,1)} %slice.17), channel_id=1, source_target_pairs={{0,15},{1,0},{2,1},{3,2},{4,3},{5,4},{6,5},{7,6},{8,7},{9,8},{10,9... | collective-permute-start | bytes 1179656 | tf_op jit(solution)/shard_map/ppermute | solution.py:87
  181.2 8.9 %copy-start.2 = (bf16[768,512]{1,0:T(8,128)(2,1)S(1)}, bf16[768,512]{1,0:T(8,128)(2,1)}, u32[]{:S(2)}) copy-start(bf16[768,512]{1,0:T(8,128)(2,1)} %copy-done.1) | copy-start | bytes 2359300

commit v4 on v2

--- a/solution.py
+++ b/solution.py
@@ -32,7 +32,7 @@
     return jnp.concatenate([rows.reshape(groups, owner_slots, d), ids], axis=1), place
 
 
-def lora(here, place, adapter_down, adapter_up, groups, tp):
+def lora(here, place, adapter_down, adapter_up, groups):
     per_group, rank, d = adapter_down.shape
     ho = adapter_up.shape[2]
     slots = groups * owner_slots
@@ -43,12 +43,8 @@
         adapter_down.reshape(per_group * rank, d), rows, (((1,), (1,)), ((), ())), preferred_element_type=F32
     ).reshape(per_group, rank, slots)
     part = jnp.sum(jnp.where(mine, part, 0.0), axis=0)
-    share = rank // tp
-    part = lax.all_to_all(part.reshape(tp, share, slots), "tp", 0, 0, tiled=True)
-    scaled = (adapter_scale_factor * jnp.sum(part, axis=0)).astype(BF16)
-    scaled = lax.all_to_all(
-        jnp.broadcast_to(scaled[None], (tp, share, slots)), "tp", 0, 0, tiled=True
-    ).reshape(1, rank, slots)
+    part = lax.all_gather(part.astype(BF16), "tp", axis=0, tiled=False)
+    scaled = (adapter_scale_factor * jnp.sum(part.astype(F32), axis=0)).astype(BF16)[None]
     spread = jnp.where(mine, scaled, jnp.zeros((), BF16)).reshape(per_group * rank, slots)
     delta = lax.dot_general(
         spread, adapter_up.reshape(per_group * rank, ho), (((0,), (0,)), ((), ())), preferred_element_type=F32
@@ -59,28 +55,30 @@
     ).astype(BF16)
 
 
-def partial_kernel(tok_a, tok_b, w_a, w_b, out):
-    depth = tok_a.shape[1]
-    cols = out.shape[2]
-    acc = jnp.dot(tok_a[...], w_a[...].reshape(depth, cols), preferred_element_type=F32)
-    acc += jnp.dot(tok_b[...], w_b[...].reshape(depth, cols), preferred_element_type=F32)
-    out[0] = acc.astype(out.dtype)
+per_step = 4
+gathered_share = 3
 
 
-def partials(tok_a, tok_b, w_a, w_b):
-    n, depth = tok_a.shape
+def partial_kernel(tok, w_a, w_b, out):
+    half = tok.shape[1] // 2
+    for i in range(out.shape[0]):
+        w = jnp.concatenate([w_a[:, i].reshape(half, -1), w_b[:, i].reshape(half, -1)], axis=0)
+        out[i] = jnp.dot(tok[...], w, preferred_element_type=F32).astype(out.dtype)
+
+
+def partials(tok, w_a, w_b):
+    n, depth = tok.shape
     chips, tp, r, cols = w_a.shape
-    tok_spec = pl.BlockSpec((n, depth), lambda q: (0, 0))
-    w_spec = pl.BlockSpec((chips, 1, r, cols), lambda q: (0, q, 0, 0))
+    w_spec = pl.BlockSpec((chips, per_step, r, cols), lambda q: (0, q, 0, 0))
     return pl.pallas_call(
         partial_kernel,
-        grid=(tp,),
-        in_specs=[tok_spec, tok_spec, w_spec, w_spec],
-        out_specs=pl.BlockSpec((1, n, cols), lambda q: (q, 0, 0)),
+        grid=(tp // per_step,),
+        in_specs=[pl.BlockSpec((n, depth), lambda q: (0, 0)), w_spec, w_spec],
+        out_specs=pl.BlockSpec((per_step, n, cols), lambda q: (q, 0, 0)),
         out_shape=jax.ShapeDtypeStruct((tp, n, cols), BF16),
         compiler_params=pltpu.CompilerParams(dimension_semantics=("arbitrary",)),
         name="partials",
-    )(tok_a, tok_b, w_a, w_b)
+    )(tok, w_a, w_b)
 
 
 def solution(mesh):
@@ -93,26 +91,39 @@
         n, depth = tokens.shape
         cols = w_query.shape[1]
         r = depth // groups
+        half = depth // 2
+        whole = n // gathered_share
         me = lax.axis_index("group")
         core, chip = me % 2, me // 2
+        gathered = lax.all_gather(tokens[:whole], "tp", axis=0, tiled=False)
         w_mine = lax.dynamic_index_in_dim(
             w_query.reshape(tp, groups, r, cols), core * chips + chip, 1, keepdims=False
         )
         w_mine = lax.all_to_all(w_mine, "tp", 0, 0, tiled=True)
-        w_half = lax.all_to_all(
+        w_own = lax.all_to_all(
             jnp.broadcast_to(w_mine[None], (chips, tp, r, cols)), "group", 0, 0, axis_index_groups=same_core, tiled=True
         )
         sent, place = outgoing(tokens, adapter_id, groups, adapter_down.shape[0])
-        w_half, sent = lax.optimization_barrier((w_half, sent))
-        w_other = lax.ppermute(w_half, "group", other_core)
+        tok = jnp.concatenate(
+            [
+                lax.dynamic_slice_in_dim(tokens[whole:], core * half, half, 1),
+                lax.dynamic_slice_in_dim(tokens[whole:], (1 - core) * half, half, 1),
+            ],
+            axis=1,
+        )
+        w_own, sent, tok = lax.optimization_barrier((w_own, sent, tok))
+        w_other = lax.ppermute(w_own, "group", other_core)
         here = lax.all_to_all(sent, "group", 0, 0, tiled=True)
-        half = depth // 2
-        tok_half = lax.dynamic_slice_in_dim(tokens, core * half, half, 1)
-        tok_other = lax.dynamic_slice_in_dim(tokens, (1 - core) * half, half, 1)
-        part = partials(tok_half, tok_other, w_half, w_other)
+        part = partials(tok, w_own, w_other)
         base = lax.psum_scatter(part, "tp", scatter_dimension=0, tiled=False)
-        delta = lora(here, place, adapter_down, adapter_up, groups, tp)
-        return (base.astype(F32) + delta.astype(F32)).astype(BF16)
+        here, gathered, _ = lax.optimization_barrier((here, gathered, part))
+        first = jnp.einsum(
+            "znd,zdh->nh", gathered, w_query.reshape(tp, depth, cols), preferred_element_type=F32
+        )
+        delta = lora(here, place, adapter_down, adapter_up, groups).astype(F32)
+        return jnp.concatenate(
+            [(first + delta[:whole]).astype(BF16), (base.astype(F32) + delta[whole:]).astype(BF16)], axis=0
+        )
 
     placed = (
         P("group", "tp"),

time: 197 us -> 194 us (0.985)
  Pallas kernels: 13.6 us -> 6.19 us
  blocking collectives: 113 us -> 115 us
    all_gather x0 -> x1, blocking collectives: none -> 35.4 us  [lora(): part = lax.all_gather(part.astype(BF16), 'tp', axis=0, tiled=False)]
    all_to_all x2 -> x0, blocking collectives: 35.3 us -> none  [the longest x1 17.8 us: lora(): lax.all_to_all(part.reshape(tp, share, slots), 'tp', 0, 0, tiled=True)]
    pallas_call x1, Pallas kernels: 13.6 us -> 6.19 us  [partials(): pl.pallas_call(partial_kernel, grid=(tp // per_step,), in_specs=[pl.Block...]
  transfers between devices with their start and end apart: 3 -> 4, of which waited for: 2 -> 2; matrix products, arithmetic and copies ran while one was open for 5% -> 7% of each run, Pallas kernels for 0% -> 3%
where the time goes in v4:
time: 194 us; the launch traced here: 193 us
  blocking collectives  115 us (59%)
  waiting for transfers between devices  23.2 us (12%)
  starting transfers between devices  14.8 us (8%)
  between operations  13.6 us (7%)
  local copies, waits for them, and re-layouts  8.58 us (4%)
  matrix products  6.39 us (3%)
  Pallas kernels  6.19 us (3%)
  other arithmetic  5.25 us (3%)
    all_gather x1, blocking collectives, lora(): part = lax.all_gather(part.astype(BF16), 'tp', axis=0, tiled=False)  35.4 us
    all_to_all x1, blocking collectives, on_device(): here = lax.all_to_all(sent, 'group', 0, 0, tiled=True)  30.3 us
    all_to_all x1, blocking collectives, on_device(): w_mine = lax.all_to_all(w_mine, 'tp', 0, 0, tiled=True)  27.6 us
    all_to_all x1, blocking collectives, lora(): lax.all_to_all(delta.reshape(groups, owner_slots, ho), 'group', 0, 0, til...  21.6 us
    all_to_all x1, waiting for transfers between devices, on_device(): lax.all_to_all(jnp.broadcast_to(w_mine[None], (chips, tp, r, cols)), 'gro...  19.3 us
    ppermute x1, starting transfers between devices, on_device(): w_other = lax.ppermute(w_own, 'group', other_core)  7.92 us
    all_to_all x1, starting transfers between devices, on_device(): lax.all_to_all(jnp.broadcast_to(w_mine[None], (chips, tp, r, cols)), 'gro...  6.86 us
    pallas_call x1, Pallas kernels, partials(): pl.pallas_call(partial_kernel, grid=(tp // per_step,), in_specs=[pl.Block...  6.19 us
  transfers between devices with their start and end apart: 4, of which 2 were waited for; matrix products, arithmetic and copies ran while one was open for 7% of the time, Pallas kernels for 3%

profile of v4, /device:TPU:1, one launch (start us, length us, event | category | flops | bytes accessed | tf_op | source)
XLA Modules:
  0.0 193.0 jit_solution(15002571914592970780)
XLA Ops:
  6.5 0.0 copy-start
  6.5 0.0 all-gather.4.cloned.1.call-start
  6.5 1.7 slice.20
  8.2 0.0 all-gather.4.cloned.1.call-update
  8.3 0.9 dynamic-slice_bitcast_fusion
  9.2 27.6 %all_to_all.20 = bf16[16,16,256]{2,1,0:T(8,128)(2,1)S(1)} all-to-all(bf16[16,16,256]{2,1,0:T(8,128)(2,1)S(1)} %dynamic-slice_bitcast_fusion), channel_id=1, replica_groups=mesh['group'=32,'tp'=16] {'tp'}, dimensions={0} | all-to-all | bytes 262144 | tf_op jit(solution)/shard_map/all_to_all | solution.py:102
  36.8 1.5 broadcast_in_dim.44
  38.3 0.0 copy-start.4
  38.3 6.9 %all-to-all-start.1 = ((bf16[16,16,16,256]{3,2,1,0:T(8,128)(2,1)}), bf16[16,16,16,256]{3,2,1,0:T(8,128)(2,1)S(1)}, u32[]{:S(2)}, u32[]{:S(2)}) async-start(bf16[16,16,16,256]{3,2,1,0:T(8,128)(2,1)} %broadcast_in_dim.44), calls=%async_computation.1 | async-start | bytes 4194304 | tf_op jit(solution)/shard_map/all_to_all | solution.py:103
  45.2 0.0 slice-start
  45.2 0.0 reduce-scatter.2.cloned.1.call-start
  45.3 0.0 copy-done.4
  45.3 0.4 fusion.16
  45.7 0.9 fusion.17
  46.6 0.1 reshape.97
  46.7 0.0 slice-done
  46.7 0.0 copy-start.3
  46.8 0.8 pad_maximum_fusion.tok
  47.6 0.4 copy-done.3
  48.0 1.4 fusion.4
  49.4 1.4 fusion.10
  50.8 19.3 %all-to-all-done.1.w_a = bf16[16,16,16,256]{3,2,1,0:T(8,128)(2,1)S(1)} async-done(((bf16[16,16,16,256]{3,2,1,0:T(8,128)(2,1)}), bf16[16,16,16,256]{3,2,1,0:T(8,128)(2,1)S(1)}, u32[]{:S(2)}, u32[]{:S(2)}) %all-to-all-start.1) | async-done | bytes 2097184 | tf_op jit(solution)/shard_map/all_to_all | solution.py:103
  70.1 0.0 copy-start.1
  70.1 7.9 %collective-permute-start = (bf16[16,16,16,256]{3,2,1,0:T(8,128)(2,1)S(1)}, bf16[16,16,16,256]{3,2,1,0:T(8,128)(2,1)}, u32[]{:S(2)}, u32[]{:S(2)}) collective-permute-start(bf16[16,16,16,256]{3,2,1,0:T(8,128)(2,1)S(1)} %all-to-all-done.1.w_a), channel_id=1, source_target_pairs={{0,16},{16,0},{32,48},{48,32},{64,80},{80,64},{96,112},{112,96},{1... | collective-permute-start | bytes 6291464 | tf_op jit(solution)/shard_map/ppermute | solution.py:115
  78.1 3.9 %collective-permute-done.w_b = bf16[16,16,16,256]{3,2,1,0:T(8,128)(2,1)} collective-permute-done((bf16[16,16,16,256]{3,2,1,0:T(8,128)(2,1)S(1)}, bf16[16,16,16,256]{3,2,1,0:T(8,128)(2,1)}, u32[]{:S(2)}, u32[]{:S(2)}) %collective-permute-start) | collective-permute-done | bytes 2097184 | tf_op jit(solution)/shard_map/ppermute | solution.py:115
  82.0 0.0 copy-done.1
  82.0 6.2 %partials.1 = bf16[16,512,256]{2,1,0:T(8,128)(2,1)} custom-call(bf16[512,512]{1,0:T(8,128)(2,1)} %pad_maximum_fusion.tok, bf16[16,16,16,256]{3,2,1,0:T(8,128)(2,1)} %copy-done.1, bf16[16,16,16,256]{3,2,1,0:T(8,128)(2,1)} %collective-permute-done.w_b), custom_call_target="tpu_custom_call" | custom-call | tf_op jit(solution)/shard_map/partials/pallas_call | solution.py:73
  88.2 0.0 copy-start.2
  88.2 0.0 reduce-scatter.2.cloned.1.call-update
  88.2 1.5 copy-done.2
  89.7 30.3 %all_to_all.21 = bf16[32,56,512]{2,1,0:T(8,128)(2,1)} all-to-all(bf16[32,56,512]{2,1,0:T(8,128)(2,1)S(1)} %copy-done.2), channel_id=1, replica_groups=mesh['group'=32,'tp'=16] {'group'}, dimensions={0} | all-to-all | bytes 3670016 | tf_op jit(solution)/shard_map/all_to_all | solution.py:116
  120.0 0.0 all-gather.4.cloned.1.call-done
  120.0 1.5 slice.22
  121.5 0.9 convert_reduce_fusion.1
  122.4 0.1 reshape.87
  122.5 0.0 copy-done
  122.5 0.7 fusion.27
  123.2 0.0 copy-start.7
  123.2 0.1 select_reduce_fusion
  123.4 35.4 %all-gather.1 = bf16[256,1536]{1,0:T(8,128)(2,1)S(1)} all-gather(bf16[16,1536]{1,0:T(8,128)(2,1)S(1)} %select_reduce_fusion), channel_id=3, replica_groups=mesh['group'=32,'tp'=16] {'tp'}, dimensions={0}, use_global_device_ids=true | all-gather | bytes 835584 | tf_op jit(solution)/shard_map/all_gather | solution.py:46
  158.7 0.1 convert_reduce_fusion
  158.9 0.0 copy-done.7
  158.9 0.4 fusion.5
  159.3 0.0 copy-start.6
  159.3 21.6 %all_to_all.22 = bf16[32,48,256]{2,1,0:T(8,128)(2,1)S(1)} all-to-all(bf16[32,48,256]{2,1,0:T(8,128)(2,1)S(1)} %bitcast.41), channel_id=1, replica_groups=mesh['group'=32,'tp'=16] {'group'}, dimensions={0} | all-to-all | bytes 1572864 | tf_op jit(solution)/shard_map/all_to_all | solution.py:52
  180.9 0.0 copy-start.5
  180.9 1.4 fusion.12
  182.3 0.0 copy-done.6
  182.3 0.8 copy-done.5
  183.1 1.2 fusion.14
  184.3 0.0 reduce-scatter.2.cloned.1.call-done
  184.4 1.0 fusion.20
  185.4 0.8 pad_maximum_fusion.1
  (6 shorter events, 0.1 us)
Async XLA Ops:
  6.5 116.0 %copy-start = (bf16[12,16,512]{2,1,0:T(8,128)(2,1)S(1)}, bf16[12,16,512]{2,1,0:T(8,128)(2,1)}, u32[]{:S(2)}) copy-start(bf16[12,16,512]{2,1,0:T(8,128)(2,1)} %param.7) | copy-start | bytes 589828
  6.5 113.5 %all-gather.4.cloned.1.call-start = ((), (), s32[]{:S(2)}) async-start(), calls=%async_computation.6 | async-start | bytes 4456448 | tf_op jit(solution)/shard_map/all_gather | solution.py:98
  38.3 6.9 %copy-start.4 = (s32[768]{0:T(1024)S(1)}, s32[768]{0:T(1024)}, u32[]{:S(2)}) copy-start(s32[768]{0:T(1024)} %param.9) | copy-start | bytes 9220
  38.3 31.8 %all-to-all-start.1 = ((bf16[16,16,16,256]{3,2,1,0:T(8,128)(2,1)}), bf16[16,16,16,256]{3,2,1,0:T(8,128)(2,1)S(1)}, u32[]{:S(2)}, u32[]{:S(2)}) async-start(bf16[16,16,16,256]{3,2,1,0:T(8,128)(2,1)} %broadcast_in_dim.44), calls=%async_computation.1 | async-start | bytes 4194304 | tf_op jit(solution)/shard_map/all_to_all | solution.py:103
  45.2 1.5 slice-start
  45.2 139.2 %reduce-scatter.2.cloned.1.call-start = ((), (), s32[]{:S(2)}) async-start(), calls=%async_computation.5 | async-start | bytes 4456448 | tf_op jit(solution)/shard_map/reduce_scatter | solution.py:118
  46.7 1.3 copy-start.3
  70.1 11.8 %copy-start.1 = (bf16[16,16,16,256]{3,2,1,0:T(8,128)(2,1)}, bf16[16,16,16,256]{3,2,1,0:T(8,128)(2,1)S(1)}, u32[]{:S(2)}) copy-start(bf16[16,16,16,256]{3,2,1,0:T(8,128)(2,1)S(1)} %all-to-all-done.1.w_a) | copy-start | bytes 6291460
  70.1 11.8 %collective-permute-start = (bf16[16,16,16,256]{3,2,1,0:T(8,128)(2,1)S(1)}, bf16[16,16,16,256]{3,2,1,0:T(8,128)(2,1)}, u32[]{:S(2)}, u32[]{:S(2)}) collective-permute-start(bf16[16,16,16,256]{3,2,1,0:T(8,128)(2,1)S(1)} %all-to-all-done.1.w_a), channel_id=1, source_target_pairs={{0,16},{16,0},{32,48},{48,32},{64,80},{80,64},{96,112},{112,96},{1... | collective-permute-start | bytes 6291464 | tf_op jit(solution)/shard_map/ppermute | solution.py:115
  88.2 1.5 copy-start.2
  123.2 35.7 %copy-start.7 = (bf16[12,16,256]{2,1,0:T(8,128)(2,1)S(1)}, bf16[12,16,256]{2,1,0:T(8,128)(2,1)}, u32[]{:S(2)}) copy-start(bf16[12,16,256]{2,1,0:T(8,128)(2,1)} %param.8) | copy-start | bytes 294916
  159.3 23.0 %copy-start.6 = (bf16[4096,512]{1,0:T(8,128)(2,1)S(1)}, bf16[4096,512]{1,0:T(8,128)(2,1)}, u32[]{:S(2)}) copy-start(bf16[4096,512]{1,0:T(8,128)(2,1)} %all-gather.4.cloned.1.call-done) | copy-start | bytes 12582916
  180.9 2.2 %copy-start.5 = (bf16[8192,256]{1,0:T(8,128)(2,1)S(1)}, bf16[8192,256]{1,0:T(8,128)(2,1)}, u32[]{:S(2)}) copy-start(bf16[8192,256]{1,0:T(8,128)(2,1)} %param.6) | copy-start | bytes 12582916
Sparse Core Ops, SparseCore 0:
  9.4 76.0 all-gather.3
  88.4 80.0 reduce-scatter.1

commit v5 on v3

--- a/solution.py
+++ b/solution.py
@@ -5,6 +5,7 @@
 
 adapter_scale_factor = 2.0
 owner_slots = 48
+ring_share = 3
 F32, BF16 = jnp.float32, jnp.bfloat16
 
 
@@ -76,8 +77,12 @@
             block = lax.dynamic_index_in_dim(w, owner % tp, 0, keepdims=False)
             return jnp.dot(rows, block, preferred_element_type=F32)
 
-        from_left = [tokens]
-        from_right = [tokens]
+        whole = n - n // ring_share
+        gathered = lax.all_gather(tokens[:whole], "tp", axis=1, tiled=True)
+        ring = tokens[whole:]
+        n = n - whole
+        from_left = [ring]
+        from_right = [ring]
         for t in range(1, tp // 2):
             from_left.append(lax.ppermute(from_left[-1], "tp", right))
             from_right.append(lax.ppermute(from_right[-1], "tp", left))
@@ -88,7 +93,7 @@
             ],
             axis=0,
         )
-        base = times_w(tokens, z)
+        base = times_w(ring, z)
         for t in range(1, tp // 2):
             base += times_w(from_left[t], z + tp - t)
             base += times_w(from_right[t], z + t)
@@ -99,7 +104,10 @@
 
         sent, place = outgoing(tokens, adapter_id, groups, adapter_down.shape[0])
         delta = lora(sent, place, at, adapter_down, adapter_up, groups, tp)
-        return (base + delta.astype(F32)).astype(BF16)
+        delta, base, gathered = lax.optimization_barrier((delta, base, gathered))
+        first = jnp.dot(gathered, w_query, preferred_element_type=F32) + delta[:whole].astype(F32)
+        base += delta[whole:].astype(F32)
+        return jnp.concatenate([first.astype(BF16), base.astype(BF16)], axis=0)
 
     placed = (
         P("group", "tp"),

time: 196 us -> 204 us (1.041); the launches traced: 192 us -> 203 us
  between operations: 0.77 us -> 14.1 us
  waiting for transfers between devices: 47.4 us -> 43.8 us
  starting transfers between devices: 101 us -> 98.7 us
    ppermute x7, waiting for transfers between devices: 22.1 us -> 0.94 us  [on_device(): from_left.append(lax.ppermute(from_left[-1], 'tp', right))]
    all_to_all x1, waiting for transfers between devices: 2.07 us -> 10.7 us  [lora(): lax.all_to_all(jnp.broadcast_to(scaled[None], (tp, share, slots)), 'tp',...]
    dot_general x0 -> x1, matrix products: none -> 6.9 us  [on_device(): jnp.dot(gathered, w_query, preferred_element_type=F32)]
    dot_general x16, matrix products: 25.4 us -> 19 us  [times_w(): return jnp.dot(rows, block, preferred_element_type=F32)]
    ppermute x7, waiting for transfers between devices: 19.8 us -> 25.9 us  [on_device(): from_right.append(lax.ppermute(from_right[-1], 'tp', left))]
    all_to_all x1, waiting for transfers between devices: 0.01 us -> 3.61 us  [lora(): lax.all_to_all(part.reshape(tp, share, slots), 'tp', 0, 0, tiled=True)]
    slice x0 -> x2, local copies, waits for them, and re-layouts: none -> 2.9 us  [the longest x1 1.93 us: on_device(): gathered = lax.all_gather(tokens[:whole], 'tp', axis=1, tiled=True)]
    all_to_all x1, starting transfers between devices: 15.5 us -> 13 us  [lora(): lax.all_to_all(delta.reshape(groups, owner_slots, ho), 'group', 0, 0, til...]
  transfers between devices with their start and end apart: 20 -> 21, of which waited for: 9 -> 13; matrix products, arithmetic and copies ran while one was open for 20% -> 18% of each run, Pallas kernels for 0% -> 0%
where the time goes in v5:
time: 204 us; the launch traced here: 203 us
  starting transfers between devices  98.7 us (48%)
  waiting for transfers between devices  43.8 us (21%)
  matrix products  34.6 us (17%)
  between operations  14.1 us (7%)
  local copies, waits for them, and re-layouts  6.46 us (3%)
  other arithmetic  4.86 us (2%)
    ppermute x7, starting transfers between devices, on_device(): from_right.append(lax.ppermute(from_right[-1], 'tp', left))  38 us
    ppermute x7, waiting for transfers between devices, on_device(): from_right.append(lax.ppermute(from_right[-1], 'tp', left))  25.9 us
    dot_general x16, matrix products, times_w(): return jnp.dot(rows, block, preferred_element_type=F32)  19 us
    ppermute x7, starting transfers between devices, on_device(): from_left.append(lax.ppermute(from_left[-1], 'tp', right))  17.2 us
    all_to_all x1, starting transfers between devices, lora(): lax.all_to_all(delta.reshape(groups, owner_slots, ho), 'group', 0, 0, til...  13 us
    all_to_all x1, waiting for transfers between devices, lora(): lax.all_to_all(jnp.broadcast_to(scaled[None], (tp, share, slots)), 'tp',...  10.7 us
    all_to_all x1, starting transfers between devices, lora(): here = lax.all_to_all(at(0, sent), 'group', 0, 0, tiled=True)  8.04 us
    all_to_all x1, starting transfers between devices, lora(): lax.all_to_all(part.reshape(tp, share, slots), 'tp', 0, 0, tiled=True)  7.91 us
  transfers between devices with their start and end apart: 21, of which 13 were waited for; matrix products, arithmetic and copies ran while one was open for 18% of the time, Pallas kernels for 0%

profile of v5, /device:TPU:1, one launch (start us, length us, event | category | flops | bytes accessed | tf_op | source)
XLA Modules:
  0.0 202.6 jit_solution(9362071527639114805)
XLA Ops:
  6.5 1.9 slice.29
  8.5 1.0 slice.24
  9.5 4.4 %collective-permute-start = (bf16[256,512]{1,0:T(8,128)(2,1)S(1)}, bf16[256,512]{1,0:T(8,128)(2,1)S(1)}, u32[]{:S(2)}, u32[]{:S(2)}) collective-permute-start(bf16[256,512]{1,0:T(8,128)(2,1)S(1)} %slice.24), channel_id=1, source_target_pairs={{0,1},{1,2},{2,3},{3,4},{4,5},{5,6},{6,7},{7,8},{8,9},{9,10},{10,1... | collective-permute-start | bytes 786440 | tf_op jit(solution)/shard_map/ppermute | solution.py:87
  13.9 9.5 %collective-permute-start.6 = (bf16[256,512]{1,0:T(8,128)(2,1)S(1)}, bf16[256,512]{1,0:T(8,128)(2,1)S(1)}, u32[]{:S(2)}, u32[]{:S(2)}) collective-permute-start(bf16[256,512]{1,0:T(8,128)(2,1)S(1)} %slice.24), channel_id=1, source_target_pairs={{0,15},{1,0},{2,1},{3,2},{4,3},{5,4},{6,5},{7,6},{8,7},{9,8},{10,9... | collective-permute-start | bytes 786440 | tf_op jit(solution)/shard_map/ppermute | solution.py:88
  23.4 0.7 add_select_fusion.1
  24.1 0.4 fusion.22
  24.4 0.7 convert_add_fusion
  25.1 0.9 fusion.23
  26.1 2.5 %fusion.4 = bf16[1536,512]{1,0:T(8,128)(2,1)S(1)} fusion(bf16[768,512]{1,0:T(8,128)(2,1)} %param.5, s32[768]{0:T(1024)S(1)} %get-tuple-element.19), kind=kOutput, calls=%fused_computation.6 | convolution fusion | flops 1209925632 | bytes 2362368 | tf_op jit(solution)/shard_map/dot_general | solution.py:27
  28.7 1.4 fusion.10
  30.1 8.0 %all-to-all-start = ((bf16[32,56,512]{2,1,0:T(8,128)(2,1)}), bf16[32,56,512]{2,1,0:T(8,128)(2,1)S(1)}, u32[]{:S(2)}, u32[]{:S(2)}) async-start(bf16[32,56,512]{2,1,0:T(8,128)(2,1)} %fusion.10), calls=%async_computation | async-start | bytes 3670016 | tf_op jit(solution)/shard_map/all_to_all | solution.py:38
  38.4 1.3 fusion.53
  39.7 3.6 %collective-permute-start.7 = (bf16[256,512]{1,0:T(8,128)(2,1)S(1)}, bf16[256,512]{1,0:T(8,128)(2,1)S(1)}, u32[]{:S(2)}, u32[]{:S(2)}) collective-permute-start(bf16[256,512]{1,0:T(8,128)(2,1)S(1)} %collective-permute-done.6), channel_id=1, source_target_pairs={{0,15},{1,0},{2,1},{3,2},{4,3},{5,4},{6,5},{7,6},{8,7},{9,8},{10,9... | collective-permute-start | bytes 786440 | tf_op jit(solution)/shard_map/ppermute | solution.py:88
  43.3 1.9 collective-permute-start.1
  45.2 1.2 convolution_add_fusion.8
  46.4 1.2 convolution_add_fusion.7
  47.6 6.8 %collective-permute-done.7 = bf16[256,512]{1,0:T(8,128)(2,1)S(1)} collective-permute-done((bf16[256,512]{1,0:T(8,128)(2,1)S(1)}, bf16[256,512]{1,0:T(8,128)(2,1)S(1)}, u32[]{:S(2)}, u32[]{:S(2)}) %collective-permute-start.7) | collective-permute-done | bytes 262176 | tf_op jit(solution)/shard_map/ppermute | solution.py:88
  54.4 5.4 %collective-permute-start.8 = (bf16[256,512]{1,0:T(8,128)(2,1)S(1)}, bf16[256,512]{1,0:T(8,128)(2,1)S(1)}, u32[]{:S(2)}, u32[]{:S(2)}) collective-permute-start(bf16[256,512]{1,0:T(8,128)(2,1)S(1)} %collective-permute-done.7), channel_id=1, source_target_pairs={{0,15},{1,0},{2,1},{3,2},{4,3},{5,4},{6,5},{7,6},{8,7},{9,8},{10,9... | collective-permute-start | bytes 786440 | tf_op jit(solution)/shard_map/ppermute | solution.py:88
  59.8 0.3 collective-permute-done.1
  60.1 1.9 collective-permute-start.2
  62.0 1.2 fusion.48
  63.2 1.2 fusion.19
  64.4 6.5 %collective-permute-done.8 = bf16[256,512]{1,0:T(8,128)(2,1)S(1)} collective-permute-done((bf16[256,512]{1,0:T(8,128)(2,1)S(1)}, bf16[256,512]{1,0:T(8,128)(2,1)S(1)}, u32[]{:S(2)}, u32[]{:S(2)}) %collective-permute-start.8) | collective-permute-done | bytes 262176 | tf_op jit(solution)/shard_map/ppermute | solution.py:88
  71.0 5.4 %collective-permute-start.9 = (bf16[256,512]{1,0:T(8,128)(2,1)S(1)}, bf16[256,512]{1,0:T(8,128)(2,1)S(1)}, u32[]{:S(2)}, u32[]{:S(2)}) collective-permute-start(bf16[256,512]{1,0:T(8,128)(2,1)S(1)} %collective-permute-done.8), channel_id=1, source_target_pairs={{0,15},{1,0},{2,1},{3,2},{4,3},{5,4},{6,5},{7,6},{8,7},{9,8},{10,9... | collective-permute-start | bytes 786440 | tf_op jit(solution)/shard_map/ppermute | solution.py:88
  76.4 0.3 collective-permute-done.2
  76.7 1.9 collective-permute-start.3
  78.6 1.2 fusion.45
  79.8 1.2 fusion.18
  81.0 6.4 %collective-permute-done.9 = bf16[256,512]{1,0:T(8,128)(2,1)S(1)} collective-permute-done((bf16[256,512]{1,0:T(8,128)(2,1)S(1)}, bf16[256,512]{1,0:T(8,128)(2,1)S(1)}, u32[]{:S(2)}, u32[]{:S(2)}) %collective-permute-start.9) | collective-permute-done | bytes 262176 | tf_op jit(solution)/shard_map/ppermute | solution.py:88
  87.3 5.4 %collective-permute-start.10 = (bf16[256,512]{1,0:T(8,128)(2,1)S(1)}, bf16[256,512]{1,0:T(8,128)(2,1)S(1)}, u32[]{:S(2)}, u32[]{:S(2)}) collective-permute-start(bf16[256,512]{1,0:T(8,128)(2,1)S(1)} %collective-permute-done.9), channel_id=1, source_target_pairs={{0,15},{1,0},{2,1},{3,2},{4,3},{5,4},{6,5},{7,6},{8,7},{9,8},{10,9... | collective-permute-start | bytes 786440 | tf_op jit(solution)/shard_map/ppermute | solution.py:88
  93.0 1.9 collective-permute-start.4
  94.9 1.2 fusion.42
  96.1 1.2 fusion.17
  97.3 6.2 %collective-permute-done.10 = bf16[256,512]{1,0:T(8,128)(2,1)S(1)} collective-permute-done((bf16[256,512]{1,0:T(8,128)(2,1)S(1)}, bf16[256,512]{1,0:T(8,128)(2,1)S(1)}, u32[]{:S(2)}, u32[]{:S(2)}) %collective-permute-start.10) | collective-permute-done | bytes 262176 | tf_op jit(solution)/shard_map/ppermute | solution.py:88
  103.4 5.4 %collective-permute-start.11 = (bf16[256,512]{1,0:T(8,128)(2,1)S(1)}, bf16[256,512]{1,0:T(8,128)(2,1)S(1)}, u32[]{:S(2)}, u32[]{:S(2)}) collective-permute-start(bf16[256,512]{1,0:T(8,128)(2,1)S(1)} %collective-permute-done.10), channel_id=1, source_target_pairs={{0,15},{1,0},{2,1},{3,2},{4,3},{5,4},{6,5},{7,6},{8,7},{9,8},{10,9... | collective-permute-start | bytes 786440 | tf_op jit(solution)/shard_map/ppermute | solution.py:88
  109.0 1.9 collective-permute-start.5
  110.9 1.4 slice.26
  112.5 2.1 %fusion.93 = f32[1536,192]{0,1:T(8,128)S(1)} fusion(bf16[1536,512]{1,0:T(8,128)(2,1)} %bitcast.91, bf16[192,512]{1,0:T(8,128)(2,1)S(1)} %bitcast.90), kind=kOutput, calls=%fused_computation.119 | convolution fusion | flops 301989888 | bytes 2949120 | tf_op jit(solution)/shard_map/dot_general | solution.py:43
  114.7 0.7 reshape.81
  115.5 7.9 %all-to-all-start.1 = ((f32[16,1,1536]{2,1,0:T(1,128)}), f32[16,1,1536]{2,1,0:T(1,128)S(1)}, u32[]{:S(2)}, u32[]{:S(2)}) async-start(f32[16,1,1536]{2,1,0:T(1,128)} %reshape.81), calls=%async_computation.1 | async-start | bytes 196608 | tf_op jit(solution)/shard_map/all_to_all | solution.py:48
  123.4 1.2 fusion.39
  124.6 1.2 fusion.16
  125.8 3.3 %collective-permute-start.12 = (bf16[256,512]{1,0:T(8,128)(2,1)S(1)}, bf16[256,512]{1,0:T(8,128)(2,1)S(1)}, u32[]{:S(2)}, u32[]{:S(2)}) collective-permute-start(bf16[256,512]{1,0:T(8,128)(2,1)S(1)} %collective-permute-done.5), channel_id=1, source_target_pairs={{0,1},{1,2},{2,3},{3,4},{4,5},{5,6},{6,7},{7,8},{8,9},{9,10},{10,1... | collective-permute-start | bytes 786440 | tf_op jit(solution)/shard_map/ppermute | solution.py:87
  129.1 3.2 %collective-permute-start.13 = (bf16[256,512]{1,0:T(8,128)(2,1)S(1)}, bf16[256,512]{1,0:T(8,128)(2,1)S(1)}, u32[]{:S(2)}, u32[]{:S(2)}) collective-permute-start(bf16[256,512]{1,0:T(8,128)(2,1)S(1)} %collective-permute-done.11), channel_id=1, source_target_pairs={{0,15},{1,0},{2,1},{3,2},{4,3},{5,4},{6,5},{7,6},{8,7},{9,8},{10,9... | collective-permute-start | bytes 786440 | tf_op jit(solution)/shard_map/ppermute | solution.py:88
  132.3 3.6 %all-to-all-done.1 = f32[16,1,1536]{2,1,0:T(1,128)S(1)} async-done(((f32[16,1,1536]{2,1,0:T(1,128)}), f32[16,1,1536]{2,1,0:T(1,128)S(1)}, u32[]{:S(2)}, u32[]{:S(2)}) %all-to-all-start.1) | async-done | bytes 98336 | tf_op jit(solution)/shard_map/all_to_all | solution.py:48
  136.0 0.5 broadcast.53
  136.5 0.9 reduce.7
  137.5 0.6 reshape.98
  138.1 7.9 %all-to-all-start.2 = ((bf16[16,2,768]{2,1,0:T(2,128)(2,1)}), bf16[16,2,768]{2,1,0:T(2,128)(2,1)S(1)}, u32[]{:S(2)}, u32[]{:S(2)}) async-start(bf16[16,2,768]{2,1,0:T(2,128)(2,1)} %reshape.98), calls=%async_computation.2 | async-start | bytes 98304 | tf_op jit(solution)/shard_map/all_to_all | solution.py:51
  146.0 1.2 fusion.36
  147.2 10.7 %all-to-all-done.2 = bf16[16,2,768]{2,1,0:T(2,128)(2,1)S(1)} async-done(((bf16[16,2,768]{2,1,0:T(2,128)(2,1)}), bf16[16,2,768]{2,1,0:T(2,128)(2,1)S(1)}, u32[]{:S(2)}, u32[]{:S(2)}) %all-to-all-start.2) | async-done | bytes 49184 | tf_op jit(solution)/shard_map/all_to_all | solution.py:51
  157.9 1.4 fusion.5
  159.3 13.0 %all-to-all-start.3 = ((bf16[32,48,256]{2,1,0:T(8,128)(2,1)}), bf16[32,48,256]{2,1,0:T(8,128)(2,1)S(1)}, u32[]{:S(2)}, u32[]{:S(2)}) async-start(bf16[32,48,256]{2,1,0:T(8,128)(2,1)} %bitcast.6), calls=%async_computation.3 | async-start | bytes 1572864 | tf_op jit(solution)/shard_map/all_to_all | solution.py:59
  172.3 1.2 fusion.15
  173.6 2.5 %collective-permute-start.14 = (bf16[128,512]{1,0:T(8,128)(2,1)S(1)}, bf16[128,512]{1,0:T(8,128)(2,1)S(1)}, u32[]{:S(2)}, u32[]{:S(2)}) collective-permute-start(bf16[128,512]{1,0:T(8,128)(2,1)S(1)} %slice.32), channel_id=1, source_target_pairs={{0,1},{1,2},{2,3},{3,4},{4,5},{5,6},{6,7},{7,8},{8,9},{9,10},{10,1... | collective-permute-start | bytes 393224 | tf_op jit(solution)/shard_map/ppermute | solution.py:91
  176.1 4.2 %collective-permute-start.15 = (bf16[128,512]{1,0:T(8,128)(2,1)S(1)}, bf16[128,512]{1,0:T(8,128)(2,1)S(1)}, u32[]{:S(2)}, u32[]{:S(2)}) collective-permute-start(bf16[128,512]{1,0:T(8,128)(2,1)S(1)} %slice.33), channel_id=1, source_target_pairs={{0,15},{1,0},{2,1},{3,2},{4,3},{5,4},{6,5},{7,6},{8,7},{9,8},{10,9... | collective-permute-start | bytes 393224 | tf_op jit(solution)/shard_map/ppermute | solution.py:92
  180.3 1.2 fusion.33
  181.5 1.0 collective-permute-done.15
  182.5 1.2 fusion.28
  183.7 1.2 fusion.20
  184.9 1.7 all-to-all-done.3
  186.6 1.4 fusion.11
  188.0 6.9 %fusion.12 = bf16[512,256]{1,0:T(8,128)(2,1)S(1)} fusion(bf16[512,8192]{1,0:T(8,128)(2,1)} %all-gather.2.cloned.1.call-done, bf16[8192,256]{1,0:T(8,128)(2,1)} %param.6, bf16[768,256]{1,0:T(8,128)(2,1)S(1)} %fusion.11), kind=kOutput, calls=%fused_computation.17 | convolution fusion | flops 2147876864 | bytes 13107200 | tf_op jit(solution)/shard_map/dot_general | solution.py:108
  195.0 0.8 pad_maximum_fusion
  (31 shorter events, 1.1 us)
Async XLA Ops:
  6.5 105.9 %copy-start = (bf16[12,16,512]{2,1,0:T(8,128)(2,1)S(1)}, bf16[12,16,512]{2,1,0:T(8,128)(2,1)}, u32[]{:S(2)}) copy-start(bf16[12,16,512]{2,1,0:T(8,128)(2,1)} %param.7) | copy-start | bytes 589828
  6.5 181.5 %all-gather.2.cloned.1.call-start = ((), (), s32[]{:S(2)}) async-start(), calls=%async_computation.4 | async-start | bytes 8912896 | tf_op jit(solution)/shard_map/all_gather | solution.py:81
  9.5 33.8 %collective-permute-start = (bf16[256,512]{1,0:T(8,128)(2,1)S(1)}, bf16[256,512]{1,0:T(8,128)(2,1)S(1)}, u32[]{:S(2)}, u32[]{:S(2)}) collective-permute-start(bf16[256,512]{1,0:T(8,128)(2,1)S(1)} %slice.24), channel_id=1, source_target_pairs={{0,1},{1,2},{2,3},{3,4},{4,5},{5,6},{6,7},{7,8},{8,9},{9,10},{10,1... | collective-permute-start | bytes 786440 | tf_op jit(solution)/shard_map/ppermute | solution.py:87
  13.9 25.8 %collective-permute-start.6 = (bf16[256,512]{1,0:T(8,128)(2,1)S(1)}, bf16[256,512]{1,0:T(8,128)(2,1)S(1)}, u32[]{:S(2)}, u32[]{:S(2)}) collective-permute-start(bf16[256,512]{1,0:T(8,128)(2,1)S(1)} %slice.24), channel_id=1, source_target_pairs={{0,15},{1,0},{2,1},{3,2},{4,3},{5,4},{6,5},{7,6},{8,7},{9,8},{10,9... | collective-permute-start | bytes 786440 | tf_op jit(solution)/shard_map/ppermute | solution.py:88
  30.1 80.8 %all-to-all-start = ((bf16[32,56,512]{2,1,0:T(8,128)(2,1)}), bf16[32,56,512]{2,1,0:T(8,128)(2,1)S(1)}, u32[]{:S(2)}, u32[]{:S(2)}) async-start(bf16[32,56,512]{2,1,0:T(8,128)(2,1)} %fusion.10), calls=%async_computation | async-start | bytes 3670016 | tf_op jit(solution)/shard_map/all_to_all | solution.py:38
  39.7 14.8 %collective-permute-start.7 = (bf16[256,512]{1,0:T(8,128)(2,1)S(1)}, bf16[256,512]{1,0:T(8,128)(2,1)S(1)}, u32[]{:S(2)}, u32[]{:S(2)}) collective-permute-start(bf16[256,512]{1,0:T(8,128)(2,1)S(1)} %collective-permute-done.6), channel_id=1, source_target_pairs={{0,15},{1,0},{2,1},{3,2},{4,3},{5,4},{6,5},{7,6},{8,7},{9,8},{10,9... | collective-permute-start | bytes 786440 | tf_op jit(solution)/shard_map/ppermute | solution.py:88
  43.3 16.8 %collective-permute-start.1 = (bf16[256,512]{1,0:T(8,128)(2,1)S(1)}, bf16[256,512]{1,0:T(8,128)(2,1)S(1)}, u32[]{:S(2)}, u32[]{:S(2)}) collective-permute-start(bf16[256,512]{1,0:T(8,128)(2,1)S(1)} %collective-permute-done), channel_id=1, source_target_pairs={{0,1},{1,2},{2,3},{3,4},{4,5},{5,6},{6,7},{7,8},{8,9},{9,10},{10,1... | collective-permute-start | bytes 786440 | tf_op jit(solution)/shard_map/ppermute | solution.py:87
  54.4 16.5 %collective-permute-start.8 = (bf16[256,512]{1,0:T(8,128)(2,1)S(1)}, bf16[256,512]{1,0:T(8,128)(2,1)S(1)}, u32[]{:S(2)}, u32[]{:S(2)}) collective-permute-start(bf16[256,512]{1,0:T(8,128)(2,1)S(1)} %collective-permute-done.7), channel_id=1, source_target_pairs={{0,15},{1,0},{2,1},{3,2},{4,3},{5,4},{6,5},{7,6},{8,7},{9,8},{10,9... | collective-permute-start | bytes 786440 | tf_op jit(solution)/shard_map/ppermute | solution.py:88
  60.1 16.5 %collective-permute-start.2 = (bf16[256,512]{1,0:T(8,128)(2,1)S(1)}, bf16[256,512]{1,0:T(8,128)(2,1)S(1)}, u32[]{:S(2)}, u32[]{:S(2)}) collective-permute-start(bf16[256,512]{1,0:T(8,128)(2,1)S(1)} %collective-permute-done.1), channel_id=1, source_target_pairs={{0,1},{1,2},{2,3},{3,4},{4,5},{5,6},{6,7},{7,8},{8,9},{9,10},{10,1... | collective-permute-start | bytes 786440 | tf_op jit(solution)/shard_map/ppermute | solution.py:87
  71.0 16.4 %collective-permute-start.9 = (bf16[256,512]{1,0:T(8,128)(2,1)S(1)}, bf16[256,512]{1,0:T(8,128)(2,1)S(1)}, u32[]{:S(2)}, u32[]{:S(2)}) collective-permute-start(bf16[256,512]{1,0:T(8,128)(2,1)S(1)} %collective-permute-done.8), channel_id=1, source_target_pairs={{0,15},{1,0},{2,1},{3,2},{4,3},{5,4},{6,5},{7,6},{8,7},{9,8},{10,9... | collective-permute-start | bytes 786440 | tf_op jit(solution)/shard_map/ppermute | solution.py:88
  76.7 16.3 %collective-permute-start.3 = (bf16[256,512]{1,0:T(8,128)(2,1)S(1)}, bf16[256,512]{1,0:T(8,128)(2,1)S(1)}, u32[]{:S(2)}, u32[]{:S(2)}) collective-permute-start(bf16[256,512]{1,0:T(8,128)(2,1)S(1)} %collective-permute-done.2), channel_id=1, source_target_pairs={{0,1},{1,2},{2,3},{3,4},{4,5},{5,6},{6,7},{7,8},{8,9},{9,10},{10,1... | collective-permute-start | bytes 786440 | tf_op jit(solution)/shard_map/ppermute | solution.py:87
  87.3 16.1 %collective-permute-start.10 = (bf16[256,512]{1,0:T(8,128)(2,1)S(1)}, bf16[256,512]{1,0:T(8,128)(2,1)S(1)}, u32[]{:S(2)}, u32[]{:S(2)}) collective-permute-start(bf16[256,512]{1,0:T(8,128)(2,1)S(1)} %collective-permute-done.9), channel_id=1, source_target_pairs={{0,15},{1,0},{2,1},{3,2},{4,3},{5,4},{6,5},{7,6},{8,7},{9,8},{10,9... | collective-permute-start | bytes 786440 | tf_op jit(solution)/shard_map/ppermute | solution.py:88
  93.0 16.0 %collective-permute-start.4 = (bf16[256,512]{1,0:T(8,128)(2,1)S(1)}, bf16[256,512]{1,0:T(8,128)(2,1)S(1)}, u32[]{:S(2)}, u32[]{:S(2)}) collective-permute-start(bf16[256,512]{1,0:T(8,128)(2,1)S(1)} %collective-permute-done.3), channel_id=1, source_target_pairs={{0,1},{1,2},{2,3},{3,4},{4,5},{5,6},{6,7},{7,8},{8,9},{9,10},{10,1... | collective-permute-start | bytes 786440 | tf_op jit(solution)/shard_map/ppermute | solution.py:87
  103.4 25.6 %collective-permute-start.11 = (bf16[256,512]{1,0:T(8,128)(2,1)S(1)}, bf16[256,512]{1,0:T(8,128)(2,1)S(1)}, u32[]{:S(2)}, u32[]{:S(2)}) collective-permute-start(bf16[256,512]{1,0:T(8,128)(2,1)S(1)} %collective-permute-done.10), channel_id=1, source_target_pairs={{0,15},{1,0},{2,1},{3,2},{4,3},{5,4},{6,5},{7,6},{8,7},{9,8},{10,9... | collective-permute-start | bytes 786440 | tf_op jit(solution)/shard_map/ppermute | solution.py:88
  109.0 16.7 %collective-permute-start.5 = (bf16[256,512]{1,0:T(8,128)(2,1)S(1)}, bf16[256,512]{1,0:T(8,128)(2,1)S(1)}, u32[]{:S(2)}, u32[]{:S(2)}) collective-permute-start(bf16[256,512]{1,0:T(8,128)(2,1)S(1)} %collective-permute-done.4), channel_id=1, source_target_pairs={{0,1},{1,2},{2,3},{3,4},{4,5},{5,6},{6,7},{7,8},{8,9},{9,10},{10,1... | collective-permute-start | bytes 786440 | tf_op jit(solution)/shard_map/ppermute | solution.py:87
  112.5 45.4 %copy-start.1 = (bf16[12,16,256]{2,1,0:T(8,128)(2,1)S(1)}, bf16[12,16,256]{2,1,0:T(8,128)(2,1)}, u32[]{:S(2)}) copy-start(bf16[12,16,256]{2,1,0:T(8,128)(2,1)} %param.8) | copy-start | bytes 294916
  115.5 20.4 %all-to-all-start.1 = ((f32[16,1,1536]{2,1,0:T(1,128)}), f32[16,1,1536]{2,1,0:T(1,128)S(1)}, u32[]{:S(2)}, u32[]{:S(2)}) async-start(f32[16,1,1536]{2,1,0:T(1,128)} %reshape.81), calls=%async_computation.1 | async-start | bytes 196608 | tf_op jit(solution)/shard_map/all_to_all | solution.py:48
  125.8 47.8 %collective-permute-start.12 = (bf16[256,512]{1,0:T(8,128)(2,1)S(1)}, bf16[256,512]{1,0:T(8,128)(2,1)S(1)}, u32[]{:S(2)}, u32[]{:S(2)}) collective-permute-start(bf16[256,512]{1,0:T(8,128)(2,1)S(1)} %collective-permute-done.5), channel_id=1, source_target_pairs={{0,1},{1,2},{2,3},{3,4},{4,5},{5,6},{6,7},{7,8},{8,9},{9,10},{10,1... | collective-permute-start | bytes 786440 | tf_op jit(solution)/shard_map/ppermute | solution.py:87
  129.1 47.0 %collective-permute-start.13 = (bf16[256,512]{1,0:T(8,128)(2,1)S(1)}, bf16[256,512]{1,0:T(8,128)(2,1)S(1)}, u32[]{:S(2)}, u32[]{:S(2)}) collective-permute-start(bf16[256,512]{1,0:T(8,128)(2,1)S(1)} %collective-permute-done.11), channel_id=1, source_target_pairs={{0,15},{1,0},{2,1},{3,2},{4,3},{5,4},{6,5},{7,6},{8,7},{9,8},{10,9... | collective-permute-start | bytes 786440 | tf_op jit(solution)/shard_map/ppermute | solution.py:88
  138.1 19.7 %all-to-all-start.2 = ((bf16[16,2,768]{2,1,0:T(2,128)(2,1)}), bf16[16,2,768]{2,1,0:T(2,128)(2,1)S(1)}, u32[]{:S(2)}, u32[]{:S(2)}) async-start(bf16[16,2,768]{2,1,0:T(2,128)(2,1)} %reshape.98), calls=%async_computation.2 | async-start | bytes 98304 | tf_op jit(solution)/shard_map/all_to_all | solution.py:51
  159.3 27.3 %all-to-all-start.3 = ((bf16[32,48,256]{2,1,0:T(8,128)(2,1)}), bf16[32,48,256]{2,1,0:T(8,128)(2,1)S(1)}, u32[]{:S(2)}, u32[]{:S(2)}) async-start(bf16[32,48,256]{2,1,0:T(8,128)(2,1)} %bitcast.6), calls=%async_computation.3 | async-start | bytes 1572864 | tf_op jit(solution)/shard_map/all_to_all | solution.py:59
  173.6 8.0 %collective-permute-start.14 = (bf16[128,512]{1,0:T(8,128)(2,1)S(1)}, bf16[128,512]{1,0:T(8,128)(2,1)S(1)}, u32[]{:S(2)}, u32[]{:S(2)}) collective-permute-start(bf16[128,512]{1,0:T(8,128)(2,1)S(1)} %slice.32), channel_id=1, source_target_pairs={{0,1},{1,2},{2,3},{3,4},{4,5},{5,6},{6,7},{7,8},{8,9},{9,10},{10,1... | collective-permute-start | bytes 393224 | tf_op jit(solution)/shard_map/ppermute | solution.py:91
  176.1 6.4 %collective-permute-start.15 = (bf16[128,512]{1,0:T(8,128)(2,1)S(1)}, bf16[128,512]{1,0:T(8,128)(2,1)S(1)}, u32[]{:S(2)}, u32[]{:S(2)}) collective-permute-start(bf16[128,512]{1,0:T(8,128)(2,1)S(1)} %slice.33), channel_id=1, source_target_pairs={{0,15},{1,0},{2,1},{3,2},{4,3},{5,4},{6,5},{7,6},{8,7},{9,8},{10,9... | collective-permute-start | bytes 393224 | tf_op jit(solution)/shard_map/ppermute | solution.py:92
Sparse Core Ops, SparseCore 0:
  9.4 150.9 all-gather.1

commit v6 on v1

--- a/solution.py
+++ b/solution.py
@@ -1,6 +1,8 @@
 import jax
 import jax.numpy as jnp
 from jax import lax
+from jax.experimental import pallas as pl
+from jax.experimental.pallas import tpu as pltpu
 from jax.sharding import PartitionSpec as P
 
 adapter_scale_factor = 2.0
@@ -55,14 +57,39 @@
     ).astype(BF16)
 
 
+def query_kernel(tok, w, delta, out):
+    base = jnp.dot(tok[...], w[...], preferred_element_type=F32)
+    rows = tok.shape[0]
+    at = pl.ds(pl.multiple_of(pl.program_id(0) * rows, rows), rows)
+    out[...] = (base + delta[at, :].astype(F32)).astype(out.dtype)
+
+
+def query_of(tokens, w, delta):
+    n, d = tokens.shape
+    cols = w.shape[1]
+    rows = n // 4
+    return pl.pallas_call(
+        query_kernel,
+        grid=(n // rows,),
+        in_specs=[
+            pl.BlockSpec((rows, d), lambda i: (i, 0)),
+            pl.BlockSpec(memory_space=pltpu.VMEM),
+            pl.BlockSpec(memory_space=pltpu.VMEM),
+        ],
+        out_specs=pl.BlockSpec((rows, cols), lambda i: (i, 0)),
+        out_shape=jax.ShapeDtypeStruct((n, cols), BF16),
+        compiler_params=pltpu.CompilerParams(dimension_semantics=("arbitrary",)),
+        name="query",
+    )(tokens, w, delta)
+
+
 def solution(mesh):
     groups, tp = mesh.shape["group"], mesh.shape["tp"]
 
     def on_device(tokens, w_query, adapter_down, adapter_up, adapter_id):
         gathered = lax.all_gather(tokens, "tp", axis=1, tiled=True)
         delta = lora(tokens, adapter_down, adapter_up, adapter_id, groups, tp)
-        base = jnp.dot(gathered, w_query, preferred_element_type=F32)
-        return (base + delta.astype(F32)).astype(BF16)
+        return query_of(gathered, w_query, delta)
 
     placed = (
         P("group", "tp"),

time: 186 us -> 185 us (level)
  blocking collectives: 78.7 us -> 98.3 us
  waiting for transfers between devices: 69.6 us -> 54.4 us
  Pallas kernels: 0 us -> 8.94 us
  matrix products: 14.5 us -> 5.94 us
  starting transfers between devices: 5.74 us -> 0.01 us
    all_to_all x0 -> x1, blocking collectives: none -> 19.6 us  [lora(): lax.all_to_all(delta.reshape(groups, owner_slots, ho), 'group', 0, 0, til...]
    all_gather x1, waiting for transfers between devices: 68.9 us -> 53.7 us  [on_device(): gathered = lax.all_gather(tokens, 'tp', axis=1, tiled=True)]
    pallas_call x0 -> x1, Pallas kernels: none -> 8.94 us  [query_of(): pl.pallas_call(query_kernel, grid=(n // rows,), in_specs=[pl.BlockSpec((r...]
    dot_general x1 -> x0, matrix products: 7.62 us -> none  [on_device(): base = jnp.dot(gathered, w_query, preferred_element_type=F32)]
    all_to_all x1 -> x0, starting transfers between devices: 5.74 us -> none  [lora(): lax.all_to_all(delta.reshape(groups, owner_slots, ho), 'group', 0, 0, til...]
  transfers between devices with their start and end apart: 2 -> 1, of which waited for: 1 -> 1; matrix products, arithmetic and copies ran while one was open for 9% -> 5% of each run, Pallas kernels for 0% -> 0%
where the time goes in v6:
time: 185 us
  blocking collectives  98.3 us (53%)
  waiting for transfers between devices  54.4 us (29%)
  between operations  13.5 us (7%)
  Pallas kernels  8.94 us (5%)
  matrix products  5.94 us (3%)
  other arithmetic  2.74 us (1%)
    all_gather x1, waiting for transfers between devices, on_device(): gathered = lax.all_gather(tokens, 'tp', axis=1, tiled=True)  53.7 us
    all_to_all x1, blocking collectives, lora(): here = lax.all_to_all(sent, 'group', 0, 0, tiled=True)  35.1 us
    all_to_all x1, blocking collectives, lora(): lax.all_to_all(part.reshape(tp, share, slots), 'tp', 0, 0, tiled=True)  26 us
    all_to_all x1, blocking collectives, lora(): lax.all_to_all(delta.reshape(groups, owner_slots, ho), 'group', 0, 0, til...  19.6 us
    all_to_all x1, blocking collectives, lora(): lax.all_to_all(jnp.broadcast_to(scaled[None], (tp, share, slots)), 'tp',...  17.6 us
    pallas_call x1, Pallas kernels, query_of(): pl.pallas_call(query_kernel, grid=(n // rows,), in_specs=[pl.BlockSpec((r...  8.94 us
  transfers between devices with their start and end apart: 1, of which 1 were waited for; matrix products, arithmetic and copies ran while one was open for 5% of the time, Pallas kernels for 0%

profile of v6, /device:TPU:1, one launch (start us, length us, event | category | flops | bytes accessed | tf_op | source)
XLA Modules:
  0.0 184.9 jit_solution(10753752776306810808)
XLA Ops:
  6.5 0.0 copy-start
  6.5 0.0 copy-start.1
  6.5 0.0 all-gather.2.cloned.1.call-start
  6.5 0.7 all-gather.2.cloned.1.call-update
  7.3 0.7 add_select_fusion.1
  8.0 0.4 fusion.13
  8.3 0.7 convert_add_fusion
  9.0 0.9 fusion.14
  9.9 0.1 reshape.86
  10.0 0.0 copy-done.1
  10.0 1.4 fusion.4
  11.4 0.1 fusion.10
  11.6 35.1 %all_to_all.20 = bf16[32,56,512]{2,1,0:T(8,128)(2,1)S(1)} all-to-all(bf16[32,56,512]{2,1,0:T(8,128)(2,1)S(1)} %fusion.10), channel_id=1, replica_groups=mesh['group'=32,'tp'=16] {'group'}, dimensions={0} | all-to-all | bytes 3670016 | tf_op jit(solution)/shard_map/all_to_all | solution.py:36
  46.7 0.1 fusion.20
  46.8 0.1 reshape.81
  46.8 0.2 slice.9
  47.0 0.0 copy-done
  47.0 0.7 fusion.24
  47.7 0.0 copy-start.2
  47.7 0.1 select_reduce_fusion
  47.9 0.1 reshape.78
  47.9 26.0 %all_to_all.21 = f32[16,1,1536]{2,1,0:T(1,128)S(1)} all-to-all(f32[16,1,1536]{2,1,0:T(1,128)S(1)} %reshape.78), channel_id=1, replica_groups=mesh['group'=32,'tp'=16] {'tp'}, dimensions={0} | all-to-all | bytes 196608 | tf_op jit(solution)/shard_map/all_to_all | solution.py:45
  74.0 0.1 reduce_sum.29
  74.0 0.1 broadcast_in_dim.48
  74.1 0.5 broadcast.31
  74.6 0.9 reduce.7
  75.6 17.6 %all_to_all.22 = bf16[16,2,768]{2,1,0:T(2,128)(2,1)S(1)} all-to-all(bf16[16,2,768]{2,1,0:T(2,128)(2,1)S(1)} %reshape.94), channel_id=1, replica_groups=mesh['group'=32,'tp'=16] {'tp'}, dimensions={0} | all-to-all | bytes 98304 | tf_op jit(solution)/shard_map/all_to_all | solution.py:47
  93.2 0.0 copy-done.2
  93.2 0.4 fusion.5
  93.6 19.6 %all_to_all.23 = bf16[32,48,256]{2,1,0:T(8,128)(2,1)S(1)} all-to-all(bf16[32,48,256]{2,1,0:T(8,128)(2,1)S(1)} %bitcast.25), channel_id=1, replica_groups=mesh['group'=32,'tp'=16] {'group'}, dimensions={0} | all-to-all | bytes 1572864 | tf_op jit(solution)/shard_map/all_to_all | solution.py:54
  113.3 2.2 %fusion.11.delta = bf16[768,256]{1,0:T(8,128)(2,1)} fusion(bf16[1536,256]{1,0:T(8,128)(2,1)S(1)} %bitcast.26, s32[768]{0:T(1024)S(1)} %get-tuple-element.5), kind=kOutput, calls=%fused_computation.15 | convolution fusion | flops 605356032 | bytes 1182720 | tf_op jit(solution)/shard_map/dot_general | solution.py:55
  115.5 53.7 %all-gather.2.cloned.1.call-done.tok = bf16[768,8192]{1,0:T(8,128)(2,1)} async-done(((bf16[768,512]{1,0:T(8,128)(2,1)}), bf16[768,8192]{1,0:T(8,128)(2,1)}) %all-gather.2.cloned.1.call-update) | async-done | bytes 12582928 | tf_op jit(solution)/shard_map/all_gather | solution.py:90
  169.1 8.9 %query.1 = bf16[768,256]{1,0:T(8,128)(2,1)} custom-call(bf16[768,8192]{1,0:T(8,128)(2,1)} %all-gather.2.cloned.1.call-done.tok, bf16[8192,256]{1,0:T(8,128)(2,1)} %w.1, bf16[768,256]{1,0:T(8,128)(2,1)} %fusion.11.delta), custom_call_target="tpu_custom_call" | custom-call | tf_op jit(solution)/shard_map/query/pallas_call | solution.py:71
  (6 shorter events, 0.1 us)
Async XLA Ops:
  6.5 40.5 %copy-start = (bf16[12,16,512]{2,1,0:T(8,128)(2,1)S(1)}, bf16[12,16,512]{2,1,0:T(8,128)(2,1)}, u32[]{:S(2)}) copy-start(bf16[12,16,512]{2,1,0:T(8,128)(2,1)} %param.7) | copy-start | bytes 589828
  6.5 3.5 %copy-start.1 = (bf16[768,512]{1,0:T(8,128)(2,1)S(1)}, bf16[768,512]{1,0:T(8,128)(2,1)}, u32[]{:S(2)}) copy-start(bf16[768,512]{1,0:T(8,128)(2,1)} %param.5) | copy-start | bytes 2359300
  6.5 162.6 %all-gather.2.cloned.1.call-start = ((), (), s32[]{:S(2)}) async-start(), calls=%async_computation.4 | async-start | bytes 13369344 | tf_op jit(solution)/shard_map/all_gather | solution.py:90
  47.7 45.5 %copy-start.2 = (bf16[12,16,256]{2,1,0:T(8,128)(2,1)S(1)}, bf16[12,16,256]{2,1,0:T(8,128)(2,1)}, u32[]{:S(2)}) copy-start(bf16[12,16,256]{2,1,0:T(8,128)(2,1)} %param.8) | copy-start | bytes 294916
Sparse Core Ops, SparseCore 0:
  9.4 159.6 all-gather.1

commit v7 on v1

--- a/solution.py
+++ b/solution.py
@@ -1,6 +1,8 @@
 import jax
 import jax.numpy as jnp
 from jax import lax
+from jax.experimental import pallas as pl
+from jax.experimental.pallas import tpu as pltpu
 from jax.sharding import PartitionSpec as P
 
 adapter_scale_factor = 2.0
@@ -55,14 +57,53 @@
     ).astype(BF16)
 
 
+chunks = 8
+
+
+def query_kernel(tok, w, delta, out, held, held_w, sems, sems_w):
+    depth = held.shape[2]
+    copies = []
+    for k in range(chunks):
+        part = pl.ds(k * depth, depth)
+        copies.append(pltpu.make_async_copy(tok.at[:, part], held.at[k], sems.at[k]))
+        copies.append(pltpu.make_async_copy(w.at[part, :], held_w.at[k], sems_w.at[k]))
+    for copy in copies:
+        copy.start()
+    base = delta[...].astype(F32)
+    for k in range(chunks):
+        copies[2 * k].wait()
+        copies[2 * k + 1].wait()
+        base += jnp.dot(held[k], held_w[k], preferred_element_type=F32)
+    out[...] = base.astype(out.dtype)
+
+
+def query_of(tokens, w, delta):
+    n, d = tokens.shape
+    cols = w.shape[1]
+    vmem, far = pl.BlockSpec(memory_space=pltpu.VMEM), pl.BlockSpec(memory_space=pl.ANY)
+    return pl.pallas_call(
+        query_kernel,
+        in_specs=[far, far, vmem],
+        out_specs=vmem,
+        out_shape=jax.ShapeDtypeStruct((n, cols), BF16),
+        scratch_shapes=[
+            pltpu.VMEM((chunks, n, d // chunks), BF16),
+            pltpu.VMEM((chunks, d // chunks, cols), BF16),
+            pltpu.SemaphoreType.DMA((chunks,)),
+            pltpu.SemaphoreType.DMA((chunks,)),
+        ],
+        compiler_params=pltpu.CompilerParams(vmem_limit_bytes=60 * 1024 * 1024),
+        name="query",
+    )(tokens, w, delta)
+
+
 def solution(mesh):
     groups, tp = mesh.shape["group"], mesh.shape["tp"]
 
     def on_device(tokens, w_query, adapter_down, adapter_up, adapter_id):
         gathered = lax.all_gather(tokens, "tp", axis=1, tiled=True)
         delta = lora(tokens, adapter_down, adapter_up, adapter_id, groups, tp)
-        base = jnp.dot(gathered, w_query, preferred_element_type=F32)
-        return (base + delta.astype(F32)).astype(BF16)
+        return query_of(gathered, w_query, delta)
 
     placed = (
         P("group", "tp"),

time: 186 us -> 187 us (level)
  blocking collectives: 78.7 us -> 98.3 us
  waiting for transfers between devices: 69.6 us -> 54.4 us
  Pallas kernels: 0 us -> 10.4 us
  matrix products: 14.5 us -> 5.94 us
  starting transfers between devices: 5.74 us -> 0.01 us
    all_to_all x0 -> x1, blocking collectives: none -> 19.6 us  [lora(): lax.all_to_all(delta.reshape(groups, owner_slots, ho), 'group', 0, 0, til...]
    all_gather x1, waiting for transfers between devices: 68.9 us -> 53.7 us  [on_device(): gathered = lax.all_gather(tokens, 'tp', axis=1, tiled=True)]
    pallas_call x0 -> x1, Pallas kernels: none -> 10.4 us  [query_of(): pl.pallas_call(query_kernel, in_specs=[far, far, vmem], out_specs=vmem, o...]
    dot_general x1 -> x0, matrix products: 7.62 us -> none  [on_device(): base = jnp.dot(gathered, w_query, preferred_element_type=F32)]
    all_to_all x1 -> x0, starting transfers between devices: 5.74 us -> none  [lora(): lax.all_to_all(delta.reshape(groups, owner_slots, ho), 'group', 0, 0, til...]
  transfers between devices with their start and end apart: 2 -> 1, of which waited for: 1 -> 1; matrix products, arithmetic and copies ran while one was open for 9% -> 5% of each run, Pallas kernels for 0% -> 0%
where the time goes in v7:
time: 187 us; the launch traced here: 186 us
  blocking collectives  98.3 us (53%)
  waiting for transfers between devices  54.4 us (29%)
  between operations  13.6 us (7%)
  Pallas kernels  10.4 us (6%)
  matrix products  5.94 us (3%)
  other arithmetic  2.74 us (1%)
    all_gather x1, waiting for transfers between devices, on_device(): gathered = lax.all_gather(tokens, 'tp', axis=1, tiled=True)  53.7 us
    all_to_all x1, blocking collectives, lora(): here = lax.all_to_all(sent, 'group', 0, 0, tiled=True)  35.1 us
    all_to_all x1, blocking collectives, lora(): lax.all_to_all(part.reshape(tp, share, slots), 'tp', 0, 0, tiled=True)  26 us
    all_to_all x1, blocking collectives, lora(): lax.all_to_all(delta.reshape(groups, owner_slots, ho), 'group', 0, 0, til...  19.6 us
    all_to_all x1, blocking collectives, lora(): lax.all_to_all(jnp.broadcast_to(scaled[None], (tp, share, slots)), 'tp',...  17.6 us
    pallas_call x1, Pallas kernels, query_of(): pl.pallas_call(query_kernel, in_specs=[far, far, vmem], out_specs=vmem, o...  10.4 us
  transfers between devices with their start and end apart: 1, of which 1 were waited for; matrix products, arithmetic and copies ran while one was open for 5% of the time, Pallas kernels for 0%

profile of v7, /device:TPU:1, one launch (start us, length us, event | category | flops | bytes accessed | tf_op | source)
XLA Modules:
  0.0 186.4 jit_solution(17781792412340490562)
XLA Ops:
  6.5 0.0 copy-start
  6.5 0.0 copy-start.1
  6.5 0.0 all-gather.2.cloned.1.call-start
  6.5 0.7 all-gather.2.cloned.1.call-update
  7.3 0.7 add_select_fusion.1
  8.0 0.4 fusion.13
  8.3 0.7 convert_add_fusion
  9.0 0.9 fusion.14
  9.9 0.1 reshape.86
  10.0 0.0 copy-done.1
  10.0 1.4 fusion.4
  11.4 0.1 fusion.10
  11.6 35.1 %all_to_all.20 = bf16[32,56,512]{2,1,0:T(8,128)(2,1)S(1)} all-to-all(bf16[32,56,512]{2,1,0:T(8,128)(2,1)S(1)} %fusion.10), channel_id=1, replica_groups=mesh['group'=32,'tp'=16] {'group'}, dimensions={0} | all-to-all | bytes 3670016 | tf_op jit(solution)/shard_map/all_to_all | solution.py:36
  46.7 0.1 fusion.20
  46.8 0.1 reshape.81
  46.8 0.2 slice.9
  47.0 0.0 copy-done
  47.0 0.7 fusion.24
  47.7 0.0 copy-start.2
  47.7 0.1 select_reduce_fusion
  47.9 0.1 reshape.78
  47.9 26.0 %all_to_all.21 = f32[16,1,1536]{2,1,0:T(1,128)S(1)} all-to-all(f32[16,1,1536]{2,1,0:T(1,128)S(1)} %reshape.78), channel_id=1, replica_groups=mesh['group'=32,'tp'=16] {'tp'}, dimensions={0} | all-to-all | bytes 196608 | tf_op jit(solution)/shard_map/all_to_all | solution.py:45
  74.0 0.1 reduce_sum.29
  74.0 0.1 broadcast_in_dim.48
  74.1 0.5 broadcast.31
  74.6 0.9 reduce.7
  75.6 17.6 %all_to_all.22 = bf16[16,2,768]{2,1,0:T(2,128)(2,1)S(1)} all-to-all(bf16[16,2,768]{2,1,0:T(2,128)(2,1)S(1)} %reshape.94), channel_id=1, replica_groups=mesh['group'=32,'tp'=16] {'tp'}, dimensions={0} | all-to-all | bytes 98304 | tf_op jit(solution)/shard_map/all_to_all | solution.py:47
  93.2 0.0 copy-done.2
  93.2 0.4 fusion.5
  93.6 19.6 %all_to_all.23 = bf16[32,48,256]{2,1,0:T(8,128)(2,1)S(1)} all-to-all(bf16[32,48,256]{2,1,0:T(8,128)(2,1)S(1)} %bitcast.25), channel_id=1, replica_groups=mesh['group'=32,'tp'=16] {'group'}, dimensions={0} | all-to-all | bytes 1572864 | tf_op jit(solution)/shard_map/all_to_all | solution.py:54
  113.3 2.2 %fusion.11.delta = bf16[768,256]{1,0:T(8,128)(2,1)} fusion(bf16[1536,256]{1,0:T(8,128)(2,1)S(1)} %bitcast.26, s32[768]{0:T(1024)S(1)} %get-tuple-element.5), kind=kOutput, calls=%fused_computation.15 | convolution fusion | flops 605356032 | bytes 1182720 | tf_op jit(solution)/shard_map/dot_general | solution.py:55
  115.5 53.7 %all-gather.2.cloned.1.call-done.tok = bf16[768,8192]{1,0:T(8,128)(2,1)} async-done(((bf16[768,512]{1,0:T(8,128)(2,1)}), bf16[768,8192]{1,0:T(8,128)(2,1)}) %all-gather.2.cloned.1.call-update) | async-done | bytes 12582928 | tf_op jit(solution)/shard_map/all_gather | solution.py:104
  169.1 10.4 %query.1 = bf16[768,256]{1,0:T(8,128)(2,1)} custom-call(bf16[768,8192]{1,0:T(8,128)(2,1)} %all-gather.2.cloned.1.call-done.tok, bf16[8192,256]{1,0:T(8,128)(2,1)} %w.1, bf16[768,256]{1,0:T(8,128)(2,1)} %fusion.11.delta), custom_call_target="tpu_custom_call" | custom-call | tf_op jit(solution)/shard_map/query/pallas_call | solution.py:84
  (6 shorter events, 0.1 us)
Async XLA Ops:
  6.5 40.5 %copy-start = (bf16[12,16,512]{2,1,0:T(8,128)(2,1)S(1)}, bf16[12,16,512]{2,1,0:T(8,128)(2,1)}, u32[]{:S(2)}) copy-start(bf16[12,16,512]{2,1,0:T(8,128)(2,1)} %param.7) | copy-start | bytes 589828
  6.5 3.5 %copy-start.1 = (bf16[768,512]{1,0:T(8,128)(2,1)S(1)}, bf16[768,512]{1,0:T(8,128)(2,1)}, u32[]{:S(2)}) copy-start(bf16[768,512]{1,0:T(8,128)(2,1)} %param.5) | copy-start | bytes 2359300
  6.5 162.6 %all-gather.2.cloned.1.call-start = ((), (), s32[]{:S(2)}) async-start(), calls=%async_computation.4 | async-start | bytes 13369344 | tf_op jit(solution)/shard_map/all_gather | solution.py:104
  47.7 45.5 %copy-start.2 = (bf16[12,16,256]{2,1,0:T(8,128)(2,1)S(1)}, bf16[12,16,256]{2,1,0:T(8,128)(2,1)}, u32[]{:S(2)}) copy-start(bf16[12,16,256]{2,1,0:T(8,128)(2,1)} %param.8) | copy-start | bytes 294916
Sparse Core Ops, SparseCore 0:
  9.4 159.6 all-gather.1

commit v8 on v7

--- a/solution.py
+++ b/solution.py
@@ -57,23 +57,33 @@
     ).astype(BF16)
 
 
-chunks = 8
+chunk_parts = (1, 1, 2, 2, 2, 2, 2, 2, 2)
 
 
 def query_kernel(tok, w, delta, out, held, held_w, sems, sems_w):
-    depth = held.shape[2]
-    copies = []
-    for k in range(chunks):
-        part = pl.ds(k * depth, depth)
-        copies.append(pltpu.make_async_copy(tok.at[:, part], held.at[k], sems.at[k]))
-        copies.append(pltpu.make_async_copy(w.at[part, :], held_w.at[k], sems_w.at[k]))
-    for copy in copies:
-        copy.start()
+    unit = held.shape[1] // sum(chunk_parts)
+    parts, copies, start = [], [], 0
+    for k, size in enumerate(chunk_parts):
+        part = pl.ds(start * unit, size * unit)
+        start += size
+        parts.append(part)
+        copies.append(
+            (
+                pltpu.make_async_copy(tok.at[:, part], held.at[:, part], sems.at[k]),
+                pltpu.make_async_copy(w.at[part, :], held_w.at[part, :], sems_w.at[k]),
+            )
+        )
+    for pair in copies[:2]:
+        for copy in pair:
+            copy.start()
     base = delta[...].astype(F32)
-    for k in range(chunks):
-        copies[2 * k].wait()
-        copies[2 * k + 1].wait()
-        base += jnp.dot(held[k], held_w[k], preferred_element_type=F32)
+    for k, part in enumerate(parts):
+        for copy in copies[k]:
+            copy.wait()
+        if k + 2 < len(copies):
+            for copy in copies[k + 2]:
+                copy.start()
+        base += jnp.dot(held[:, part], held_w[part, :], preferred_element_type=F32)
     out[...] = base.astype(out.dtype)
 
 
@@ -87,10 +97,10 @@
         out_specs=vmem,
         out_shape=jax.ShapeDtypeStruct((n, cols), BF16),
         scratch_shapes=[
-            pltpu.VMEM((chunks, n, d // chunks), BF16),
-            pltpu.VMEM((chunks, d // chunks, cols), BF16),
-            pltpu.SemaphoreType.DMA((chunks,)),
-            pltpu.SemaphoreType.DMA((chunks,)),
+            pltpu.VMEM((n, d), BF16),
+            pltpu.VMEM((d, cols), BF16),
+            pltpu.SemaphoreType.DMA((len(chunk_parts),)),
+            pltpu.SemaphoreType.DMA((len(chunk_parts),)),
         ],
         compiler_params=pltpu.CompilerParams(vmem_limit_bytes=60 * 1024 * 1024),
         name="query",

time: 187 us -> 187 us (level)
  no operation moved by 1% of the time
where the time goes in v8:
time: 187 us
  blocking collectives  98.3 us (53%)
  waiting for transfers between devices  54.4 us (29%)
  between operations  13.6 us (7%)
  Pallas kernels  10.9 us (6%)
  matrix products  5.94 us (3%)
  other arithmetic  2.74 us (1%)
    all_gather x1, waiting for transfers between devices, on_device(): gathered = lax.all_gather(tokens, 'tp', axis=1, tiled=True)  53.7 us
    all_to_all x1, blocking collectives, lora(): here = lax.all_to_all(sent, 'group', 0, 0, tiled=True)  35.1 us
    all_to_all x1, blocking collectives, lora(): lax.all_to_all(part.reshape(tp, share, slots), 'tp', 0, 0, tiled=True)  26 us
    all_to_all x1, blocking collectives, lora(): lax.all_to_all(delta.reshape(groups, owner_slots, ho), 'group', 0, 0, til...  19.6 us
    all_to_all x1, blocking collectives, lora(): lax.all_to_all(jnp.broadcast_to(scaled[None], (tp, share, slots)), 'tp',...  17.6 us
    pallas_call x1, Pallas kernels, query_of(): pl.pallas_call(query_kernel, in_specs=[far, far, vmem], out_specs=vmem, o...  10.9 us
  transfers between devices with their start and end apart: 1, of which 1 were waited for; matrix products, arithmetic and copies ran while one was open for 5% of the time, Pallas kernels for 0%

profile of v8, /device:TPU:1, one launch (start us, length us, event | category | flops | bytes accessed | tf_op | source)
XLA Modules:
  0.0 186.9 jit_solution(1081553206735220686)
XLA Ops:
  6.5 0.0 copy-start
  6.5 0.0 copy-start.1
  6.5 0.0 all-gather.2.cloned.1.call-start
  6.5 0.7 all-gather.2.cloned.1.call-update
  7.3 0.7 add_select_fusion.1
  8.0 0.4 fusion.13
  8.3 0.7 convert_add_fusion
  9.0 0.9 fusion.14
  9.9 0.1 reshape.86
  10.0 0.0 copy-done.1
  10.0 1.4 fusion.4
  11.4 0.1 fusion.10
  11.6 35.1 %all_to_all.20 = bf16[32,56,512]{2,1,0:T(8,128)(2,1)S(1)} all-to-all(bf16[32,56,512]{2,1,0:T(8,128)(2,1)S(1)} %fusion.10), channel_id=1, replica_groups=mesh['group'=32,'tp'=16] {'group'}, dimensions={0} | all-to-all | bytes 3670016 | tf_op jit(solution)/shard_map/all_to_all | solution.py:36
  46.7 0.1 fusion.20
  46.8 0.1 reshape.81
  46.8 0.2 slice.9
  47.0 0.0 copy-done
  47.0 0.7 fusion.24
  47.7 0.0 copy-start.2
  47.7 0.1 select_reduce_fusion
  47.9 0.1 reshape.78
  47.9 26.0 %all_to_all.21 = f32[16,1,1536]{2,1,0:T(1,128)S(1)} all-to-all(f32[16,1,1536]{2,1,0:T(1,128)S(1)} %reshape.78), channel_id=1, replica_groups=mesh['group'=32,'tp'=16] {'tp'}, dimensions={0} | all-to-all | bytes 196608 | tf_op jit(solution)/shard_map/all_to_all | solution.py:45
  74.0 0.1 reduce_sum.29
  74.0 0.1 broadcast_in_dim.48
  74.1 0.5 broadcast.31
  74.6 0.9 reduce.7
  75.6 17.6 %all_to_all.22 = bf16[16,2,768]{2,1,0:T(2,128)(2,1)S(1)} all-to-all(bf16[16,2,768]{2,1,0:T(2,128)(2,1)S(1)} %reshape.94), channel_id=1, replica_groups=mesh['group'=32,'tp'=16] {'tp'}, dimensions={0} | all-to-all | bytes 98304 | tf_op jit(solution)/shard_map/all_to_all | solution.py:47
  93.2 0.0 copy-done.2
  93.2 0.4 fusion.5
  93.6 19.6 %all_to_all.23 = bf16[32,48,256]{2,1,0:T(8,128)(2,1)S(1)} all-to-all(bf16[32,48,256]{2,1,0:T(8,128)(2,1)S(1)} %bitcast.25), channel_id=1, replica_groups=mesh['group'=32,'tp'=16] {'group'}, dimensions={0} | all-to-all | bytes 1572864 | tf_op jit(solution)/shard_map/all_to_all | solution.py:54
  113.3 2.2 %fusion.11.delta = bf16[768,256]{1,0:T(8,128)(2,1)} fusion(bf16[1536,256]{1,0:T(8,128)(2,1)S(1)} %bitcast.26, s32[768]{0:T(1024)S(1)} %get-tuple-element.5), kind=kOutput, calls=%fused_computation.15 | convolution fusion | flops 605356032 | bytes 1182720 | tf_op jit(solution)/shard_map/dot_general | solution.py:55
  115.5 53.7 %all-gather.2.cloned.1.call-done.tok = bf16[768,8192]{1,0:T(8,128)(2,1)} async-done(((bf16[768,512]{1,0:T(8,128)(2,1)}), bf16[768,8192]{1,0:T(8,128)(2,1)}) %all-gather.2.cloned.1.call-update) | async-done | bytes 12582928 | tf_op jit(solution)/shard_map/all_gather | solution.py:114
  169.1 10.9 %query.1 = bf16[768,256]{1,0:T(8,128)(2,1)} custom-call(bf16[768,8192]{1,0:T(8,128)(2,1)} %all-gather.2.cloned.1.call-done.tok, bf16[8192,256]{1,0:T(8,128)(2,1)} %w.1, bf16[768,256]{1,0:T(8,128)(2,1)} %fusion.11.delta), custom_call_target="tpu_custom_call" | custom-call | tf_op jit(solution)/shard_map/query/pallas_call | solution.py:94
  (6 shorter events, 0.1 us)
Async XLA Ops:
  6.5 40.5 %copy-start = (bf16[12,16,512]{2,1,0:T(8,128)(2,1)S(1)}, bf16[12,16,512]{2,1,0:T(8,128)(2,1)}, u32[]{:S(2)}) copy-start(bf16[12,16,512]{2,1,0:T(8,128)(2,1)} %param.7) | copy-start | bytes 589828
  6.5 3.5 %copy-start.1 = (bf16[768,512]{1,0:T(8,128)(2,1)S(1)}, bf16[768,512]{1,0:T(8,128)(2,1)}, u32[]{:S(2)}) copy-start(bf16[768,512]{1,0:T(8,128)(2,1)} %param.5) | copy-start | bytes 2359300
  6.5 162.6 %all-gather.2.cloned.1.call-start = ((), (), s32[]{:S(2)}) async-start(), calls=%async_computation.4 | async-start | bytes 13369344 | tf_op jit(solution)/shard_map/all_gather | solution.py:114
  47.7 45.5 %copy-start.2 = (bf16[12,16,256]{2,1,0:T(8,128)(2,1)S(1)}, bf16[12,16,256]{2,1,0:T(8,128)(2,1)}, u32[]{:S(2)}) copy-start(bf16[12,16,256]{2,1,0:T(8,128)(2,1)} %param.8) | copy-start | bytes 294916
Sparse Core Ops, SparseCore 0:
  9.4 159.6 all-gather.1

commit v9 on v1

--- a/solution.py
+++ b/solution.py
@@ -61,7 +61,8 @@
     def on_device(tokens, w_query, adapter_down, adapter_up, adapter_id):
         gathered = lax.all_gather(tokens, "tp", axis=1, tiled=True)
         delta = lora(tokens, adapter_down, adapter_up, adapter_id, groups, tp)
-        base = jnp.dot(gathered, w_query, preferred_element_type=F32)
+        delta, gathered = lax.optimization_barrier((delta, gathered))
+        base = lax.optimization_barrier(jnp.dot(gathered, w_query, preferred_element_type=F32))
         return (base + delta.astype(F32)).astype(BF16)
 
     placed = (

time: 186 us -> 185 us (level)
  blocking collectives: 78.7 us -> 98.4 us
  waiting for transfers between devices: 69.6 us -> 55.1 us
  starting transfers between devices: 5.74 us -> 0.01 us
    all_to_all x0 -> x1, blocking collectives: none -> 19.7 us  [lora(): lax.all_to_all(delta.reshape(groups, owner_slots, ho), 'group', 0, 0, til...]
    all_gather x1, waiting for transfers between devices: 68.9 us -> 54.4 us  [on_device(): gathered = lax.all_gather(tokens, 'tp', axis=1, tiled=True)]
    all_to_all x1 -> x0, starting transfers between devices: 5.74 us -> none  [lora(): lax.all_to_all(delta.reshape(groups, owner_slots, ho), 'group', 0, 0, til...]
  transfers between devices with their start and end apart: 2 -> 1, of which waited for: 1 -> 1; matrix products, arithmetic and copies ran while one was open for 9% -> 5% of each run, Pallas kernels for 0% -> 0%
where the time goes in v9:
time: 185 us; the launch traced here: 184 us
  blocking collectives  98.4 us (53%)
  waiting for transfers between devices  55.1 us (30%)
  between operations  13.5 us (7%)
  matrix products  12.8 us (7%)
  other arithmetic  3.6 us (2%)
    all_gather x1, waiting for transfers between devices, on_device(): gathered = lax.all_gather(tokens, 'tp', axis=1, tiled=True)  54.4 us
    all_to_all x1, blocking collectives, lora(): here = lax.all_to_all(sent, 'group', 0, 0, tiled=True)  35.1 us
    all_to_all x1, blocking collectives, lora(): lax.all_to_all(part.reshape(tp, share, slots), 'tp', 0, 0, tiled=True)  26 us
    all_to_all x1, blocking collectives, lora(): lax.all_to_all(delta.reshape(groups, owner_slots, ho), 'group', 0, 0, til...  19.7 us
    all_to_all x1, blocking collectives, lora(): lax.all_to_all(jnp.broadcast_to(scaled[None], (tp, share, slots)), 'tp',...  17.6 us
    dot_general x1, matrix products, on_device(): jnp.dot(gathered, w_query, preferred_element_type=F32)  7.62 us
  transfers between devices with their start and end apart: 1, of which 1 were waited for; matrix products, arithmetic and copies ran while one was open for 5% of the time, Pallas kernels for 0%

profile of v9, /device:TPU:1, one launch (start us, length us, event | category | flops | bytes accessed | tf_op | source)
XLA Modules:
  0.0 184.5 jit_solution(3652003243455348917)
XLA Ops:
  6.5 0.0 copy-start
  6.5 0.0 copy-start.1
  6.5 0.0 all-gather.2.cloned.1.call-start
  6.5 0.7 all-gather.2.cloned.1.call-update
  7.3 0.7 add_select_fusion.1
  8.0 0.4 fusion.13
  8.3 0.7 convert_add_fusion
  9.0 0.9 fusion.14
  9.9 0.1 reshape.86
  10.0 0.0 copy-done.1
  10.0 1.4 fusion.4
  11.4 0.1 fusion.10
  11.6 35.1 %all_to_all.20 = bf16[32,56,512]{2,1,0:T(8,128)(2,1)S(1)} all-to-all(bf16[32,56,512]{2,1,0:T(8,128)(2,1)S(1)} %fusion.10), channel_id=1, replica_groups=mesh['group'=32,'tp'=16] {'group'}, dimensions={0} | all-to-all | bytes 3670016 | tf_op jit(solution)/shard_map/all_to_all | solution.py:34
  46.7 0.1 fusion.20
  46.8 0.1 reshape.81
  46.8 0.2 slice.9
  47.0 0.0 copy-done
  47.0 0.7 fusion.24
  47.7 0.0 copy-start.2
  47.7 0.1 select_reduce_fusion
  47.9 0.1 reshape.78
  47.9 26.0 %all_to_all.21 = f32[16,1,1536]{2,1,0:T(1,128)S(1)} all-to-all(f32[16,1,1536]{2,1,0:T(1,128)S(1)} %reshape.78), channel_id=1, replica_groups=mesh['group'=32,'tp'=16] {'tp'}, dimensions={0} | all-to-all | bytes 196608 | tf_op jit(solution)/shard_map/all_to_all | solution.py:43
  74.0 0.1 reduce_sum.29
  74.0 0.1 broadcast_in_dim.48
  74.1 0.5 broadcast.31
  74.6 0.9 reduce.7
  75.6 17.6 %all_to_all.22 = bf16[16,2,768]{2,1,0:T(2,128)(2,1)S(1)} all-to-all(bf16[16,2,768]{2,1,0:T(2,128)(2,1)S(1)} %reshape.94), channel_id=1, replica_groups=mesh['group'=32,'tp'=16] {'tp'}, dimensions={0} | all-to-all | bytes 98304 | tf_op jit(solution)/shard_map/all_to_all | solution.py:45
  93.2 0.0 copy-done.2
  93.2 0.4 fusion.5
  93.6 19.7 %all_to_all.23 = bf16[32,48,256]{2,1,0:T(8,128)(2,1)S(1)} all-to-all(bf16[32,48,256]{2,1,0:T(8,128)(2,1)S(1)} %bitcast.27), channel_id=1, replica_groups=mesh['group'=32,'tp'=16] {'group'}, dimensions={0} | all-to-all | bytes 1572864 | tf_op jit(solution)/shard_map/all_to_all | solution.py:52
  113.3 1.4 fusion.11
  114.7 54.4 %all-gather.2.cloned.1.call-done = bf16[768,8192]{1,0:T(8,128)(2,1)} async-done(((bf16[768,512]{1,0:T(8,128)(2,1)}), bf16[768,8192]{1,0:T(8,128)(2,1)}) %all-gather.2.cloned.1.call-update) | async-done | bytes 12582928 | tf_op jit(solution)/shard_map/all_gather | solution.py:62
  169.1 7.6 %fusion.25 = f32[768,256]{1,0:T(8,128)S(1)} fusion(bf16[768,8192]{1,0:T(8,128)(2,1)} %all-gather.2.cloned.1.call-done, bf16[8192,256]{1,0:T(8,128)(2,1)} %param.6), kind=kOutput, calls=%fused_computation.41 | convolution fusion | flops 3221225472 | bytes 17563648 | tf_op jit(solution)/shard_map/dot_general | solution.py:65
  176.8 0.9 add_convert_fusion
  (6 shorter events, 0.1 us)
Async XLA Ops:
  6.5 40.5 %copy-start = (bf16[12,16,512]{2,1,0:T(8,128)(2,1)S(1)}, bf16[12,16,512]{2,1,0:T(8,128)(2,1)}, u32[]{:S(2)}) copy-start(bf16[12,16,512]{2,1,0:T(8,128)(2,1)} %param.7) | copy-start | bytes 589828
  6.5 3.5 %copy-start.1 = (bf16[768,512]{1,0:T(8,128)(2,1)S(1)}, bf16[768,512]{1,0:T(8,128)(2,1)}, u32[]{:S(2)}) copy-start(bf16[768,512]{1,0:T(8,128)(2,1)} %param.5) | copy-start | bytes 2359300
  6.5 162.6 %all-gather.2.cloned.1.call-start = ((), (), s32[]{:S(2)}) async-start(), calls=%async_computation.4 | async-start | bytes 13369344 | tf_op jit(solution)/shard_map/all_gather | solution.py:62
  47.7 45.5 %copy-start.2 = (bf16[12,16,256]{2,1,0:T(8,128)(2,1)S(1)}, bf16[12,16,256]{2,1,0:T(8,128)(2,1)}, u32[]{:S(2)}) copy-start(bf16[12,16,256]{2,1,0:T(8,128)(2,1)} %param.8) | copy-start | bytes 294916
Sparse Core Ops, SparseCore 0:
  9.4 159.6 all-gather.1

commit v10 on v9

--- a/solution.py
+++ b/solution.py
@@ -59,10 +59,14 @@
     groups, tp = mesh.shape["group"], mesh.shape["tp"]
 
     def on_device(tokens, w_query, adapter_down, adapter_up, adapter_id):
-        gathered = lax.all_gather(tokens, "tp", axis=1, tiled=True)
+        gathered = lax.all_gather(tokens, "tp", axis=0, tiled=False)
         delta = lora(tokens, adapter_down, adapter_up, adapter_id, groups, tp)
         delta, gathered = lax.optimization_barrier((delta, gathered))
-        base = lax.optimization_barrier(jnp.dot(gathered, w_query, preferred_element_type=F32))
+        base = lax.optimization_barrier(
+            jnp.einsum(
+                "znd,zdh->nh", gathered, w_query.reshape(gathered.shape[0], -1, w_query.shape[1]), preferred_element_type=F32
+            )
+        )
         return (base + delta.astype(F32)).astype(BF16)
 
     placed = (

time: 185 us -> 185 us (level)
  no operation moved by 1% of the time
where the time goes in v10:
time: 185 us
  blocking collectives  98.4 us (53%)
  waiting for transfers between devices  55.2 us (30%)
  between operations  13.5 us (7%)
  matrix products  12.8 us (7%)
  other arithmetic  3.6 us (2%)
    all_gather x1, waiting for transfers between devices, on_device(): gathered = lax.all_gather(tokens, 'tp', axis=0, tiled=False)  54.5 us
    all_to_all x1, blocking collectives, lora(): here = lax.all_to_all(sent, 'group', 0, 0, tiled=True)  35.1 us
    all_to_all x1, blocking collectives, lora(): lax.all_to_all(part.reshape(tp, share, slots), 'tp', 0, 0, tiled=True)  26 us
    all_to_all x1, blocking collectives, lora(): lax.all_to_all(delta.reshape(groups, owner_slots, ho), 'group', 0, 0, til...  19.7 us
    all_to_all x1, blocking collectives, lora(): lax.all_to_all(jnp.broadcast_to(scaled[None], (tp, share, slots)), 'tp',...  17.6 us
    dot_general x1, matrix products, on_device(): jnp.einsum('znd,zdh->nh', gathered, w_query.reshape(gathered.shape[0], -1...  7.62 us
  transfers between devices with their start and end apart: 1, of which 1 were waited for; matrix products, arithmetic and copies ran while one was open for 5% of the time, Pallas kernels for 0%

profile of v10, /device:TPU:1, one launch (start us, length us, event | category | flops | bytes accessed | tf_op | source)
XLA Modules:
  0.0 184.5 jit_solution(9102295107902027289)
XLA Ops:
  6.5 0.0 copy-start
  6.5 0.0 copy-start.1
  6.5 0.0 all-gather.3.cloned.1.call-start
  6.5 0.7 all-gather.3.cloned.1.call-update
  7.3 0.7 add_select_fusion.1
  8.0 0.4 fusion.13
  8.3 0.7 convert_add_fusion
  9.0 0.9 fusion.14
  9.9 0.1 reshape.92
  10.0 0.0 copy-done.1
  10.0 1.4 fusion.4
  11.4 0.1 fusion.10
  11.6 35.1 %all_to_all.20 = bf16[32,56,512]{2,1,0:T(8,128)(2,1)S(1)} all-to-all(bf16[32,56,512]{2,1,0:T(8,128)(2,1)S(1)} %fusion.10), channel_id=1, replica_groups=mesh['group'=32,'tp'=16] {'group'}, dimensions={0} | all-to-all | bytes 3670016 | tf_op jit(solution)/shard_map/all_to_all | solution.py:34
  46.7 0.1 fusion.20
  46.8 0.1 reshape.85
  46.8 0.2 slice.9
  47.0 0.0 copy-done
  47.0 0.7 fusion.24
  47.7 0.0 copy-start.2
  47.7 0.1 select_reduce_fusion
  47.9 0.1 reshape.81
  47.9 26.0 %all_to_all.21 = f32[16,1,1536]{2,1,0:T(1,128)S(1)} all-to-all(f32[16,1,1536]{2,1,0:T(1,128)S(1)} %reshape.81), channel_id=1, replica_groups=mesh['group'=32,'tp'=16] {'tp'}, dimensions={0} | all-to-all | bytes 196608 | tf_op jit(solution)/shard_map/all_to_all | solution.py:43
  73.9 0.1 reduce_sum.29
  74.0 0.1 broadcast_in_dim.48
  74.1 0.5 broadcast.31
  74.6 0.9 reduce.7
  75.5 17.6 %all_to_all.22 = bf16[16,2,768]{2,1,0:T(2,128)(2,1)S(1)} all-to-all(bf16[16,2,768]{2,1,0:T(2,128)(2,1)S(1)} %reshape.100), channel_id=1, replica_groups=mesh['group'=32,'tp'=16] {'tp'}, dimensions={0} | all-to-all | bytes 98304 | tf_op jit(solution)/shard_map/all_to_all | solution.py:45
  93.2 0.0 copy-done.2
  93.2 0.4 fusion.5
  93.6 19.7 %all_to_all.23 = bf16[32,48,256]{2,1,0:T(8,128)(2,1)S(1)} all-to-all(bf16[32,48,256]{2,1,0:T(8,128)(2,1)S(1)} %bitcast.31), channel_id=1, replica_groups=mesh['group'=32,'tp'=16] {'group'}, dimensions={0} | all-to-all | bytes 1572864 | tf_op jit(solution)/shard_map/all_to_all | solution.py:52
  113.3 1.4 fusion.11
  114.7 54.5 %all-gather.3.cloned.1.call-done = bf16[12288,512]{1,0:T(8,128)(2,1)} async-done(((bf16[768,512]{1,0:T(8,128)(2,1)}), bf16[12288,512]{1,0:T(8,128)(2,1)}) %all-gather.3.cloned.1.call-update) | async-done | bytes 12582928 | tf_op jit(solution)/shard_map/all_gather | solution.py:62
  169.2 7.6 %convolution_bitcast_fusion.1 = f32[768,256]{1,0:T(8,128)S(1)} fusion(bf16[16,768,512]{2,1,0:T(8,128)(2,1)} %bitcast.34, bf16[16,512,256]{2,1,0:T(8,128)(2,1)} %bitcast.35), kind=kOutput, calls=%fused_computation.15 | convolution fusion | flops 3221225472 | bytes 17563648 | tf_op jit(solution)/shard_map/znd,zdh->nh/dot_general | solution.py:66
  176.8 0.9 add_convert_fusion
  (6 shorter events, 0.1 us)
Async XLA Ops:
  6.5 40.5 %copy-start = (bf16[12,16,512]{2,1,0:T(8,128)(2,1)S(1)}, bf16[12,16,512]{2,1,0:T(8,128)(2,1)}, u32[]{:S(2)}) copy-start(bf16[12,16,512]{2,1,0:T(8,128)(2,1)} %param.7) | copy-start | bytes 589828
  6.5 3.5 %copy-start.1 = (bf16[768,512]{1,0:T(8,128)(2,1)S(1)}, bf16[768,512]{1,0:T(8,128)(2,1)}, u32[]{:S(2)}) copy-start(bf16[768,512]{1,0:T(8,128)(2,1)} %param.5) | copy-start | bytes 2359300
  6.5 162.6 %all-gather.3.cloned.1.call-start = ((), (), s32[]{:S(2)}) async-start(), calls=%async_computation.4 | async-start | bytes 13369344 | tf_op jit(solution)/shard_map/all_gather | solution.py:62
  47.7 45.5 %copy-start.2 = (bf16[12,16,256]{2,1,0:T(8,128)(2,1)S(1)}, bf16[12,16,256]{2,1,0:T(8,128)(2,1)}, u32[]{:S(2)}) copy-start(bf16[12,16,256]{2,1,0:T(8,128)(2,1)} %param.8) | copy-start | bytes 294916
Sparse Core Ops, SparseCore 0:
  9.4 159.6 all-gather.2

commit v11 on v9

--- a/solution.py
+++ b/solution.py
@@ -40,8 +40,8 @@
     ).reshape(per_group, rank, slots)
     part = jnp.sum(jnp.where(mine, part, 0.0), axis=0)
     share = rank // tp
-    part = lax.all_to_all(part.reshape(tp, share, slots), "tp", 0, 0, tiled=True)
-    scaled = (adapter_scale_factor * jnp.sum(part, axis=0)).astype(BF16)
+    part = lax.all_to_all(part.astype(BF16).reshape(tp, share, slots), "tp", 0, 0, tiled=True)
+    scaled = (adapter_scale_factor * jnp.sum(part.astype(F32), axis=0)).astype(BF16)
     scaled = lax.all_to_all(
         jnp.broadcast_to(scaled[None], (tp, share, slots)), "tp", 0, 0, tiled=True
     ).reshape(1, rank, slots)

time: 185 us -> 183 us (0.989)
  blocking collectives: 98.4 us -> 95.6 us
    all_to_all x1, blocking collectives: 17.6 us -> 15.6 us  [lora(): lax.all_to_all(jnp.broadcast_to(scaled[None], (tp, share, slots)), 'tp',...]
where the time goes in v11:
time: 183 us; the launch traced here: 182 us
  blocking collectives  95.6 us (52%)
  waiting for transfers between devices  55.1 us (30%)
  between operations  13.6 us (7%)
  matrix products  12.8 us (7%)
  other arithmetic  4.3 us (2%)
    all_gather x1, waiting for transfers between devices, on_device(): gathered = lax.all_gather(tokens, 'tp', axis=1, tiled=True)  54.4 us
    all_to_all x1, blocking collectives, lora(): here = lax.all_to_all(sent, 'group', 0, 0, tiled=True)  35.1 us
    all_to_all x1, blocking collectives, lora(): lax.all_to_all(part.astype(BF16).reshape(tp, share, slots), 'tp', 0, 0, t...  25.2 us
    all_to_all x1, blocking collectives, lora(): lax.all_to_all(delta.reshape(groups, owner_slots, ho), 'group', 0, 0, til...  19.7 us
    all_to_all x1, blocking collectives, lora(): lax.all_to_all(jnp.broadcast_to(scaled[None], (tp, share, slots)), 'tp',...  15.6 us
    dot_general x1, matrix products, on_device(): jnp.dot(gathered, w_query, preferred_element_type=F32)  7.62 us
  transfers between devices with their start and end apart: 1, of which 1 were waited for; matrix products, arithmetic and copies ran while one was open for 5% of the time, Pallas kernels for 0%

profile of v11, /device:TPU:1, one launch (start us, length us, event | category | flops | bytes accessed | tf_op | source)
XLA Modules:
  0.0 182.4 jit_solution(1290667721489595639)
XLA Ops:
  6.5 0.0 copy-start
  6.5 0.0 copy-start.1
  6.5 0.0 all-gather.2.cloned.1.call-start
  6.5 0.7 all-gather.2.cloned.1.call-update
  7.3 0.7 add_select_fusion.1
  8.0 0.4 fusion.13
  8.3 0.7 convert_add_fusion
  9.0 0.9 fusion.14
  9.9 0.1 reshape.91
  10.0 0.0 copy-done.1
  10.0 1.4 fusion.4
  11.4 0.1 fusion.10
  11.6 35.1 %all_to_all.20 = bf16[32,56,512]{2,1,0:T(8,128)(2,1)S(1)} all-to-all(bf16[32,56,512]{2,1,0:T(8,128)(2,1)S(1)} %fusion.10), channel_id=1, replica_groups=mesh['group'=32,'tp'=16] {'group'}, dimensions={0} | all-to-all | bytes 3670016 | tf_op jit(solution)/shard_map/all_to_all | solution.py:34
  46.7 0.1 fusion.20
  46.8 0.1 reshape.86
  46.8 0.2 slice.9
  47.0 0.0 copy-done
  47.0 0.7 fusion.24
  47.7 0.0 copy-start.2
  47.7 0.1 select_reduce_fusion
  47.9 0.5 broadcast.31
  48.4 0.7 reduce.7
  49.1 25.2 %all_to_all.21 = bf16[16,2,768]{2,1,0:T(2,128)(2,1)S(1)} all-to-all(bf16[16,2,768]{2,1,0:T(2,128)(2,1)S(1)} %reshape.99), channel_id=1, replica_groups=mesh['group'=32,'tp'=16] {'tp'}, dimensions={0} | all-to-all | bytes 98304 | tf_op jit(solution)/shard_map/all_to_all | solution.py:43
  74.3 0.1 convert_reduce_fusion
  74.5 0.1 broadcast_in_dim.48
  74.5 0.9 reduce.8
  75.5 15.6 %all_to_all.22 = bf16[16,2,768]{2,1,0:T(2,128)(2,1)S(1)} all-to-all(bf16[16,2,768]{2,1,0:T(2,128)(2,1)S(1)} %reshape.101), channel_id=1, replica_groups=mesh['group'=32,'tp'=16] {'tp'}, dimensions={0} | all-to-all | bytes 98304 | tf_op jit(solution)/shard_map/all_to_all | solution.py:45
  91.1 0.0 copy-done.2
  91.2 0.4 fusion.5
  91.6 19.7 %all_to_all.23 = bf16[32,48,256]{2,1,0:T(8,128)(2,1)S(1)} all-to-all(bf16[32,48,256]{2,1,0:T(8,128)(2,1)S(1)} %bitcast.30), channel_id=1, replica_groups=mesh['group'=32,'tp'=16] {'group'}, dimensions={0} | all-to-all | bytes 1572864 | tf_op jit(solution)/shard_map/all_to_all | solution.py:52
  111.3 1.4 fusion.11
  112.7 54.4 %all-gather.2.cloned.1.call-done = bf16[768,8192]{1,0:T(8,128)(2,1)} async-done(((bf16[768,512]{1,0:T(8,128)(2,1)}), bf16[768,8192]{1,0:T(8,128)(2,1)}) %all-gather.2.cloned.1.call-update) | async-done | bytes 12582928 | tf_op jit(solution)/shard_map/all_gather | solution.py:62
  167.0 7.6 %fusion.25 = f32[768,256]{1,0:T(8,128)S(1)} fusion(bf16[768,8192]{1,0:T(8,128)(2,1)} %all-gather.2.cloned.1.call-done, bf16[8192,256]{1,0:T(8,128)(2,1)} %param.6), kind=kOutput, calls=%fused_computation.43 | convolution fusion | flops 3221225472 | bytes 17563648 | tf_op jit(solution)/shard_map/dot_general | solution.py:65
  174.7 0.9 add_convert_fusion
  (8 shorter events, 0.2 us)
Async XLA Ops:
  6.5 40.5 %copy-start = (bf16[12,16,512]{2,1,0:T(8,128)(2,1)S(1)}, bf16[12,16,512]{2,1,0:T(8,128)(2,1)}, u32[]{:S(2)}) copy-start(bf16[12,16,512]{2,1,0:T(8,128)(2,1)} %param.7) | copy-start | bytes 589828
  6.5 3.5 %copy-start.1 = (bf16[768,512]{1,0:T(8,128)(2,1)S(1)}, bf16[768,512]{1,0:T(8,128)(2,1)}, u32[]{:S(2)}) copy-start(bf16[768,512]{1,0:T(8,128)(2,1)} %param.5) | copy-start | bytes 2359300
  6.5 160.5 %all-gather.2.cloned.1.call-start = ((), (), s32[]{:S(2)}) async-start(), calls=%async_computation.4 | async-start | bytes 13369344 | tf_op jit(solution)/shard_map/all_gather | solution.py:62
  47.7 43.5 %copy-start.2 = (bf16[12,16,256]{2,1,0:T(8,128)(2,1)S(1)}, bf16[12,16,256]{2,1,0:T(8,128)(2,1)}, u32[]{:S(2)}) copy-start(bf16[12,16,256]{2,1,0:T(8,128)(2,1)} %param.8) | copy-start | bytes 294916
Sparse Core Ops, SparseCore 0:
  9.4 157.5 all-gather.1

commit v12 on v11

--- a/solution.py
+++ b/solution.py
@@ -27,13 +27,9 @@
     place = (lax.broadcasted_iota(jnp.int32, (slots, n), 0) == slot[None, :]).astype(BF16)
     out_rows = jnp.dot(place, tokens, preferred_element_type=F32).astype(BF16)
     local = (adapter_id % per_group).astype(BF16)
-    out_ids = jnp.dot(place, local[:, None], preferred_element_type=F32).astype(BF16)
-    out_ids = out_ids.reshape(groups, 1, owner_slots)
-    out_ids = jnp.pad(out_ids, ((0, 0), (0, 7), (0, d - owner_slots)))
-    sent = jnp.concatenate([out_rows.reshape(groups, owner_slots, d), out_ids], axis=1)
-    here = lax.all_to_all(sent, "group", 0, 0, tiled=True)
-    rows = here[:, :owner_slots].reshape(slots, d)
-    ids = here[:, owner_slots, :owner_slots].astype(jnp.int32).reshape(1, 1, slots)
+    out_ids = jnp.dot(place, local[:, None], preferred_element_type=F32).astype(jnp.int32)
+    ids = lax.all_to_all(out_ids.reshape(groups, 1, owner_slots), "group", 0, 0, tiled=True).reshape(1, 1, slots)
+    rows = lax.all_to_all(out_rows.reshape(groups, owner_slots, d), "group", 0, 0, tiled=True).reshape(slots, d)
     mine = lax.broadcasted_iota(jnp.int32, (per_group, 1, slots), 0) == ids
     part = lax.dot_general(
         adapter_down.reshape(per_group * rank, d), rows, (((1,), (1,)), ((), ())), preferred_element_type=F32

time: 183 us -> 183 us (level)
  blocking collectives: 95.6 us -> 59.9 us
  waiting for transfers between devices: 55.1 us -> 74.2 us
  starting transfers between devices: 0.01 us -> 14.6 us
    all_to_all x1 -> x0, blocking collectives: 35.1 us -> none  [lora(): here = lax.all_to_all(sent, 'group', 0, 0, tiled=True)]
    all_to_all x0 -> x2, waiting for transfers between devices: none -> 25.8 us  [the longest x1 21.5 us: lora(): lax.all_to_all(out_rows.reshape(groups, owner_slots, d), 'group', 0, 0, t...]
    all_to_all x0 -> x2, starting transfers between devices: none -> 14.6 us  [the longest x1 10.4 us: lora(): lax.all_to_all(out_ids.reshape(groups, 1, owner_slots), 'group', 0, 0, ti...]
    all_gather x1, waiting for transfers between devices: 54.4 us -> 47.7 us  [on_device(): gathered = lax.all_gather(tokens, 'tp', axis=1, tiled=True)]
  transfers between devices with their start and end apart: 1 -> 3, of which waited for: 1 -> 3; matrix products, arithmetic and copies ran while one was open for 5% -> 6% of each run, Pallas kernels for 0% -> 0%
where the time goes in v12:
time: 183 us; the launch traced here: 182 us
  waiting for transfers between devices  74.2 us (41%)
  blocking collectives  59.9 us (33%)
  starting transfers between devices  14.6 us (8%)
  matrix products  14 us (8%)
  between operations  13.6 us (7%)
  other arithmetic  4.11 us (2%)
  local copies, waits for them, and re-layouts  2 us (1%)
    all_gather x1, waiting for transfers between devices, on_device(): gathered = lax.all_gather(tokens, 'tp', axis=1, tiled=True)  47.7 us
    all_to_all x1, blocking collectives, lora(): lax.all_to_all(part.astype(BF16).reshape(tp, share, slots), 'tp', 0, 0, t...  24.7 us
    all_to_all x1, waiting for transfers between devices, lora(): lax.all_to_all(out_rows.reshape(groups, owner_slots, d), 'group', 0, 0, t...  21.5 us
    all_to_all x1, blocking collectives, lora(): lax.all_to_all(delta.reshape(groups, owner_slots, ho), 'group', 0, 0, til...  20.2 us
    all_to_all x1, blocking collectives, lora(): lax.all_to_all(jnp.broadcast_to(scaled[None], (tp, share, slots)), 'tp',...  15 us
    all_to_all x1, starting transfers between devices, lora(): lax.all_to_all(out_ids.reshape(groups, 1, owner_slots), 'group', 0, 0, ti...  10.4 us
    dot_general x1, matrix products, on_device(): jnp.dot(gathered, w_query, preferred_element_type=F32)  7.62 us
    all_to_all x1, waiting for transfers between devices, lora(): lax.all_to_all(out_ids.reshape(groups, 1, owner_slots), 'group', 0, 0, ti...  4.37 us
  transfers between devices with their start and end apart: 3, of which 3 were waited for; matrix products, arithmetic and copies ran while one was open for 6% of the time, Pallas kernels for 0%

profile of v12, /device:TPU:1, one launch (start us, length us, event | category | flops | bytes accessed | tf_op | source)
XLA Modules:
  0.0 182.4 jit_solution(894740431936136106)
XLA Ops:
  6.5 0.0 copy-start
  6.5 0.0 copy-start.1
  6.5 0.0 copy-start.2
  6.5 0.0 all-gather.2.cloned.1.call-start
  6.5 0.7 all-gather.2.cloned.1.call-update
  7.3 0.7 add_select_fusion.1
  8.0 0.4 fusion.11
  8.3 0.0 copy-done.2
  8.4 0.9 fusion.12
  9.3 0.7 reshape.74
  10.0 10.4 %all-to-all-start = ((s32[32,1,48]{2,1,0:T(1,128)}), s32[32,1,48]{2,1,0:T(1,128)S(1)}, u32[]{:S(2)}, u32[]{:S(2)}) async-start(s32[32,1,48]{2,1,0:T(1,128)} %reshape.74), calls=%async_computation | async-start | bytes 32768 | tf_op jit(solution)/shard_map/all_to_all | solution.py:31
  20.3 0.0 copy-done.1
  20.4 2.6 %fusion.3 = bf16[1536,512]{1,0:T(8,128)(2,1)} fusion(bf16[768,512]{1,0:T(8,128)(2,1)S(1)} %copy-done.1, s32[768]{0:T(1024)S(1)} %get-tuple-element.9), kind=kOutput, calls=%fused_computation.4 | convolution fusion | flops 1209925632 | bytes 2362368 | tf_op jit(solution)/shard_map/dot_general | solution.py:28
  22.9 4.4 %all-to-all-done = s32[32,1,48]{2,1,0:T(1,128)S(1)} async-done(((s32[32,1,48]{2,1,0:T(1,128)}), s32[32,1,48]{2,1,0:T(1,128)S(1)}, u32[]{:S(2)}, u32[]{:S(2)}) %all-to-all-start) | async-done | bytes 6176 | tf_op jit(solution)/shard_map/all_to_all | solution.py:31
  27.3 4.3 %all-to-all-start.1 = ((bf16[32,48,512]{2,1,0:T(8,128)(2,1)}), bf16[32,48,512]{2,1,0:T(8,128)(2,1)S(1)}, u32[]{:S(2)}, u32[]{:S(2)}) async-start(bf16[32,48,512]{2,1,0:T(8,128)(2,1)} %bitcast), calls=%async_computation.1 | async-start | bytes 3145728 | tf_op jit(solution)/shard_map/all_to_all | solution.py:32
  31.6 0.5 broadcast.24
  32.1 0.7 reduce.6
  32.8 0.1 eq.37
  32.9 21.5 %all-to-all-done.1 = bf16[32,48,512]{2,1,0:T(8,128)(2,1)S(1)} async-done(((bf16[32,48,512]{2,1,0:T(8,128)(2,1)}), bf16[32,48,512]{2,1,0:T(8,128)(2,1)S(1)}, u32[]{:S(2)}, u32[]{:S(2)}) %all-to-all-start.1) | async-done | bytes 1572896 | tf_op jit(solution)/shard_map/all_to_all | solution.py:32
  54.4 0.0 copy-done
  54.4 0.7 fusion.21
  55.0 0.0 copy-start.3
  55.1 0.1 select_reduce_fusion
  55.2 0.5 broadcast.25
  55.7 0.7 reduce.7
  56.4 24.7 %all_to_all.25 = bf16[16,2,768]{2,1,0:T(2,128)(2,1)S(1)} all-to-all(bf16[16,2,768]{2,1,0:T(2,128)(2,1)S(1)} %reshape.94), channel_id=1, replica_groups=mesh['group'=32,'tp'=16] {'tp'}, dimensions={0} | all-to-all | bytes 98304 | tf_op jit(solution)/shard_map/all_to_all | solution.py:39
  81.1 0.1 convert_reduce_fusion
  81.2 0.1 broadcast_in_dim.48
  81.3 0.9 reduce.8
  82.3 15.0 %all_to_all.26 = bf16[16,2,768]{2,1,0:T(2,128)(2,1)S(1)} all-to-all(bf16[16,2,768]{2,1,0:T(2,128)(2,1)S(1)} %reshape.96), channel_id=1, replica_groups=mesh['group'=32,'tp'=16] {'tp'}, dimensions={0} | all-to-all | bytes 98304 | tf_op jit(solution)/shard_map/all_to_all | solution.py:41
  97.3 0.0 copy-done.3
  97.3 0.4 fusion.4
  97.7 20.2 %all_to_all.27 = bf16[32,48,256]{2,1,0:T(8,128)(2,1)S(1)} all-to-all(bf16[32,48,256]{2,1,0:T(8,128)(2,1)S(1)} %bitcast.29), channel_id=1, replica_groups=mesh['group'=32,'tp'=16] {'group'}, dimensions={0} | all-to-all | bytes 1572864 | tf_op jit(solution)/shard_map/all_to_all | solution.py:48
  118.0 1.4 fusion.9
  119.4 47.7 %all-gather.2.cloned.1.call-done = bf16[768,8192]{1,0:T(8,128)(2,1)} async-done(((bf16[768,512]{1,0:T(8,128)(2,1)}), bf16[768,8192]{1,0:T(8,128)(2,1)}) %all-gather.2.cloned.1.call-update) | async-done | bytes 12582928 | tf_op jit(solution)/shard_map/all_gather | solution.py:58
  167.0 7.6 %fusion.22 = f32[768,256]{1,0:T(8,128)S(1)} fusion(bf16[768,8192]{1,0:T(8,128)(2,1)} %all-gather.2.cloned.1.call-done, bf16[8192,256]{1,0:T(8,128)(2,1)} %param.6), kind=kOutput, calls=%fused_computation.38 | convolution fusion | flops 3221225472 | bytes 17563648 | tf_op jit(solution)/shard_map/dot_general | solution.py:61
  174.7 0.9 add_convert_fusion
  (10 shorter events, 0.2 us)
Async XLA Ops:
  6.5 47.8 %copy-start = (bf16[12,16,512]{2,1,0:T(8,128)(2,1)S(1)}, bf16[12,16,512]{2,1,0:T(8,128)(2,1)}, u32[]{:S(2)}) copy-start(bf16[12,16,512]{2,1,0:T(8,128)(2,1)} %param.7) | copy-start | bytes 589828
  6.5 13.8 %copy-start.1 = (bf16[768,512]{1,0:T(8,128)(2,1)S(1)}, bf16[768,512]{1,0:T(8,128)(2,1)}, u32[]{:S(2)}) copy-start(bf16[768,512]{1,0:T(8,128)(2,1)} %param.5) | copy-start | bytes 2359300
  6.5 1.8 copy-start.2
  6.5 160.5 %all-gather.2.cloned.1.call-start = ((), (), s32[]{:S(2)}) async-start(), calls=%async_computation.5 | async-start | bytes 13369344 | tf_op jit(solution)/shard_map/all_gather | solution.py:58
  10.0 17.3 %all-to-all-start = ((s32[32,1,48]{2,1,0:T(1,128)}), s32[32,1,48]{2,1,0:T(1,128)S(1)}, u32[]{:S(2)}, u32[]{:S(2)}) async-start(s32[32,1,48]{2,1,0:T(1,128)} %reshape.74), calls=%async_computation | async-start | bytes 32768 | tf_op jit(solution)/shard_map/all_to_all | solution.py:31
  27.3 27.1 %all-to-all-start.1 = ((bf16[32,48,512]{2,1,0:T(8,128)(2,1)}), bf16[32,48,512]{2,1,0:T(8,128)(2,1)S(1)}, u32[]{:S(2)}, u32[]{:S(2)}) async-start(bf16[32,48,512]{2,1,0:T(8,128)(2,1)} %bitcast), calls=%async_computation.1 | async-start | bytes 3145728 | tf_op jit(solution)/shard_map/all_to_all | solution.py:32
  55.0 42.3 %copy-start.3 = (bf16[12,16,256]{2,1,0:T(8,128)(2,1)S(1)}, bf16[12,16,256]{2,1,0:T(8,128)(2,1)}, u32[]{:S(2)}) copy-start(bf16[12,16,256]{2,1,0:T(8,128)(2,1)} %param.8) | copy-start | bytes 294916
Sparse Core Ops, SparseCore 0:
  9.4 157.5 all-gather.1
